TPU v7x, 32 devices: a whole 2x2x4 slice. The times are simulated.
32 devices in a mesh: ctx: 4 (over y, x), shard: 8 (over z, core).
Axes of the slice: x: 2, y: 2, z: 4, core: 2. Of those that a mesh axis runs over, the one named last changes fastest.
Arguments:
- tokens: bfloat16 [4096, 1024], P(('ctx', 'shard')), may hold values from -6 to 6
- w_query: bfloat16 [1024, 1024], P('shard'), may hold values from -0.625 to 0.625
- key_weight: bfloat16 [1024, 512], P('shard'), may hold values from -0.625 to 0.625
- value_weight: bfloat16 [1024, 512], P('shard'), may hold values from -0.1875 to 0.1875
- w_out: bfloat16 [1024, 1024], P('shard'), may hold values from -6 to 6
- norm_attn: bfloat16 [1024], P('shard'), may hold values from 0.5 to 1.5
- norm_ffn: bfloat16 [1024], P('shard'), may hold values from 0.5 to 1.5
- w_router: bfloat16 [1024, 16], P('shard'), may hold values from -0.09375 to 0.09375
- w_gate: bfloat16 [1024, 16, 512], P('shard', 'ctx'), may hold values from -0.1875 to 0.1875
- w_up: bfloat16 [1024, 16, 512], P('shard', 'ctx'), may hold values from -0.1875 to 0.1875
- w_down: bfloat16 [512, 16, 1024], P('shard', 'ctx'), may hold values from -6 to 6
- cotangent: bfloat16 [4096, 1024], P(('ctx', 'shard')), may hold values from -6 to 6
- choices: int32 [4096, 8], P(('ctx', 'shard')), may hold values from 0 to 15, all different within a row
- priority: int32 [4096, 8], P(('ctx', 'shard')), may hold values from 0 to 1023, as said below
Outputs:
- block_out: bfloat16 [4096, 1024], P(('ctx', 'shard'))
- grad_tokens: float32 [4096, 1024], P(('ctx', 'shard'))
- grad_query: float32 [1024, 1024], P(('ctx', 'shard'))
- grad_key: float32 [1024, 512], P(('ctx', 'shard'))
- grad_value: float32 [1024, 512], P(('ctx', 'shard'))
- grad_out: float32 [1024, 1024], P(('ctx', 'shard'))
- grad_norm_attn: float32 [1024], P(('ctx', 'shard'))
- grad_norm_ffn: float32 [1024], P(('ctx', 'shard'))
- grad_router: float32 [1024, 16], P(('ctx', 'shard'))
- grad_gate: float32 [1024, 16, 512], P('shard', 'ctx')
- grad_up: float32 [1024, 16, 512], P('shard', 'ctx')
- grad_down: float32 [512, 16, 1024], P('shard', 'ctx')
Inputs may be any that keep to these rules, and one draw needn't show every extreme that they name: `choices`: each row names 8 different experts, and every expert is named by some row. `priority`: within each group of 128 consecutive rows the 1024 entries are 0 to 1023, each once.
All inputs are finite; a program needn't handle non-finite values.
Results may differ from a plain program's by a relative error of at most 0.025.
Values may be sent and summed in bfloat16 or wider, within the bound.
No kernel may reach another device: no remote copies, remote signals or barrier semaphores. Data moves between devices by JAX's collectives and lax.ppermute only.
A program may use at most 192 MiB of HBM per device.

v0:
```python
import functools
import math

import jax
import jax.numpy as jnp
from jax import lax
from jax.experimental import pallas as pl
from jax.experimental.pallas import tpu as pltpu
from jax.sharding import PartitionSpec as P

MODEL_WIDTH = 1024
QUERY_HEADS = 16
KEY_VALUE_HEADS = 8
HEAD_SIZE = 64
FF = 512
TOPK = 8

NORM_EPS = 1e-06
RESIDUAL_SCALE = 0.22
SCORE_SCALE = 0.015625
ROPE_BASE = 10000.0
PRECISE = lax.Precision.HIGHEST
MASKED = -1e30
UNCHOSEN = 1 << 20
LANES = 128

F32 = jnp.float32
BF16 = jnp.bfloat16


def whole(shape):
    return pl.BlockSpec(tuple(shape), lambda i: (0,) * len(shape))


def dot(a, b, dims=((1,), (0,))):
    return lax.dot_general(a, b, (dims, ((), ())), preferred_element_type=F32)


def rotary_tables(positions):
    halfway = HEAD_SIZE // 2
    frequency = jnp.exp(
        jnp.arange(halfway, dtype=F32) * (-2.0 * math.log(ROPE_BASE) / HEAD_SIZE)
    )
    angles = frequency[:, None] * positions.astype(F32)[None, :]
    return (jnp.cos(angles), jnp.sin(angles))


def rotate(vectors, cosine, sine):
    rows, count = vectors.shape
    shaped = vectors.reshape(rows // HEAD_SIZE, 2, HEAD_SIZE // 2, count)
    front, behind = shaped[:, 0], shaped[:, 1]
    turned = jnp.stack(
        [front * cosine - behind * sine, behind * cosine + front * sine], axis=1
    )
    return turned.reshape(rows, count)


def rms_scale(value_rows):
    return lax.rsqrt(jnp.mean(value_rows * value_rows, axis=1, keepdims=True) + NORM_EPS)


def norm_back(upward, inputs, inverse_rms, gain_vector):
    weighted = upward * gain_vector.reshape(1, -1)
    cubed = inverse_rms * inverse_rms * inverse_rms
    return inverse_rms * weighted - inputs * cubed * jnp.mean(
        weighted * inputs, axis=1, keepdims=True
    )


def project_kernel(
    at_ref, columns_ref, cos_ref, sin_ref, *refs, count, tile, depth
):
    parts = refs[: 2 * count]
    normed_ref, q_ref, kv_ref, small_ref, block, gain = refs[2 * count :]
    shards = 2 * count
    width = normed_ref.shape[1]
    lane = lax.broadcasted_iota(jnp.int32, (1, width), 1) // depth
    gain[...] = jnp.zeros_like(gain)
    for k in range(count):
        for side in range(2):
            slot = at_ref[1] if side == 0 else 1 - at_ref[1]
            index = 2 * lax.rem(at_ref[0] - k + count, count) + slot
            part = parts[side * count + k]
            block[pl.ds(pl.multiple_of(index * tile, tile), tile), :] = part[:tile, :]
            small_ref[index] = part[tile:, :]
            row = part[tile : tile + 1, :].astype(F32)
            gain[...] += jnp.where(lane == index, row, 0.0)
    for s in range(shards):
        at = slice(s * tile, (s + 1) * tile)
        x = block[at, :].astype(F32)
        normed_ref[at, :] = (x * rms_scale(x) * gain[...]).astype(BF16)
    lin = dot(columns_ref[...].T, normed_ref[...], ((1,), (1,)))
    q_width = q_ref.shape[0]
    half = HEAD_SIZE // 2
    cosine, sine = cos_ref[...], sin_ref[...]

    def turn(first):
        front, behind = lin[first : first + half], lin[first + half : first + 2 * half]
        return front * cosine - behind * sine, behind * cosine + front * sine

    for h in range(q_width // HEAD_SIZE):
        front, behind = turn(h * HEAD_SIZE)
        at = h * HEAD_SIZE
        q_ref[at : at + half, :] = front.astype(BF16) * jnp.asarray(SCORE_SCALE, BF16)
        q_ref[at + half : at + 2 * half, :] = behind.astype(BF16) * jnp.asarray(SCORE_SCALE, BF16)
    front, behind = turn(q_width)
    kv_ref[:half, :] = front.astype(BF16)
    kv_ref[half:HEAD_SIZE, :] = behind.astype(BF16)
    kv_ref[HEAD_SIZE:, :] = lin[q_width + HEAD_SIZE :].astype(BF16)


def project(parts, others, columns, cosine, sine, at, tile, depth):
    count = len(parts)
    height, width = parts[0].shape
    rows = 2 * count * tile
    lin_width = columns.shape[1]
    shapes = [
        (rows, width),
        (lin_width - 2 * HEAD_SIZE, rows),
        (2 * HEAD_SIZE, rows),
        (2 * count, height - tile, width),
    ]
    args = [at, columns, cosine, sine, *parts, *others]
    return pl.pallas_call(
        functools.partial(project_kernel, count=count, tile=tile, depth=depth),
        grid=(1,),
        in_specs=[pl.BlockSpec(memory_space=pltpu.SMEM)] + [whole(v.shape) for v in args[1:]],
        out_specs=[whole(shape) for shape in shapes],
        out_shape=[jax.ShapeDtypeStruct(shape, BF16) for shape in shapes],
        scratch_shapes=[pltpu.VMEM((rows, width), BF16), pltpu.VMEM((1, width), F32)],
        compiler_params=pltpu.CompilerParams(vmem_limit_bytes=60 << 20),
        cost_estimate=pl.CostEstimate(
            flops=2 * rows * width * lin_width,
            transcendentals=0,
            bytes_accessed=4 * rows * width,
        ),
        name="project",
    )(*args)


def attention_blocks(rows):
    return min(512, rows)


def attend_kernel(c_ref, q_ref, *refs, ctx_count, heads, rows, block, tile):
    kv_refs = refs[:ctx_count]
    out_ref, wide_ref, log_ref = refs[ctx_count : ctx_count + 3]
    natural, peak, total, acc = refs[ctx_count + 3 :]
    step = pl.program_id(0)
    mine = c_ref[0]

    @pl.when(step == 0)
    def _():
        for k in range(ctx_count):

            @pl.when(mine >= k)
            def _(k=k):
                natural[k] = kv_refs[k][...].T

    zeros = jnp.zeros((HEAD_SIZE, block), BF16)
    wide_q = [
        jnp.concatenate([q_ref[h * HEAD_SIZE : (h + 1) * HEAD_SIZE, :], zeros], axis=0)
        for h in range(heads)
    ]
    for h in range(heads):
        peak[h] = jnp.full((1, block), MASKED, F32)
        total[h] = jnp.zeros((1, block), F32)
        acc[h] = jnp.zeros((HEAD_SIZE, block), F32)

    def visit(k, start, masked):
        keys = natural[k, pl.ds(start, block), :]
        values = kv_refs[k][HEAD_SIZE:, pl.ds(start, block)]
        for h in range(heads):
            scores = dot(keys, wide_q[h])
            if masked:
                place = lax.broadcasted_iota(jnp.int32, (block, block), 0)
                query = lax.broadcasted_iota(jnp.int32, (block, block), 1)
                scores = jnp.where(place <= query, scores, MASKED)
            old = peak[h]
            new = jnp.maximum(old, jnp.max(scores, axis=0, keepdims=True))
            shrink = jnp.exp(old - new)
            weights = jnp.exp(scores - new)
            peak[h] = new
            total[h] = total[h] * shrink + jnp.sum(weights, axis=0, keepdims=True)
            acc[h] = acc[h] * shrink + dot(values, weights.astype(BF16))

    def full(k):
        def body(j, carry):
            visit(k, pl.multiple_of(j * block, block), False)
            return carry

        return body

    for k in range(1, ctx_count):

        @pl.when(mine >= k)
        def _(k=k):
            lax.fori_loop(0, rows // block, full(k), 0, unroll=2)

    lax.fori_loop(0, step, full(0), 0)
    visit(0, pl.multiple_of(step * block, block), True)
    for h in range(heads):
        result = acc[h] / total[h]
        at = slice(h * HEAD_SIZE, (h + 1) * HEAD_SIZE)
        wide_ref[at, :] = result
        log_ref[h : h + 1, :] = peak[h] + jnp.log(total[h])
        for j in range(block // tile):
            out_ref[j, at, :] = result[:, j * tile : (j + 1) * tile].astype(BF16)


def attend(queries, key_values, ctx_index, tile):
    width, rows = queries.shape
    heads = width // HEAD_SIZE
    ctx_count = len(key_values)
    block = attention_blocks(rows)
    kv_width = key_values[0].shape[0]
    whole = pl.BlockSpec((kv_width, rows), lambda i, c: (0, 0))
    return pl.pallas_call(
        functools.partial(
            attend_kernel, ctx_count=ctx_count, heads=heads, rows=rows, block=block, tile=tile
        ),
        grid_spec=pltpu.PrefetchScalarGridSpec(
            num_scalar_prefetch=1,
            grid=(rows // block,),
            in_specs=[pl.BlockSpec((width, block), lambda i, c: (0, i))] + [whole] * ctx_count,
            out_specs=[
                pl.BlockSpec((block // tile, width, tile), lambda i, c: (i, 0, 0)),
                pl.BlockSpec((width, block), lambda i, c: (0, i)),
                pl.BlockSpec((heads, block), lambda i, c: (0, i)),
            ],
            scratch_shapes=[
                pltpu.VMEM((ctx_count, rows, kv_width), BF16),
                pltpu.VMEM((heads, 1, block), F32),
                pltpu.VMEM((heads, 1, block), F32),
                pltpu.VMEM((heads, HEAD_SIZE, block), F32),
            ],
        ),
        out_shape=[
            jax.ShapeDtypeStruct((rows // tile, width, tile), BF16),
            jax.ShapeDtypeStruct((width, rows), F32),
            jax.ShapeDtypeStruct((heads, rows), F32),
        ],
        compiler_params=pltpu.CompilerParams(
            dimension_semantics=("arbitrary",), vmem_limit_bytes=48 << 20
        ),
        cost_estimate=pl.CostEstimate(
            flops=64 * width * rows * rows * ctx_count // 2,
            transcendentals=heads * rows * rows * ctx_count // 2,
            bytes_accessed=2 * ctx_count * rows * kv_width,
        ),
        name="attend",
    )(ctx_index, queries, *key_values)


def attend_back_kernel(
    c_ref, q_ref, grad_ref, wide_ref, log_ref, *refs, ctx_count, heads, rows, block, tile
):
    kv_refs = refs[:ctx_count]
    gq_ref = refs[ctx_count]
    gkv_refs = refs[ctx_count + 1 : 2 * ctx_count + 1]
    natural, sums, gq_acc = refs[2 * ctx_count + 1 :]
    step = pl.program_id(0)
    last = pl.num_programs(0) - 1
    mine = c_ref[0]

    @pl.when(step == 0)
    def _():
        for k in range(ctx_count):

            @pl.when(mine >= k)
            def _(k=k):
                natural[k] = kv_refs[k][...].T
                sums[k] = jnp.zeros_like(sums[k])

    zeros = jnp.zeros((HEAD_SIZE, block), BF16)
    wide_q, wide_g, tall_q, tall_g, delta, level = [], [], [], [], [], []
    for h in range(heads):
        at = slice(h * HEAD_SIZE, (h + 1) * HEAD_SIZE)
        grad = jnp.concatenate([grad_ref[j, at, :] for j in range(block // tile)], axis=1)
        q_part = jnp.concatenate([q_ref[at, :], zeros], axis=0)
        g_part = jnp.concatenate([zeros, grad], axis=0)
        wide_q.append(q_part)
        wide_g.append(g_part)
        tall_q.append(q_part.T)
        tall_g.append(g_part.T)
        delta.append(jnp.sum(grad.astype(F32) * wide_ref[at, :], axis=0, keepdims=True))
        level.append(log_ref[h : h + 1, :])
        gq_acc[h] = jnp.zeros((HEAD_SIZE, block), F32)

    def visit(k, start, masked):
        both = natural[k, pl.ds(start, block), :]
        keys = kv_refs[k][:HEAD_SIZE, pl.ds(start, block)]
        add = None
        for h in range(heads):
            scores = dot(both, wide_q[h])
            if masked:
                place = lax.broadcasted_iota(jnp.int32, (block, block), 0)
                query = lax.broadcasted_iota(jnp.int32, (block, block), 1)
                scores = jnp.where(place <= query, scores, MASKED)
            weights = jnp.exp(scores - level[h])
            grad_probs = dot(both, wide_g[h])
            grad_scores = (weights * (grad_probs - delta[h])).astype(BF16)
            part = dot(grad_scores, tall_q[h]) + dot(weights.astype(BF16), tall_g[h])
            add = part if add is None else add + part
            gq_acc[h] += dot(keys, grad_scores)
        sums[k, pl.ds(start, block), :] += add

    def full(k):
        def body(j, carry):
            visit(k, pl.multiple_of(j * block, block), False)
            return carry

        return body

    for k in range(1, ctx_count):

        @pl.when(mine >= k)
        def _(k=k):
            lax.fori_loop(0, rows // block, full(k), 0, unroll=2)

    lax.fori_loop(0, step, full(0), 0)
    visit(0, pl.multiple_of(step * block, block), True)
    for h in range(heads):
        gq_ref[h * HEAD_SIZE : (h + 1) * HEAD_SIZE, :] = SCORE_SCALE * gq_acc[h]

    @pl.when(step == last)
    def _():
        gkv_refs[0][...] = sums[0]
        for k in range(1, ctx_count):

            @pl.when(mine >= k)
            def _(k=k):
                gkv_refs[k][...] = sums[k].astype(BF16)

            @pl.when(mine < k)
            def _(k=k):
                gkv_refs[k][...] = jnp.zeros((rows, sums.shape[2]), BF16)


def attend_back(queries, grads, wide, level, key_values, ctx_index):
    width, rows = queries.shape
    heads = width // HEAD_SIZE
    ctx_count = len(key_values)
    block = attention_blocks(rows)
    tile = grads.shape[2]
    kv_width = key_values[0].shape[0]
    whole = pl.BlockSpec((kv_width, rows), lambda i, c: (0, 0))
    tall = pl.BlockSpec((rows, kv_width), lambda i, c: (0, 0))
    return pl.pallas_call(
        functools.partial(
            attend_back_kernel, ctx_count=ctx_count, heads=heads, rows=rows, block=block, tile=tile
        ),
        grid_spec=pltpu.PrefetchScalarGridSpec(
            num_scalar_prefetch=1,
            grid=(rows // block,),
            in_specs=[
                pl.BlockSpec((width, block), lambda i, c: (0, i)),
                pl.BlockSpec((block // tile, width, tile), lambda i, c: (i, 0, 0)),
                pl.BlockSpec((width, block), lambda i, c: (0, i)),
                pl.BlockSpec((heads, block), lambda i, c: (0, i)),
            ]
            + [whole] * ctx_count,
            out_specs=[pl.BlockSpec((width, block), lambda i, c: (0, i))] + [tall] * ctx_count,
            scratch_shapes=[
                pltpu.VMEM((ctx_count, rows, kv_width), BF16),
                pltpu.VMEM((ctx_count, rows, kv_width), F32),
                pltpu.VMEM((heads, HEAD_SIZE, block), F32),
            ],
        ),
        out_shape=[jax.ShapeDtypeStruct((width, rows), F32)]
        + [
            jax.ShapeDtypeStruct((rows, kv_width), F32 if k == 0 else BF16)
            for k in range(ctx_count)
        ],
        compiler_params=pltpu.CompilerParams(
            dimension_semantics=("arbitrary",), vmem_limit_bytes=56 << 20
        ),
        cost_estimate=pl.CostEstimate(
            flops=96 * width * rows * rows * ctx_count // 2,
            transcendentals=heads * rows * rows * ctx_count // 2,
            bytes_accessed=4 * ctx_count * rows * kv_width,
        ),
        name="attend_back",
    )(ctx_index, queries, grads, wide, level, *key_values)


def tail_kernel(
    at_ref, gq_ref, cos_ref, sin_ref, normed_ref, columns_ref, fine_ref, *refs, ctx_count, tile
):
    kv_refs, early_refs = refs[:ctx_count], refs[ctx_count : 2 * ctx_count]
    own_ref, other_ref = refs[2 * ctx_count : 2 * ctx_count + 2]
    late_refs = refs[2 * ctx_count + 2 : 3 * ctx_count + 2]
    tall, late = refs[3 * ctx_count + 2 :]
    ctx, core = at_ref[0], at_ref[1]
    q_width = gq_ref.shape[0]
    lin_width = tall.shape[1]
    half = HEAD_SIZE // 2
    cosine, sine = cos_ref[...], sin_ref[...]

    def turn_back(vectors):
        front, behind = vectors[:half], vectors[half:]
        return [front * cosine + behind * sine, behind * cosine - front * sine]

    grad_kv = add_up([ref[...] for ref in kv_refs]).T
    pieces = []
    for h in range(q_width // HEAD_SIZE):
        pieces += turn_back(gq_ref[h * HEAD_SIZE : (h + 1) * HEAD_SIZE, :])
    pieces += turn_back(grad_kv[:HEAD_SIZE]) + [grad_kv[HEAD_SIZE:]]
    grad_lin = jnp.concatenate(pieces, axis=0).astype(BF16)
    tall[...] = grad_lin.T
    late[...] = dot(grad_lin, normed_ref[...]).astype(BF16).T
    block = late.shape[0] // ctx_count
    for k in range(ctx_count):
        first = pl.multiple_of(lax.rem(ctx - k + ctx_count, ctx_count) * block, block)
        late_refs[k][:, :lin_width] = late[pl.ds(first, block), :]
        late_refs[k][:, lin_width:] = fine_ref[pl.ds(first, block), :]
    early = add_up([ref[...] for ref in early_refs]).astype(BF16)
    chips = own_ref.shape[0]
    small = own_ref.shape[1] - tile
    swap = core == 1
    for chip in range(chips):
        at = [slice((2 * chip + j) * small, (2 * chip + j + 1) * small) for j in range(2)]
        own_ref[chip, tile:, :] = jnp.where(swap, early[at[1]], early[at[0]])
        other_ref[chip, tile:, :] = jnp.where(swap, early[at[0]], early[at[1]])
        for side, ref in ((core, own_ref), (1 - core, other_ref)):
            first = pl.multiple_of((2 * chip + side) * tile, tile)
            ref[chip, :tile, :] = dot(
                tall[pl.ds(first, tile), :], columns_ref[...], ((1,), (1,))
            ).astype(BF16)


def tail(gq, cosine, sine, normed, columns, fine, kv_back, early_back, at, tile):
    ctx_count = len(kv_back)
    rows, width = normed.shape
    lin_width = columns.shape[1]
    chips = rows // (2 * tile)
    small = early_back[0].shape[0] // (2 * chips)
    block = width // ctx_count
    args = [at, gq, cosine, sine, normed, columns, fine, *kv_back, *early_back]
    shapes = [((chips, tile + small, width), BF16)] * 2 + [
        ((block, lin_width + LANES), BF16)
    ] * ctx_count
    out = pl.pallas_call(
        functools.partial(tail_kernel, ctx_count=ctx_count, tile=tile),
        grid=(1,),
        in_specs=[pl.BlockSpec(memory_space=pltpu.SMEM)] + [whole(v.shape) for v in args[1:]],
        out_specs=[whole(shape) for shape, _ in shapes],
        out_shape=[jax.ShapeDtypeStruct(*shape) for shape in shapes],
        scratch_shapes=[pltpu.VMEM((rows, lin_width), BF16), pltpu.VMEM((width, lin_width), BF16)],
        compiler_params=pltpu.CompilerParams(vmem_limit_bytes=60 << 20),
        cost_estimate=pl.CostEstimate(
            flops=4 * rows * width * lin_width, transcendentals=0, bytes_accessed=12 * rows * width
        ),
        name="tail",
    )(*args)
    return out[0], out[1], out[2:]


def finish_kernel(
    late_ref, weight_ref, gain_ref, middle_ref, token_ref, inverse_ref, norm_ref, *refs,
    q_width, copies, experts, tile
):
    parts = refs[:-8]
    tokens_ref, q_ref, k_ref, v_ref, out_ref, attn_ref, ffn_ref, router_ref = refs[-8:]
    grad_normed = add_up([ref[:tile, :] for ref in parts])
    inputs = token_ref[...].astype(F32)
    tokens_ref[...] = middle_ref[...] + norm_back(
        grad_normed, inputs, inverse_ref[...], norm_ref[...]
    )
    out_ref[...] = add_up([ref[tile:, :] for ref in parts])
    shards, rows, _ = late_ref.shape
    width = q_width + 2 * HEAD_SIZE
    gain_grad = jnp.zeros((rows, 1), F32)
    values = [late_ref[s, :, :width].astype(F32) for s in range(shards)]
    for s in range(shards):
        weights = weight_ref[:, s * width : (s + 1) * width].astype(F32)
        gain_grad += jnp.sum(values[s] * weights, axis=1, keepdims=True)
    q_ref[...] = jnp.concatenate([v[:, :q_width] for v in values], axis=1)
    for ref, first in ((k_ref, q_width), (v_ref, q_width + HEAD_SIZE)):
        heads = [v[:, first : first + HEAD_SIZE] for v in values]
        ref[...] = jnp.concatenate(
            [add_up(heads[i : i + copies]) for i in range(0, shards, copies)], axis=1
        )
    fine = add_up([late_ref[s, :, width:] for s in range(shards)])
    count = experts + 1
    router_ref[...] = (fine[:, :experts] + fine[:, count : count + experts]).T
    ffn_ref[...] = (fine[:, experts:count] + fine[:, count + experts : 2 * count]).T
    attn_ref[...] = (gain_grad / gain_ref[...]).T


def finish(
    late, own_weights, own_gain, grad_middle, tokens, inverse, gain, token_back,
    q_width, copies, experts
):
    shards, rows, _ = late.shape
    tile, model = grad_middle.shape
    args = [late, own_weights, own_gain, grad_middle, tokens, inverse, gain[None, :], *token_back]
    kv_width = shards // copies * HEAD_SIZE
    shapes = [(tile, model), (rows, shards * q_width), (rows, kv_width), (rows, kv_width)]
    shapes += [(rows, model), (1, rows), (1, rows), (experts, rows)]
    return pl.pallas_call(
        functools.partial(
            finish_kernel, q_width=q_width, copies=copies, experts=experts, tile=tile
        ),
        grid=(1,),
        in_specs=[whole(v.shape) for v in args],
        out_specs=[whole(shape) for shape in shapes],
        out_shape=[jax.ShapeDtypeStruct(shape, F32) for shape in shapes],
        compiler_params=pltpu.CompilerParams(vmem_limit_bytes=60 << 20),
        cost_estimate=pl.CostEstimate(
            flops=0, transcendentals=0, bytes_accessed=16 * tile * model
        ),
        name="finish",
    )(*args)


def unpack_kernel(first_ref, last_ref, gate_ref, up_ref, down_ref):
    rows, down_rows = gate_ref.shape[0], down_ref.shape[0]
    split = first_ref.shape[0]
    for e in range(split + last_ref.shape[0]):
        source, i = (first_ref, e) if e < split else (last_ref, e - split)
        gate_ref[:, e, :] = source[i, :rows, :].astype(F32)
        up_ref[:, e, :] = source[i, rows : 2 * rows, :].astype(F32)
        for half in range(down_ref.shape[2] // FF):
            at = 2 * rows + half * down_rows
            down_ref[:, e, half * FF : (half + 1) * FF] = source[
                i, at : at + down_rows, :
            ].astype(F32)


def unpack(first, last, rows, down_rows, model):
    experts = first.shape[0] + last.shape[0]
    shapes = [(rows, experts, FF), (rows, experts, FF), (down_rows, experts, model)]
    return pl.pallas_call(
        unpack_kernel,
        grid=(1,),
        in_specs=[whole(first.shape), whole(last.shape)],
        out_specs=[whole(shape) for shape in shapes],
        out_shape=[jax.ShapeDtypeStruct(shape, F32) for shape in shapes],
        compiler_params=pltpu.CompilerParams(vmem_limit_bytes=60 << 20),
        cost_estimate=pl.CostEstimate(
            flops=0, transcendentals=0, bytes_accessed=6 * (first.size + last.size)
        ),
        name="unpack",
    )(first, last)


def expert_kernel(
    c_ref, *refs, ctx_count, experts, first, carried, final, tile, rows, down_rows
):
    refs = list(refs)

    def take(count):
        taken = refs[:count]
        del refs[:count]
        return taken

    x_refs, u_refs, (w_ref,) = take(ctx_count), take(ctx_count), take(1)
    carry_refs = take(3 if carried else 0)
    if final:
        gin_refs, mix_refs = take(ctx_count), take(ctx_count)
    else:
        sums = take(3)
    (grad_ref,) = take(1)
    if final:
        sums = take(3)
    gin_acc, mix_acc, dots = sums
    x_all, x_turned, u_all, share, hid, g_out, g_gate, g_up = refs
    shards = w_ref.shape[0]
    e = pl.program_id(0)
    last = pl.num_programs(0) - 1
    width = u_all.shape[1]
    count = ctx_count * tile
    chunk = min(2 * tile, count)
    column = c_ref[0] * experts + first + e

    @pl.when(e == 0)
    def _():
        for k in range(ctx_count):
            at = slice(k * tile, (k + 1) * tile)
            part = x_refs[k][:, :width]
            x_all[at, :] = part
            x_turned[:, at] = part.T
            u_all[at, :] = u_refs[k][...]
            share[at, :] = x_refs[k][:, width:].astype(F32)
        for i, ref in enumerate(sums):
            ref[...] = carry_refs[i][...] if carried else jnp.zeros_like(ref)

    lane = lax.broadcasted_iota(jnp.int32, (chunk, LANES), 1)
    picked = (lane == column) | (lane == column + LANES // 2)
    down = 2 * rows

    def gate_matrix():
        return w_ref[:, 0, 0:rows, :].reshape(shards * rows, FF)

    def up_matrix():
        return w_ref[:, 0, rows : 2 * rows, :].reshape(shards * rows, FF)

    def down_matrix(half):
        at = down + half * down_rows
        return w_ref[:, 0, at : at + down_rows, :].reshape(FF, FF)

    def one_chunk(j, carry):
        at = pl.ds(pl.multiple_of(j * chunk, chunk), chunk)
        x = x_all[at, :]
        gate = dot(x, gate_matrix())
        up = dot(x, up_matrix())
        sig = jax.nn.sigmoid(gate)
        silu = gate * sig
        hidden = (silu * up).astype(BF16)
        hid[at, :] = hidden
        weight = jnp.sum(jnp.where(picked, share[at, :], 0.0), axis=1, keepdims=True)
        upstream = u_all[at, :].astype(F32) * RESIDUAL_SCALE
        down_grad = (upstream * weight).astype(BF16)
        g_out[at, :] = down_grad
        gathered = jnp.zeros((chunk, 1), F32)
        grad_hidden = jnp.zeros((chunk, FF), F32)
        for half in range(width // FF):
            cols = slice(half * FF, (half + 1) * FF)
            matrix = down_matrix(half)
            made = dot(hidden, matrix).astype(BF16).astype(F32)
            mix_acc[at, cols] += weight * made
            gathered += jnp.sum(upstream[:, cols] * made, axis=1, keepdims=True)
            grad_hidden += dot(down_grad[:, cols], matrix, ((1,), (1,)))
        dots[at, :] += jnp.where(picked, gathered, 0.0)
        grad_gate = (grad_hidden * up * sig * (1.0 + gate * (1.0 - sig))).astype(BF16)
        grad_up = (grad_hidden * silu).astype(BF16)
        g_gate[at, :] = grad_gate
        g_up[at, :] = grad_up
        gin_acc[at, :] += dot(grad_gate, gate_matrix(), ((1,), (1,))) + dot(
            grad_up, up_matrix(), ((1,), (1,))
        )
        return carry

    lax.fori_loop(0, count // chunk, one_chunk, 0, unroll=True)
    grad_ref[:, 0, 0:rows, :] = (
        dot(x_turned[...], g_gate[...]).astype(BF16).reshape(shards, rows, FF)
    )
    grad_ref[:, 0, rows : 2 * rows, :] = (
        dot(x_turned[...], g_up[...]).astype(BF16).reshape(shards, rows, FF)
    )
    hid_turned = hid[...].T
    for half in range(width // FF):
        at = down + half * down_rows
        grad_ref[:, 0, at : at + down_rows, :] = (
            dot(hid_turned, g_out[:, half * FF : (half + 1) * FF])
            .astype(BF16)
            .reshape(shards, down_rows, FF)
        )

    if not final:
        return

    @pl.when(e == last)
    def _():
        for k in range(ctx_count):
            at = slice(k * tile, (k + 1) * tile)
            gin_refs[k][:, :width] = gin_acc[at, :].astype(BF16)
            high = dots[at, :].astype(BF16)
            gin_refs[k][:, width : width + LANES // 2] = high[:, : LANES // 2]
            low = (dots[at, :] - high.astype(F32)).astype(BF16)
            gin_refs[k][:, width + LANES // 2 :] = low[:, LANES // 2 :]
            mix_refs[k][...] = mix_acc[at, :].astype(BF16)


def run_experts(x_parts, u_parts, weights, ctx_index, experts, first, carry, final):
    ctx_count = len(x_parts)
    tile, width = u_parts[0].shape
    shards, group, all_rows, _ = weights.shape
    rows = width // shards
    down_rows = FF // shards
    count = ctx_count * tile

    def flat(*shape, **options):
        return pl.BlockSpec(shape, lambda e, c: (0,) * len(shape), **options)

    expert_block = (shards, 1, all_rows, FF)
    by_expert = pl.BlockSpec(expert_block, lambda e, c: (0, e, 0, 0))
    made = pl.BlockSpec(expert_block, lambda e, c: (0, e, 0, 0))
    sum_shapes = [(count, width), (count, width), (count, LANES)]
    if final:
        out_specs = [flat(tile, width + LANES)] * ctx_count + [flat(tile, width)] * ctx_count
        out_shape = [jax.ShapeDtypeStruct((tile, width + LANES), BF16)] * ctx_count + [
            jax.ShapeDtypeStruct((tile, width), BF16)
        ] * ctx_count
        sum_scratch = [pltpu.VMEM(shape, F32) for shape in sum_shapes]
    else:
        out_specs = [flat(*shape) for shape in sum_shapes]
        out_shape = [jax.ShapeDtypeStruct(shape, F32) for shape in sum_shapes]
        sum_scratch = []
    once = pl.Buffered(1)
    out = pl.pallas_call(
        functools.partial(
            expert_kernel,
            ctx_count=ctx_count,
            experts=experts,
            first=first,
            carried=bool(carry),
            final=final,
            tile=tile,
            rows=rows,
            down_rows=down_rows,
        ),
        grid_spec=pltpu.PrefetchScalarGridSpec(
            num_scalar_prefetch=1,
            grid=(group,),
            in_specs=[flat(tile, width + LANES)] * ctx_count
            + [flat(tile, width)] * ctx_count
            + [by_expert]
            + [flat(*shape, pipeline_mode=once) for shape in sum_shapes[: len(carry)]],
            out_specs=out_specs + [made],
            scratch_shapes=sum_scratch
            + [
                pltpu.VMEM((count, width), BF16),
                pltpu.VMEM((width, count), BF16),
                pltpu.VMEM((count, width), BF16),
                pltpu.VMEM((count, LANES), F32),
                pltpu.VMEM((count, FF), BF16),
                pltpu.VMEM((count, width), BF16),
                pltpu.VMEM((count, FF), BF16),
                pltpu.VMEM((count, FF), BF16),
            ],
        ),
        out_shape=out_shape + [jax.ShapeDtypeStruct((shards, group, all_rows, FF), BF16)],
        compiler_params=pltpu.CompilerParams(
            dimension_semantics=("arbitrary",), vmem_limit_bytes=60 << 20
        ),
        cost_estimate=pl.CostEstimate(
            flops=24 * group * count * width * FF,
            transcendentals=group * count * FF,
            bytes_accessed=4 * shards * group * all_rows * FF,
        ),
        name="experts",
    )(ctx_index, *x_parts, *u_parts, weights, *carry)
    if final:
        return out[:ctx_count], out[ctx_count : 2 * ctx_count], out[2 * ctx_count]
    return out[:3], out[3]


def send_ctx(value, by):
    count = lax.axis_size("ctx")
    return lax.ppermute(value, "ctx", [(i, (i + by) % count) for i in range(count)])


def from_ctx(value):
    return [value] + [send_ctx(value, k) for k in range(1, lax.axis_size("ctx"))]


def from_later(parts):
    return [parts[0]] + [send_ctx(parts[k], -k) for k in range(1, len(parts))]


def add_up(parts):
    total = parts[0].astype(F32)
    for part in parts[1:]:
        total = total + part.astype(F32)
    return total


def to_ctx(parts):
    return add_up(from_later(parts))


def all_to_all(value):
    return lax.all_to_all(value, "shard", split_axis=0, concat_axis=0, tiled=True)


def send_chip(value, by):
    chips = lax.axis_size("shard") // 2
    return lax.ppermute(
        value,
        "shard",
        [(2 * i + j, 2 * ((i + by) % chips) + j) for i in range(chips) for j in range(2)],
    )


def send_core(value):
    return lax.ppermute(value, "shard", [(i, i ^ 1) for i in range(lax.axis_size("shard"))])


def tie(value, *others):
    return lax.optimization_barrier((value, others))[0]


def relay_chips(value):
    chips = lax.axis_size("shard") // 2
    chip = lax.axis_index("shard") // 2

    def step(block, by, done):
        pairs = [
            (2 * i + j, 2 * (i + by) + j)
            for i in range(chips)
            if 0 <= i + by < chips and 0 <= i - by * done < chips
            for j in range(2)
        ]
        return lax.ppermute(block, "shard", pairs)

    up, down = [value], [value]
    for k in range(1, chips):
        up.append(step(up[-1], 1, k - 1))
        down.append(step(down[-1], -1, k - 1))
    return [value] + [jnp.where(chip >= k, up[k], down[chips - k]) for k in range(1, chips)]


def meet(*values):
    return lax.optimization_barrier(values)


def arrive(own, send, count):
    return [own] + [send(own, k) for k in range(1, count)]


def assemble_kernel(at_ref, *refs, count, lead):
    parts, out_ref = refs[:-1], refs[-1]
    for k in range(count):
        index = lax.rem(at_ref[0] - k + count, count)
        for side in range(2):
            slot = at_ref[1] if side == 0 else 1 - at_ref[1]
            out_ref[(slice(None),) * lead + (index, slot)] = parts[side * count + k][...]


def assemble(parts, others, first, lead):
    count = len(parts)
    shape, dtype = parts[0].shape, parts[0].dtype
    at = jnp.stack([first, lax.axis_index("shard") % 2]).astype(jnp.int32)
    out_shape = shape[:lead] + (count, 2) + shape[lead:]
    return pl.pallas_call(
        functools.partial(assemble_kernel, count=count, lead=lead),
        grid=(1,),
        in_specs=[pl.BlockSpec(memory_space=pltpu.SMEM)] + [whole(shape)] * (2 * count),
        out_specs=whole(out_shape),
        out_shape=jax.ShapeDtypeStruct(out_shape, dtype),
        compiler_params=pltpu.CompilerParams(vmem_limit_bytes=60 << 20),
        cost_estimate=pl.CostEstimate(
            flops=0, transcendentals=0, bytes_accessed=8 * count * parts[0].size
        ),
        name="assemble",
    )(at, *parts, *others)


def spread_start(value):
    shards, ctx_count = lax.axis_size("shard"), lax.axis_size("ctx")
    shard, ctx = lax.axis_index("shard"), lax.axis_index("ctx")
    core, chips = shard % 2, shards // 2
    rows, columns = value.shape
    pieces = lax.dynamic_index_in_dim(
        value.reshape(ctx_count, 2, rows // (2 * ctx_count), columns), ctx, 0, keepdims=False
    )
    mine = lax.dynamic_index_in_dim(pieces, core, 0, keepdims=False)
    theirs = send_core(lax.dynamic_index_in_dim(pieces, 1 - core, 0, keepdims=False))
    pair = jnp.stack([jnp.where(core == 0, mine, theirs), jnp.where(core == 0, theirs, mine)])
    return arrive(pair, send_chip, chips)


def spread_join(parts):
    chips = len(parts)
    chip = lax.axis_index("shard") // 2
    joined = jnp.zeros((chips,) + parts[0].shape, parts[0].dtype)
    for k, part in enumerate(parts):
        joined = lax.dynamic_update_index_in_dim(joined, part, (chip - k) % chips, 0)
    return joined


def spread_ctx(joined):
    return arrive(joined, send_ctx, lax.axis_size("ctx"))


def spread_end(parts, others):
    return assemble(parts, others, lax.axis_index("ctx"), 2).reshape(MODEL_WIDTH, -1)


def halve_chips(blocks):
    shards = lax.axis_size("shard")
    chip = lax.axis_index("shard") // 2
    distance, first = 1, None
    while True:
        pairs = blocks.reshape((blocks.shape[0] // 2, 2) + blocks.shape[1:])
        side = (chip // distance) % 2
        keep = lax.dynamic_index_in_dim(pairs, side, 1, keepdims=False)
        sent = lax.dynamic_index_in_dim(pairs, 1 - side, 1, keepdims=False)
        came = lax.ppermute(sent, "shard", [(i, i ^ (2 * distance)) for i in range(shards)])
        first = came if first is None else first
        if keep.shape[0] == 1:
            return [keep[0], came[0]], first
        blocks = (keep.astype(F32) + came.astype(F32)).astype(BF16)
        distance *= 2


def local(
    tokens,
    w_query,
    key_weight,
    value_weight,
    w_out,
    norm_attn,
    norm_ffn,
    w_router,
    w_gate,
    w_up,
    w_down,
    cotangent,
    choices,
    priority,
):
    shards = lax.axis_size("shard")
    ctx_count = lax.axis_size("ctx")
    ctx = lax.axis_index("ctx")
    shard = lax.axis_index("shard")
    ctx_index = ctx.astype(jnp.int32).reshape(1)
    tile = tokens.shape[0]
    rows = tile * shards
    expert_count = w_router.shape[1]
    experts = w_gate.shape[1]
    depth = w_query.shape[0]
    down_depth = w_down.shape[0]
    capacity = tile * TOPK * 5 // (4 * expert_count)
    heads = QUERY_HEADS // shards
    copies = max(1, shards // KEY_VALUE_HEADS)
    q_width = heads * HEAD_SIZE
    width = q_width + 2 * HEAD_SIZE
    share_rows = MODEL_WIDTH // (ctx_count * shards)

    halves = w_down.reshape(down_depth, experts, MODEL_WIDTH // FF, FF)
    expert_rows = jnp.concatenate(
        [
            jnp.transpose(w_gate, (1, 0, 2)),
            jnp.transpose(w_up, (1, 0, 2)),
            jnp.transpose(halves, (1, 2, 0, 3)).reshape(experts, -1, FF),
        ],
        axis=1,
    )
    grouped = jnp.concatenate(
        [
            w_query.reshape(depth, shards, q_width),
            jnp.repeat(key_weight.reshape(depth, KEY_VALUE_HEADS, HEAD_SIZE), copies, axis=1),
            jnp.repeat(value_weight.reshape(depth, KEY_VALUE_HEADS, HEAD_SIZE), copies, axis=1),
        ],
        axis=2,
    )
    small = jnp.concatenate(
        [
            jnp.tile(norm_attn, MODEL_WIDTH // depth)[None, :],
            jnp.tile(norm_ffn, MODEL_WIDTH // depth)[None, :],
            w_router.reshape(-1, MODEL_WIDTH),
        ],
        axis=0,
    )
    small = jnp.pad(small, ((0, 16 - small.shape[0]), (0, 0)))
    chips = shards // 2
    token_parts = relay_chips(jnp.concatenate([tokens, small], axis=0))
    columns = all_to_all(jnp.transpose(grouped, (1, 0, 2))).reshape(MODEL_WIDTH, width)
    cot_parts = from_ctx(cotangent)
    token_parts, columns, cot_parts = meet(token_parts, columns, cot_parts)
    positions = ctx * rows + jnp.arange(rows, dtype=jnp.int32)
    cosine, sine = rotary_tables(positions)
    split = 1
    weights_first = lax.all_gather(expert_rows[:split], "shard", axis=0, tiled=False)
    weights_last = lax.all_gather(
        tie(expert_rows[split:], weights_first, token_parts), "shard", axis=0, tiled=False
    )

    place = jnp.stack([shard // 2, shard % 2]).astype(jnp.int32)
    normed, queries, key_values, small = project(
        token_parts,
        [send_core(part) for part in token_parts],
        columns,
        cosine,
        sine,
        place,
        tile,
        depth,
    )
    gain_attn = small[:, 0, :depth].reshape(MODEL_WIDTH).astype(F32)
    gain_ffn = small[:, 1, :depth].reshape(MODEL_WIDTH).astype(F32)
    router_rows = w_router.size // MODEL_WIDTH
    router_wide = small[:, 2 : 2 + router_rows].reshape(MODEL_WIDTH, expert_count).astype(F32)
    kv_parts = from_ctx(key_values)
    out_parts = spread_start(tie(w_out, key_values))
    outcome, outcome_wide, level = attend(queries, kv_parts, ctx_index, tile)
    outcome, out_parts = meet(outcome, out_parts)
    out_ctx = spread_ctx(spread_join(out_parts))
    out_other = [send_core(part) for part in out_ctx]

    chosen = choices[:, :, None] == jnp.arange(expert_count, dtype=jnp.int32)[None, None, :]
    rank = jnp.min(jnp.where(chosen, priority[:, :, None], UNCHOSEN), axis=1)
    earlier = jnp.sum((rank.T[:, None, :] < rank.T[:, :, None]).astype(F32), axis=2).T
    named = rank < UNCHOSEN
    kept = named & (earlier < capacity)

    attended = all_to_all(outcome).reshape(MODEL_WIDTH, tile)
    attended, out_ctx, out_other = meet(attended, out_ctx, out_other)
    out_full = spread_end(out_ctx, out_other)
    inputs = tokens.astype(F32)
    inverse_attn = rms_scale(inputs)
    branch = dot(attended, out_full, ((0,), (0,)))
    middle = inputs + RESIDUAL_SCALE * branch
    inverse_ffn = rms_scale(middle)
    normed_ffn = middle * inverse_ffn * gain_ffn[None, :]
    logits = jnp.dot(normed_ffn, router_wide, precision=PRECISE)
    masked_logits = jnp.where(named, logits, MASKED)
    raised = jnp.where(
        named, jnp.exp(masked_logits - jnp.max(masked_logits, axis=1, keepdims=True)), 0.0
    )
    gate_weights = raised / jnp.sum(raised, axis=1, keepdims=True)
    kept_weights = jnp.where(kept, gate_weights, 0.0)
    high = kept_weights.astype(BF16)
    low = (kept_weights - high.astype(F32)).astype(BF16)
    spare = ((0, 0), (0, LANES // 2 - expert_count))
    packet = jnp.concatenate([normed_ffn.astype(BF16), jnp.pad(high, spare), jnp.pad(low, spare)], 1)
    x_parts = from_ctx(packet)
    grouped_rows = tie(grouped.reshape(depth, shards * width), packet)
    own_weights = lax.ppermute(
        lax.dynamic_slice_in_dim(
            grouped_rows, ctx * share_rows, share_rows, 0
        ),
        ("ctx", "shard"),
        [(j * shards + i, ctx_count * i + j) for j in range(ctx_count) for i in range(shards)],
    )
    x_parts, own_weights = meet(x_parts, own_weights)
    carry, grads_first = run_experts(
        x_parts, cot_parts, weights_first, ctx_index, experts, 0, [], False
    )
    gin_parts, mix_parts, grads_last = run_experts(
        x_parts, cot_parts, weights_last, ctx_index, experts, split, carry, True
    )
    back = to_ctx(gin_parts)
    share_first = lax.psum_scatter(grads_first, "shard", scatter_dimension=0, tiled=False)
    share_last = lax.psum_scatter(
        tie(grads_last, share_first, back), "shard", scatter_dimension=0, tiled=False
    )
    upstream = cotangent.astype(F32)
    grad_gates = jnp.where(
        kept,
        back[:, MODEL_WIDTH : MODEL_WIDTH + expert_count]
        + back[:, MODEL_WIDTH + LANES // 2 : MODEL_WIDTH + LANES // 2 + expert_count],
        0.0,
    )
    grad_logits = gate_weights * (
        grad_gates - jnp.sum(gate_weights * grad_gates, axis=1, keepdims=True)
    )
    grad_normed_ffn = back[:, :MODEL_WIDTH] + jnp.einsum(
        "te,de->td", grad_logits, router_wide, precision=PRECISE
    )
    grad_middle = upstream + norm_back(grad_normed_ffn, middle, inverse_ffn, gain_ffn)
    grad_branch = (RESIDUAL_SCALE * grad_middle).astype(BF16)
    grad_attended = dot(out_full, grad_branch, ((1,), (1,))).astype(BF16)
    grad_heads = all_to_all(grad_attended.reshape(shards, q_width, tile))

    grad_router = jnp.einsum("te,td->ed", grad_logits, normed_ffn, precision=PRECISE)
    grad_norm_ffn = jnp.sum(grad_normed_ffn * middle * inverse_ffn, axis=0)[None, :]
    fine = jnp.concatenate([grad_router, grad_norm_ffn], axis=0)
    fine_high = fine.astype(BF16)
    fine_low = (fine - fine_high.astype(F32)).astype(BF16)
    fine_rows = expert_count + 1
    fine = jnp.concatenate(
        [fine_high, fine_low, jnp.zeros((LANES - 2 * fine_rows, MODEL_WIDTH), BF16)], axis=0
    ).T
    block = MODEL_WIDTH // ctx_count
    early_parts = []
    for k in range(ctx_count):
        first = ((ctx - k) % ctx_count) * block
        part = lax.dynamic_slice_in_dim(attended, first, block, 0)
        early_parts.append(dot(part, grad_branch).astype(BF16))
    grad_heads, early_parts = meet(grad_heads, early_parts)
    early_parts = from_later(early_parts)

    out = attend_back(queries, grad_heads, outcome_wide, level, kv_parts, ctx_index)
    early_parts, gq, kv_out = meet(early_parts, out[0], out[1:])
    kv_back = from_later(kv_out)
    mix_back = from_later(tie(mix_parts, kv_back))
    at = jnp.stack([ctx, shard % 2]).astype(jnp.int32)
    own, other, late_parts = tail(
        gq, cosine, sine, normed, columns, fine, kv_back, early_parts, at, tile
    )
    chip_sum = (own.astype(F32) + send_core(other).astype(F32)).astype(BF16)
    token_back, halfway = halve_chips(chip_sum)
    late = to_ctx(tie(late_parts, chip_sum)).astype(BF16)
    late = all_to_all(tie(late, halfway).reshape(shards, share_rows, -1))
    expert_grads = unpack(share_first, share_last, depth, down_depth, MODEL_WIDTH)
    block_out = (middle + RESIDUAL_SCALE * add_up(mix_back)).astype(BF16)
    late, token_back, block_out, expert_grads = meet(late, token_back, block_out, expert_grads)
    first_row = (ctx * shards + shard) * share_rows
    own_gain = lax.dynamic_slice_in_dim(gain_attn, first_row, share_rows, 0)[:, None]
    grad_tokens, grad_query, grad_key, grad_value, grad_out, grad_gain, grad_gain_ffn, grad_router = (
        finish(
            late, own_weights, own_gain, grad_middle, tokens, inverse_attn, gain_attn, token_back,
            q_width, copies, expert_count
        )
    )
    return (
        block_out,
        grad_tokens,
        grad_query,
        grad_key,
        grad_value,
        grad_out,
        grad_gain[0],
        grad_gain_ffn[0],
        grad_router.T,
        *expert_grads,
    )


def solution(mesh):
    placed = (
        P(("ctx", "shard"), None),
        P("shard", None),
        P("shard", None),
        P("shard", None),
        P("shard", None),
        P("shard"),
        P("shard"),
        P("shard", None),
        P("shard", "ctx", None),
        P("shard", "ctx", None),
        P("shard", "ctx", None),
        P(("ctx", "shard"), None),
        P(("ctx", "shard"), None),
        P(("ctx", "shard"), None),
    )
    return jax.shard_map(
        local,
        mesh=mesh,
        in_specs=placed,
        out_specs=(
            P(("ctx", "shard"), None),
            P(("ctx", "shard"), None),
            P(("ctx", "shard"), None),
            P(("ctx", "shard"), None),
            P(("ctx", "shard"), None),
            P(("ctx", "shard"), None),
            P(("ctx", "shard")),
            P(("ctx", "shard")),
            P(("ctx", "shard"), None),
            P("shard", "ctx", None),
            P("shard", "ctx", None),
            P("shard", "ctx", None),
        ),
        check_vma=False,
    )
```

profile of v0, /device:TPU:0, one launch (start us, length us, event | category | flops | bytes accessed | tf_op | source)
XLA Modules:
  0.0 366.8 jit_solution(16215773034708517629)
XLA Ops:
  11.0 4.9 %collective-permute-start = (bf16[144,1024]{1,0:T(8,128)(2,1)S(1)}, bf16[144,1024]{1,0:T(8,128)(2,1)S(1)}, u32[]{:S(2)}, u32[]{:S(2)}) collective-permute-start(bf16[144,1024]{1,0:T(8,128)(2,1)S(1)} %pad_maximum_fusion.3.refs_0_), channel_id=1, source_target_pairs={{0,2},{1,3},{2,4},{3,5},{4,6},{5,7},{8,10},{9,11},{10,12},{11,13},... | collective-permute-start | bytes 884744 | tf_op jit(solution)/shard_map/ppermute | solution.py:796
  17.2 6.0 %collective-permute-done = bf16[144,1024]{1,0:T(8,128)(2,1)S(1)} collective-permute-done((bf16[144,1024]{1,0:T(8,128)(2,1)S(1)}, bf16[144,1024]{1,0:T(8,128)(2,1)S(1)}, u32[]{:S(2)}, u32[]{:S(2)}) %collective-permute-start) | collective-permute-done | bytes 294944 | tf_op jit(solution)/shard_map/ppermute | solution.py:796
  25.0 9.4 %collective-permute-done.1 = bf16[144,1024]{1,0:T(8,128)(2,1)} collective-permute-done((bf16[144,1024]{1,0:T(8,128)(2,1)S(1)}, bf16[144,1024]{1,0:T(8,128)(2,1)}, u32[]{:S(2)}, u32[]{:S(2)}) %collective-permute-start.1) | collective-permute-done | bytes 294944 | tf_op jit(solution)/shard_map/ppermute | solution.py:796
  37.7 4.8 %all-to-all-start = ((bf16[8,128,256]{2,1,0:T(8,128)(2,1)}), bf16[8,128,256]{2,1,0:T(8,128)(2,1)S(1)}, u32[]{:S(2)}, u32[]{:S(2)}) async-start(bf16[8,128,256]{2,1,0:T(8,128)(2,1)} %copy.118), calls=%async_computation | async-start | bytes 1048576 | tf_op jit(solution)/shard_map/all_to_all | solution.py:765
  42.6 1.5 collective-permute-start.6
  44.1 1.5 collective-permute-start.7
  45.6 1.4 collective-permute-start.8
  50.7 10.0 %collective-permute-done.2 = bf16[144,1024]{1,0:T(8,128)(2,1)} collective-permute-done((bf16[144,1024]{1,0:T(8,128)(2,1)}, bf16[144,1024]{1,0:T(8,128)(2,1)}, u32[]{:S(2)}, u32[]{:S(2)}) %collective-permute-start.2) | collective-permute-done | bytes 294944 | tf_op jit(solution)/shard_map/ppermute | solution.py:796
  64.2 9.1 %collective-permute-done.3 = bf16[144,1024]{1,0:T(8,128)(2,1)S(1)} collective-permute-done((bf16[144,1024]{1,0:T(8,128)(2,1)}, bf16[144,1024]{1,0:T(8,128)(2,1)S(1)}, u32[]{:S(2)}, u32[]{:S(2)}) %collective-permute-start.3) | collective-permute-done | bytes 294944 | tf_op jit(solution)/shard_map/ppermute | solution.py:796
  77.5 4.7 %project.1 = (bf16[1024,1024]{1,0:T(8,128)(2,1)}, bf16[128,1024]{1,0:T(8,128)(2,1)}, bf16[128,1024]{1,0:T(8,128)(2,1)}, bf16[8,16,1024]{2,1,0:T(8,128)(2,1)}) custom-call(s32[2]{0:T(128)} %pad_add_fusion.1.at_ref, bf16[1024,256]{1,0:T(8,128)(2,1)} %bitcast.106, f32[32,1024]{1,0:T(8,128)} %get-tuple-element.238.cos_ref, ...), custom_call_target="tpu_custom_call" | custom-call | flops 536870912 | bytes 4194304 | tf_op jit(solution)/shard_map/project/pallas_call | solution.py:124
  83.1 1.5 collective-permute-start.13
  84.6 1.5 collective-permute-start.14
  86.2 1.4 collective-permute-start.15
  89.0 1.9 collective-permute-start.18
  90.9 2.5 collective-permute-done.13.refs_1_
  93.4 2.2 collective-permute-start.19
  95.6 2.9 collective-permute-done.14.refs_2_
  100.6 4.1 %attend.1 = (bf16[8,128,128]{2,1,0:T(8,128)(2,1)}, f32[128,1024]{1,0:T(8,128)S(1)}, f32[2,1024]{1,0:T(2,128)S(1)}) custom-call(s32[1]{0:T(128)} %bitcast.c_ref, bf16[128,1024]{1,0:T(8,128)(2,1)S(1)} %copy-done.2, bf16[128,1024]{1,0:T(8,128)(2,1)S(1)} %copy-done.3, bf16[128,1024]{1,0:T(8,128)(2,1)S(1)} %collective-permute-done.13.refs_1_, ...), custom_call_target="tpu_custom_call" | custom-call | flops 17179869184 | bytes 1048576 | tf_op jit(solution)/shard_map/attend/pallas_call | solution.py:218
  106.3 6.2 %collective-permute-start.20 = (bf16[4,2,16,1024]{3,2,1,0:T(8,128)(2,1)S(1)}, bf16[4,2,16,1024]{3,2,1,0:T(8,128)(2,1)S(1)}, u32[]{:S(2)}, u32[]{:S(2)}) collective-permute-start(bf16[4,2,16,1024]{3,2,1,0:T(8,128)(2,1)S(1)} %bitcast_dynamic-update-slice_fusion.refs_0_), channel_id=1, source_target_pairs={{0,8},{8,16},{16,24},{24,0},{1,9},{9,17},{17,25},{25,1},{2,10},{10... | collective-permute-start | bytes 786440 | tf_op jit(solution)/shard_map/ppermute | solution.py:742
  112.4 9.0 %collective-permute-start.21 = (bf16[4,2,16,1024]{3,2,1,0:T(8,128)(2,1)S(1)}, bf16[4,2,16,1024]{3,2,1,0:T(8,128)(2,1)S(1)}, u32[]{:S(2)}, u32[]{:S(2)}) collective-permute-start(bf16[4,2,16,1024]{3,2,1,0:T(8,128)(2,1)S(1)} %bitcast_dynamic-update-slice_fusion.refs_0_), channel_id=1, source_target_pairs={{0,16},{8,24},{16,0},{24,8},{1,17},{9,25},{17,1},{25,9},{2,18},{10... | collective-permute-start | bytes 786440 | tf_op jit(solution)/shard_map/ppermute | solution.py:742
  121.9 3.4 all-to-all-start.1
  125.8 2.2 collective-permute-done.20.refs_1_
  128.1 4.3 %collective-permute-done.21.refs_2_ = bf16[4,2,16,1024]{3,2,1,0:T(8,128)(2,1)S(1)} collective-permute-done((bf16[4,2,16,1024]{3,2,1,0:T(8,128)(2,1)S(1)}, bf16[4,2,16,1024]{3,2,1,0:T(8,128)(2,1)S(1)}, u32[]{:S(2)}, u32[]{:S(2)}) %collective-permute-start.21) | collective-permute-done | bytes 262176 | tf_op jit(solution)/shard_map/ppermute | solution.py:742
  135.7 1.4 fusion.28
  137.1 6.3 %all-to-all-done.1 = bf16[8,128,128]{2,1,0:T(8,128)(2,1)S(1)} async-done(((bf16[8,128,128]{2,1,0:T(8,128)(2,1)}), bf16[8,128,128]{2,1,0:T(8,128)(2,1)S(1)}, u32[]{:S(2)}, u32[]{:S(2)}) %all-to-all-start.1) | async-done | bytes 262176 | tf_op jit(solution)/shard_map/all_to_all | solution.py:765
  144.2 3.0 assemble.1
  147.2 2.2 multiply_reduce_fusion.2
  150.5 1.5 collective-permute-start.27
  153.4 1.5 collective-permute-start.29
  156.2 5.2 %collective-permute-done.27.refs_1_ = bf16[128,1152]{1,0:T(8,128)(2,1)S(1)} collective-permute-done((bf16[128,1152]{1,0:T(8,128)(2,1)S(1)}, bf16[128,1152]{1,0:T(8,128)(2,1)S(1)}, u32[]{:S(2)}, u32[]{:S(2)}) %collective-permute-start.27) | collective-permute-done | bytes 294944 | tf_op jit(solution)/shard_map/ppermute | solution.py:742
  161.4 6.8 %collective-permute-done.28.refs_2_ = bf16[128,1152]{1,0:T(8,128)(2,1)S(1)} collective-permute-done((bf16[128,1152]{1,0:T(8,128)(2,1)S(1)}, bf16[128,1152]{1,0:T(8,128)(2,1)S(1)}, u32[]{:S(2)}, u32[]{:S(2)}) %collective-permute-start.28) | collective-permute-done | bytes 294944 | tf_op jit(solution)/shard_map/ppermute | solution.py:742
  169.7 10.0 %experts.2 = (f32[512,1024]{1,0:T(8,128)}, f32[512,1024]{1,0:T(8,128)}, f32[512,128]{1,0:T(8,128)}, bf16[8,1,384,512]{3,2,1,0:T(8,128)(2,1)}) custom-call(s32[1]{0:T(128)} %bitcast.c_ref, bf16[128,1152]{1,0:T(8,128)(2,1)} %copy-done.28, bf16[128,1152]{1,0:T(8,128)(2,1)} %copy-done.50, bf16[128,1152]{1,0:T(8,128)(2,1)} %copy-done.51, ...), custom_call_target="tpu_custom_call" | custom-call | flops 6442450944 | bytes 6291456 | tf_op jit(solution)/shard_map/experts/pallas_call | solution.py:692
  179.7 24.9 %experts.3 = (bf16[128,1152]{1,0:T(8,128)(2,1)}, bf16[128,1152]{1,0:T(8,128)(2,1)}, bf16[128,1152]{1,0:T(8,128)(2,1)}, bf16[128,1152]{1,0:T(8,128)(2,1)}, bf16[1...) custom-call(s32[1]{0:T(128)} %bitcast.c_ref, ...), custom_call_target="tpu_custom_call" | custom-call | flops 19327352832 | bytes 18874368 | tf_op jit(solution)/shard_map/experts/pallas_call | solution.py:692
  204.6 3.0 collective-permute-start.31
  207.6 1.5 collective-permute-start.32
  209.2 2.1 collective-permute-start.33
  211.3 3.7 %collective-permute-done.31 = bf16[128,1152]{1,0:T(8,128)(2,1)S(1)} collective-permute-done((bf16[128,1152]{1,0:T(8,128)(2,1)}, bf16[128,1152]{1,0:T(8,128)(2,1)S(1)}, u32[]{:S(2)}, u32[]{:S(2)}) %collective-permute-start.31) | collective-permute-done | bytes 294944 | tf_op jit(solution)/shard_map/ppermute | solution.py:742
  215.0 8.0 %collective-permute-done.32 = bf16[128,1152]{1,0:T(8,128)(2,1)S(1)} collective-permute-done((bf16[128,1152]{1,0:T(8,128)(2,1)}, bf16[128,1152]{1,0:T(8,128)(2,1)S(1)}, u32[]{:S(2)}, u32[]{:S(2)}) %collective-permute-start.32) | collective-permute-done | bytes 294944 | tf_op jit(solution)/shard_map/ppermute | solution.py:742
  222.9 1.7 collective-permute-done.33
  226.8 2.0 multiply_convert_fusion
  228.8 1.4 convolution_convert_fusion.4
  230.2 3.4 all-to-all-start.2
  238.2 9.6 %all-to-all-done.2.grad_ref = bf16[8,128,128]{2,1,0:T(8,128)(2,1)S(1)} async-done(((bf16[8,128,128]{2,1,0:T(8,128)(2,1)}), bf16[8,128,128]{2,1,0:T(8,128)(2,1)S(1)}, u32[]{:S(2)}, u32[]{:S(2)}) %all-to-all-start.2) | async-done | bytes 262176 | tf_op jit(solution)/shard_map/all_to_all | solution.py:765
  248.5 1.7 collective-permute-start.35
  251.1 7.3 %attend_back.1 = (f32[128,1024]{1,0:T(8,128)}, f32[1024,128]{1,0:T(8,128)}, bf16[1024,128]{1,0:T(8,128)(2,1)}, bf16[1024,128]{1,0:T(8,128)(2,1)}, bf16[1024,128]{1,0:T(8,128)(2,1)}) custom-call(s32[1]{0:T(128)} %bitcast.c_ref, bf16[128,1024]{1,0:T(8,128)(2,1)} %get-tuple-element.121.q_ref, bf16[8,128,128]{2,1,0:T(8,128)(2,1)} %copy-done.41, ...), custom_call_target="tpu_custom_call" | custom-call | flops 25769803776 | bytes 2097152 | tf_op jit(solution)/shard_map/attend_back/pallas_call | solution.py:349
  258.4 5.1 %collective-permute-done.34.refs_5_ = bf16[256,1024]{1,0:T(8,128)(2,1)S(1)} collective-permute-done((bf16[256,1024]{1,0:T(8,128)(2,1)}, bf16[256,1024]{1,0:T(8,128)(2,1)S(1)}, u32[]{:S(2)}, u32[]{:S(2)}) %collective-permute-start.34) | collective-permute-done | bytes 524320 | tf_op jit(solution)/shard_map/ppermute | solution.py:742
  263.5 9.9 %collective-permute-done.36.refs_7_ = bf16[256,1024]{1,0:T(8,128)(2,1)S(1)} collective-permute-done((bf16[256,1024]{1,0:T(8,128)(2,1)S(1)}, bf16[256,1024]{1,0:T(8,128)(2,1)S(1)}, u32[]{:S(2)}, u32[]{:S(2)}) %collective-permute-start.36) | collective-permute-done | bytes 524320 | tf_op jit(solution)/shard_map/ppermute | solution.py:742
  273.5 3.3 collective-permute-start.37
  278.5 5.3 %collective-permute-done.37.refs_1_ = bf16[1024,128]{1,0:T(8,128)(2,1)S(1)} collective-permute-done((bf16[1024,128]{1,0:T(8,128)(2,1)}, bf16[1024,128]{1,0:T(8,128)(2,1)S(1)}, u32[]{:S(2)}, u32[]{:S(2)}) %collective-permute-start.37) | collective-permute-done | bytes 262176 | tf_op jit(solution)/shard_map/ppermute | solution.py:742
  283.8 5.5 %collective-permute-done.38.refs_2_ = bf16[1024,128]{1,0:T(8,128)(2,1)S(1)} collective-permute-done((bf16[1024,128]{1,0:T(8,128)(2,1)}, bf16[1024,128]{1,0:T(8,128)(2,1)S(1)}, u32[]{:S(2)}, u32[]{:S(2)}) %collective-permute-start.38) | collective-permute-done | bytes 262176 | tf_op jit(solution)/shard_map/ppermute | solution.py:742
  290.0 7.5 %tail.1 = (bf16[4,160,1024]{2,1,0:T(8,128)(2,1)}, bf16[4,160,1024]{2,1,0:T(8,128)(2,1)}, bf16[256,384]{1,0:T(8,128)(2,1)}, bf16[256,384]{1,0:T(8,128)(2,1)}, bf1...) custom-call(s32[2]{0:T(128)} %pad_add_fusion.at_ref, f32[128,1024]{1,0:T(8,128)} %get-tuple-element.169.gq_ref, ...), custom_call_target="tpu_custom_call" | custom-call | flops 1073741824 | bytes 12582912 | tf_op jit(solution)/shard_map/tail/pallas_call | solution.py:443
  297.5 3.2 collective-permute-done.40
  300.7 1.9 add_convert_fusion
  306.5 1.7 collective-permute-start.46
  308.2 2.9 collective-permute-done.41
  311.7 4.7 %collective-permute-start.48 = (bf16[128,1024]{1,0:T(8,128)(2,1)}, bf16[128,1024]{1,0:T(8,128)(2,1)}, u32[]{:S(2)}, u32[]{:S(2)}) collective-permute-start(bf16[128,1024]{1,0:T(8,128)(2,1)} %get-tuple-element.197), channel_id=1, source_target_pairs={{0,8},{8,16},{16,24},{24,0},{1,9},{9,17},{17,25},{25,1},{2,10},{10... | collective-permute-start | bytes 786440 | tf_op jit(solution)/shard_map/ppermute | solution.py:742
  316.4 1.9 add_convert_fusion.2
  318.3 16.0 %collective-permute-done.44 = bf16[2,160,1024]{2,1,0:T(8,128)(2,1)S(1)} collective-permute-done((bf16[2,160,1024]{2,1,0:T(8,128)(2,1)S(1)}, bf16[2,160,1024]{2,1,0:T(8,128)(2,1)S(1)}, u32[]{:S(2)}, u32[]{:S(2)}) %collective-permute-start.44) | collective-permute-done | bytes 655392 | tf_op jit(solution)/shard_map/ppermute | solution.py:881
  335.3 4.2 %all-to-all-start.3 = ((bf16[8,32,384]{2,1,0:T(8,128)(2,1)}), bf16[8,32,384]{2,1,0:T(8,128)(2,1)S(1)}, u32[]{:S(2)}, u32[]{:S(2)}) async-start(bf16[8,32,384]{2,1,0:T(8,128)(2,1)} %bitcast.34), calls=%async_computation.3 | async-start | bytes 393216 | tf_op jit(solution)/shard_map/all_to_all | solution.py:765
  340.3 2.1 add_convert_fusion.1
  342.4 3.4 unpack.1
  345.8 9.4 %collective-permute-done.45 = bf16[1,160,1024]{2,1,0:T(8,128)(2,1)S(1)} collective-permute-done((bf16[1,160,1024]{2,1,0:T(8,128)(2,1)S(1)}, bf16[1,160,1024]{2,1,0:T(8,128)(2,1)S(1)}, u32[]{:S(2)}, u32[]{:S(2)}) %collective-permute-start.45) | collective-permute-done | bytes 327712 | tf_op jit(solution)/shard_map/ppermute | solution.py:881
  355.2 1.5 all-to-all-done.3.late_ref
  357.3 2.7 finish.1
  (253 shorter events, 54.7 us)
Async XLA Ops:
  7.2 66.2 %all-gather.5.cloned.1.call-start = ((), (), s32[]{:S(2)}) async-start(), calls=%async_computation.8 | async-start | bytes 3538944 | tf_op jit(solution)/shard_map/all_gather | solution.py:957
  11.0 24.7 %copy-start.17 = (bf16[144,1024]{1,0:T(8,128)(2,1)}, bf16[144,1024]{1,0:T(8,128)(2,1)S(1)}, u32[]{:S(2)}) copy-start(bf16[144,1024]{1,0:T(8,128)(2,1)S(1)} %pad_maximum_fusion.3.refs_0_) | copy-start | bytes 884740
  11.0 12.2 %collective-permute-start = (bf16[144,1024]{1,0:T(8,128)(2,1)S(1)}, bf16[144,1024]{1,0:T(8,128)(2,1)S(1)}, u32[]{:S(2)}, u32[]{:S(2)}) collective-permute-start(bf16[144,1024]{1,0:T(8,128)(2,1)S(1)} %pad_maximum_fusion.3.refs_0_), channel_id=1, source_target_pairs={{0,2},{1,3},{2,4},{3,5},{4,6},{5,7},{8,10},{9,11},{10,12},{11,13},... | collective-permute-start | bytes 884744 | tf_op jit(solution)/shard_map/ppermute | solution.py:796
  15.9 18.5 %collective-permute-start.1 = (bf16[144,1024]{1,0:T(8,128)(2,1)S(1)}, bf16[144,1024]{1,0:T(8,128)(2,1)}, u32[]{:S(2)}, u32[]{:S(2)}) collective-permute-start(bf16[144,1024]{1,0:T(8,128)(2,1)S(1)} %pad_maximum_fusion.3.refs_0_), channel_id=1, source_target_pairs={{2,0},{3,1},{4,2},{5,3},{6,4},{7,5},{10,8},{11,9},{12,10},{13,11},... | collective-permute-start | bytes 884744 | tf_op jit(solution)/shard_map/ppermute | solution.py:796
  23.2 23.9 %collective-permute-start.4 = (bf16[144,1024]{1,0:T(8,128)(2,1)S(1)}, bf16[144,1024]{1,0:T(8,128)(2,1)}, u32[]{:S(2)}, u32[]{:S(2)}) collective-permute-start(bf16[144,1024]{1,0:T(8,128)(2,1)S(1)} %collective-permute-done), channel_id=1, source_target_pairs={{2,4},{3,5},{4,6},{5,7},{10,12},{11,13},{12,14},{13,15},{18,20},{1... | collective-permute-start | bytes 884744 | tf_op jit(solution)/shard_map/ppermute | solution.py:796
  34.4 26.4 %collective-permute-start.2 = (bf16[144,1024]{1,0:T(8,128)(2,1)}, bf16[144,1024]{1,0:T(8,128)(2,1)}, u32[]{:S(2)}, u32[]{:S(2)}) collective-permute-start(bf16[144,1024]{1,0:T(8,128)(2,1)} %collective-permute-done.1), channel_id=1, source_target_pairs={{2,0},{3,1},{4,2},{5,3},{10,8},{11,9},{12,10},{13,11},{18,16},{19,... | collective-permute-start | bytes 884744 | tf_op jit(solution)/shard_map/ppermute | solution.py:796
  37.7 35.7 %all-to-all-start = ((bf16[8,128,256]{2,1,0:T(8,128)(2,1)}), bf16[8,128,256]{2,1,0:T(8,128)(2,1)S(1)}, u32[]{:S(2)}, u32[]{:S(2)}) async-start(bf16[8,128,256]{2,1,0:T(8,128)(2,1)} %copy.118), calls=%async_computation | async-start | bytes 1048576 | tf_op jit(solution)/shard_map/all_to_all | solution.py:765
  42.5 137.2 %all-gather.7.cloned.1.call-start = ((), (), s32[]{:S(2)}) async-start(), calls=%async_computation.9 | async-start | bytes 10616832 | tf_op jit(solution)/shard_map/all_gather | solution.py:958
  42.6 30.8 %collective-permute-start.6 = (bf16[128,1024]{1,0:T(8,128)(2,1)}, bf16[128,1024]{1,0:T(8,128)(2,1)}, u32[]{:S(2)}, u32[]{:S(2)}) collective-permute-start(bf16[128,1024]{1,0:T(8,128)(2,1)} %refs_4_.1), channel_id=1, source_target_pairs={{0,8},{8,16},{16,24},{24,0},{1,9},{9,17},{17,25},{25,1},{2,10},{10... | collective-permute-start | bytes 786440 | tf_op jit(solution)/shard_map/ppermute | solution.py:742
  44.1 29.3 %collective-permute-start.7 = (bf16[128,1024]{1,0:T(8,128)(2,1)}, bf16[128,1024]{1,0:T(8,128)(2,1)}, u32[]{:S(2)}, u32[]{:S(2)}) collective-permute-start(bf16[128,1024]{1,0:T(8,128)(2,1)} %refs_4_.1), channel_id=1, source_target_pairs={{0,16},{8,24},{16,0},{24,8},{1,17},{9,25},{17,1},{25,9},{2,18},{10... | collective-permute-start | bytes 786440 | tf_op jit(solution)/shard_map/ppermute | solution.py:742
  45.6 27.8 %collective-permute-start.8 = (bf16[128,1024]{1,0:T(8,128)(2,1)}, bf16[128,1024]{1,0:T(8,128)(2,1)}, u32[]{:S(2)}, u32[]{:S(2)}) collective-permute-start(bf16[128,1024]{1,0:T(8,128)(2,1)} %refs_4_.1), channel_id=1, source_target_pairs={{0,24},{8,0},{16,8},{24,16},{1,25},{9,1},{17,9},{25,17},{2,26},{10... | collective-permute-start | bytes 786440 | tf_op jit(solution)/shard_map/ppermute | solution.py:742
  47.1 16.0 %collective-permute-start.5 = (bf16[144,1024]{1,0:T(8,128)(2,1)}, bf16[144,1024]{1,0:T(8,128)(2,1)}, u32[]{:S(2)}, u32[]{:S(2)}) collective-permute-start(bf16[144,1024]{1,0:T(8,128)(2,1)} %collective-permute-done.4), channel_id=1, source_target_pairs={{4,6},{5,7},{12,14},{13,15},{20,22},{21,23},{28,30},{29,31}} | collective-permute-start | bytes 884744 | tf_op jit(solution)/shard_map/ppermute | solution.py:796
  50.7 23.5 %copy-start.18 = (bf16[144,1024]{1,0:T(8,128)(2,1)S(1)}, bf16[144,1024]{1,0:T(8,128)(2,1)}, u32[]{:S(2)}) copy-start(bf16[144,1024]{1,0:T(8,128)(2,1)} %copy-done.17) | copy-start | bytes 884740
  60.8 12.5 %collective-permute-start.3 = (bf16[144,1024]{1,0:T(8,128)(2,1)}, bf16[144,1024]{1,0:T(8,128)(2,1)S(1)}, u32[]{:S(2)}, u32[]{:S(2)}) collective-permute-start(bf16[144,1024]{1,0:T(8,128)(2,1)} %collective-permute-done.2), channel_id=1, source_target_pairs={{2,0},{3,1},{10,8},{11,9},{18,16},{19,17},{26,24},{27,25}} | collective-permute-start | bytes 884744 | tf_op jit(solution)/shard_map/ppermute | solution.py:796
  73.6 2.9 collective-permute-start.10
  73.6 2.8 collective-permute-start.11
  74.1 2.4 collective-permute-start.12
  74.2 2.3 collective-permute-start.9
  82.9 4.7 %collective-permute-start.16 = (bf16[16,1024]{1,0:T(8,128)(2,1)S(1)}, bf16[16,1024]{1,0:T(8,128)(2,1)S(1)}, u32[]{:S(2)}, u32[]{:S(2)}) collective-permute-start(bf16[16,1024]{1,0:T(8,128)(2,1)S(1)} %dynamic-slice_bitcast_fusion.2), channel_id=1, source_target_pairs={{0,1},{1,0},{2,3},{3,2},{4,5},{5,4},{6,7},{7,6},{8,9},{9,8},{10,11... | collective-permute-start | bytes 98312 | tf_op jit(solution)/shard_map/ppermute | solution.py:778
  83.1 10.3 %collective-permute-start.13 = (bf16[128,1024]{1,0:T(8,128)(2,1)}, bf16[128,1024]{1,0:T(8,128)(2,1)S(1)}, u32[]{:S(2)}, u32[]{:S(2)}) collective-permute-start(bf16[128,1024]{1,0:T(8,128)(2,1)} %get-tuple-element.122.refs_0_), channel_id=1, source_target_pairs={{0,8},{8,16},{16,24},{24,0},{1,9},{9,17},{17,25},{25,1},{2,10},{10... | collective-permute-start | bytes 786440 | tf_op jit(solution)/shard_map/ppermute | solution.py:742
  84.6 13.9 %collective-permute-start.14 = (bf16[128,1024]{1,0:T(8,128)(2,1)}, bf16[128,1024]{1,0:T(8,128)(2,1)S(1)}, u32[]{:S(2)}, u32[]{:S(2)}) collective-permute-start(bf16[128,1024]{1,0:T(8,128)(2,1)} %get-tuple-element.122.refs_0_), channel_id=1, source_target_pairs={{0,16},{8,24},{16,0},{24,8},{1,17},{9,25},{17,1},{25,9},{2,18},{10... | collective-permute-start | bytes 786440 | tf_op jit(solution)/shard_map/ppermute | solution.py:742
  86.2 12.5 %collective-permute-start.15 = (bf16[128,1024]{1,0:T(8,128)(2,1)}, bf16[128,1024]{1,0:T(8,128)(2,1)S(1)}, u32[]{:S(2)}, u32[]{:S(2)}) collective-permute-start(bf16[128,1024]{1,0:T(8,128)(2,1)} %get-tuple-element.122.refs_0_), channel_id=1, source_target_pairs={{0,24},{8,0},{16,8},{24,16},{1,25},{9,1},{17,9},{25,17},{2,26},{10... | collective-permute-start | bytes 786440 | tf_op jit(solution)/shard_map/ppermute | solution.py:742
  88.4 17.7 %collective-permute-start.17 = (bf16[2,16,1024]{2,1,0:T(8,128)(2,1)S(1)}, bf16[2,16,1024]{2,1,0:T(8,128)(2,1)S(1)}, u32[]{:S(2)}, u32[]{:S(2)}) collective-permute-start(bf16[2,16,1024]{2,1,0:T(8,128)(2,1)S(1)} %pad_maximum_fusion.5), channel_id=1, source_target_pairs={{0,2},{1,3},{2,4},{3,5},{4,6},{5,7},{6,0},{7,1},{8,10},{9,11},{10,... | collective-permute-start | bytes 196616 | tf_op jit(solution)/shard_map/ppermute | solution.py:770
  89.0 17.1 %collective-permute-start.18 = (bf16[2,16,1024]{2,1,0:T(8,128)(2,1)S(1)}, bf16[2,16,1024]{2,1,0:T(8,128)(2,1)S(1)}, u32[]{:S(2)}, u32[]{:S(2)}) collective-permute-start(bf16[2,16,1024]{2,1,0:T(8,128)(2,1)S(1)} %pad_maximum_fusion.5), channel_id=1, source_target_pairs={{0,4},{1,5},{2,6},{3,7},{4,0},{5,1},{6,2},{7,3},{8,12},{9,13},{10,... | collective-permute-start | bytes 196616 | tf_op jit(solution)/shard_map/ppermute | solution.py:770
  93.4 12.7 %collective-permute-start.19 = (bf16[2,16,1024]{2,1,0:T(8,128)(2,1)S(1)}, bf16[2,16,1024]{2,1,0:T(8,128)(2,1)S(1)}, u32[]{:S(2)}, u32[]{:S(2)}) collective-permute-start(bf16[2,16,1024]{2,1,0:T(8,128)(2,1)S(1)} %pad_maximum_fusion.5), channel_id=1, source_target_pairs={{0,6},{1,7},{2,0},{3,1},{4,2},{5,3},{6,4},{7,5},{8,14},{9,15},{10,... | collective-permute-start | bytes 196616 | tf_op jit(solution)/shard_map/ppermute | solution.py:770
  100.6 33.7 %copy-start.13 = (bf16[128,8,256]{0,2,1:T(8,128)(2,1)S(1)}, bf16[128,8,256]{0,2,1:T(8,128)(2,1)}, u32[]{:S(2)}) copy-start(bf16[128,8,256]{0,2,1:T(8,128)(2,1)} %get-tuple-element.230) | copy-start | bytes 1572868
  106.2 37.3 %copy-start.19 = (bf16[4,2,16,1024]{3,2,1,0:T(8,128)(2,1)}, bf16[4,2,16,1024]{3,2,1,0:T(8,128)(2,1)S(1)}, u32[]{:S(2)}) copy-start(bf16[4,2,16,1024]{3,2,1,0:T(8,128)(2,1)S(1)} %bitcast_dynamic-update-slice_fusion.refs_0_) | copy-start | bytes 786436
  106.3 21.8 %collective-permute-start.20 = (bf16[4,2,16,1024]{3,2,1,0:T(8,128)(2,1)S(1)}, bf16[4,2,16,1024]{3,2,1,0:T(8,128)(2,1)S(1)}, u32[]{:S(2)}, u32[]{:S(2)}) collective-permute-start(bf16[4,2,16,1024]{3,2,1,0:T(8,128)(2,1)S(1)} %bitcast_dynamic-update-slice_fusion.refs_0_), channel_id=1, source_target_pairs={{0,8},{8,16},{16,24},{24,0},{1,9},{9,17},{17,25},{25,1},{2,10},{10... | collective-permute-start | bytes 786440 | tf_op jit(solution)/shard_map/ppermute | solution.py:742
  112.4 20.0 %collective-permute-start.21 = (bf16[4,2,16,1024]{3,2,1,0:T(8,128)(2,1)S(1)}, bf16[4,2,16,1024]{3,2,1,0:T(8,128)(2,1)S(1)}, u32[]{:S(2)}, u32[]{:S(2)}) collective-permute-start(bf16[4,2,16,1024]{3,2,1,0:T(8,128)(2,1)S(1)} %bitcast_dynamic-update-slice_fusion.refs_0_), channel_id=1, source_target_pairs={{0,16},{8,24},{16,0},{24,8},{1,17},{9,25},{17,1},{25,9},{2,18},{10... | collective-permute-start | bytes 786440 | tf_op jit(solution)/shard_map/ppermute | solution.py:742
  121.4 11.1 %collective-permute-start.22 = (bf16[4,2,16,1024]{3,2,1,0:T(8,128)(2,1)S(1)}, bf16[4,2,16,1024]{3,2,1,0:T(8,128)(2,1)S(1)}, u32[]{:S(2)}, u32[]{:S(2)}) collective-permute-start(bf16[4,2,16,1024]{3,2,1,0:T(8,128)(2,1)S(1)} %bitcast_dynamic-update-slice_fusion.refs_0_), channel_id=1, source_target_pairs={{0,24},{8,0},{16,8},{24,16},{1,25},{9,1},{17,9},{25,17},{2,26},{10... | collective-permute-start | bytes 786440 | tf_op jit(solution)/shard_map/ppermute | solution.py:742
  121.9 21.6 %all-to-all-start.1 = ((bf16[8,128,128]{2,1,0:T(8,128)(2,1)}), bf16[8,128,128]{2,1,0:T(8,128)(2,1)S(1)}, u32[]{:S(2)}, u32[]{:S(2)}) async-start(bf16[8,128,128]{2,1,0:T(8,128)(2,1)} %get-tuple-element.125), calls=%async_computation.1 | async-start | bytes 524288 | tf_op jit(solution)/shard_map/all_to_all | solution.py:765
  125.4 100.5 %reduce-scatter.3.cloned.1.call-start = ((), (), s32[]{:S(2)}) async-start(), calls=%async_computation.6 | async-start | bytes 3538944 | tf_op jit(solution)/shard_map/reduce_scatter | solution.py:1027
  125.4 11.7 %collective-permute-start.23 = (bf16[4,2,16,1024]{3,2,1,0:T(8,128)(2,1)S(1)}, bf16[4,2,16,1024]{3,2,1,0:T(8,128)(2,1)S(1)}, u32[]{:S(2)}, u32[]{:S(2)}) collective-permute-start(bf16[4,2,16,1024]{3,2,1,0:T(8,128)(2,1)S(1)} %bitcast_dynamic-update-slice_fusion.refs_0_), channel_id=1, source_target_pairs={{0,1},{1,0},{2,3},{3,2},{4,5},{5,4},{6,7},{7,6},{8,9},{9,8},{10,11... | collective-permute-start | bytes 786440 | tf_op jit(solution)/shard_map/ppermute | solution.py:778
  128.1 15.4 %collective-permute-start.24 = (bf16[4,2,16,1024]{3,2,1,0:T(8,128)(2,1)S(1)}, bf16[4,2,16,1024]{3,2,1,0:T(8,128)(2,1)S(1)}, u32[]{:S(2)}, u32[]{:S(2)}) collective-permute-start(bf16[4,2,16,1024]{3,2,1,0:T(8,128)(2,1)S(1)} %collective-permute-done.20.refs_1_), channel_id=1, source_target_pairs={{0,1},{1,0},{2,3},{3,2},{4,5},{5,4},{6,7},{7,6},{8,9},{9,8},{10,11... | collective-permute-start | bytes 786440 | tf_op jit(solution)/shard_map/ppermute | solution.py:778
  132.4 11.1 %collective-permute-start.25 = (bf16[4,2,16,1024]{3,2,1,0:T(8,128)(2,1)S(1)}, bf16[4,2,16,1024]{3,2,1,0:T(8,128)(2,1)}, u32[]{:S(2)}, u32[]{:S(2)}) collective-permute-start(bf16[4,2,16,1024]{3,2,1,0:T(8,128)(2,1)S(1)} %collective-permute-done.21.refs_2_), channel_id=1, source_target_pairs={{0,1},{1,0},{2,3},{3,2},{4,5},{5,4},{6,7},{7,6},{8,9},{9,8},{10,11... | collective-permute-start | bytes 786440 | tf_op jit(solution)/shard_map/ppermute | solution.py:778
  132.5 10.9 %collective-permute-start.26 = (bf16[4,2,16,1024]{3,2,1,0:T(8,128)(2,1)S(1)}, bf16[4,2,16,1024]{3,2,1,0:T(8,128)(2,1)}, u32[]{:S(2)}, u32[]{:S(2)}) collective-permute-start(bf16[4,2,16,1024]{3,2,1,0:T(8,128)(2,1)S(1)} %collective-permute-done.22.refs_3_), channel_id=1, source_target_pairs={{0,1},{1,0},{2,3},{3,2},{4,5},{5,4},{6,7},{7,6},{8,9},{9,8},{10,11... | collective-permute-start | bytes 786440 | tf_op jit(solution)/shard_map/ppermute | solution.py:778
  150.5 10.9 %collective-permute-start.27 = (bf16[128,1152]{1,0:T(8,128)(2,1)S(1)}, bf16[128,1152]{1,0:T(8,128)(2,1)S(1)}, u32[]{:S(2)}, u32[]{:S(2)}) collective-permute-start(bf16[128,1152]{1,0:T(8,128)(2,1)S(1)} %concatenate.24.refs_0_), channel_id=1, source_target_pairs={{0,8},{8,16},{16,24},{24,0},{1,9},{9,17},{17,25},{25,1},{2,10},{10... | collective-permute-start | bytes 884744 | tf_op jit(solution)/shard_map/ppermute | solution.py:742
  152.0 16.2 %collective-permute-start.28 = (bf16[128,1152]{1,0:T(8,128)(2,1)S(1)}, bf16[128,1152]{1,0:T(8,128)(2,1)S(1)}, u32[]{:S(2)}, u32[]{:S(2)}) collective-permute-start(bf16[128,1152]{1,0:T(8,128)(2,1)S(1)} %concatenate.24.refs_0_), channel_id=1, source_target_pairs={{0,16},{8,24},{16,0},{24,8},{1,17},{9,25},{17,1},{25,9},{2,18},{10... | collective-permute-start | bytes 884744 | tf_op jit(solution)/shard_map/ppermute | solution.py:742
  153.4 14.9 %collective-permute-start.29 = (bf16[128,1152]{1,0:T(8,128)(2,1)S(1)}, bf16[128,1152]{1,0:T(8,128)(2,1)S(1)}, u32[]{:S(2)}, u32[]{:S(2)}) collective-permute-start(bf16[128,1152]{1,0:T(8,128)(2,1)S(1)} %concatenate.24.refs_0_), channel_id=1, source_target_pairs={{0,24},{8,0},{16,8},{24,16},{1,25},{9,1},{17,9},{25,17},{2,26},{10... | collective-permute-start | bytes 884744 | tf_op jit(solution)/shard_map/ppermute | solution.py:742
  155.0 1.2 collective-permute-start.30
  156.2 23.4 %copy-start.43 = (bf16[32,2048]{1,0:T(8,128)(2,1)}, bf16[32,2048]{1,0:T(8,128)(2,1)S(1)}, u32[]{:S(2)}) copy-start(bf16[32,2048]{1,0:T(8,128)(2,1)S(1)} %collective-permute-done.30.weight_ref) | copy-start | bytes 393220
  179.6 162.8 %reduce-scatter.5.cloned.1.call-start = ((), (), s32[]{:S(2)}) async-start(), calls=%async_computation.7 | async-start | bytes 10616832 | tf_op jit(solution)/shard_map/reduce_scatter | solution.py:1028
  204.6 10.3 %collective-permute-start.31 = (bf16[128,1152]{1,0:T(8,128)(2,1)}, bf16[128,1152]{1,0:T(8,128)(2,1)S(1)}, u32[]{:S(2)}, u32[]{:S(2)}) collective-permute-start(bf16[128,1152]{1,0:T(8,128)(2,1)} %get-tuple-element.154), channel_id=1, source_target_pairs={{0,24},{8,0},{16,8},{24,16},{1,25},{9,1},{17,9},{25,17},{2,26},{10... | collective-permute-start | bytes 884744 | tf_op jit(solution)/shard_map/ppermute | solution.py:742
  207.6 15.3 %collective-permute-start.32 = (bf16[128,1152]{1,0:T(8,128)(2,1)}, bf16[128,1152]{1,0:T(8,128)(2,1)S(1)}, u32[]{:S(2)}, u32[]{:S(2)}) collective-permute-start(bf16[128,1152]{1,0:T(8,128)(2,1)} %get-tuple-element.155), channel_id=1, source_target_pairs={{0,16},{8,24},{16,0},{24,8},{1,17},{9,25},{17,1},{25,9},{2,18},{10... | collective-permute-start | bytes 884744 | tf_op jit(solution)/shard_map/ppermute | solution.py:742
  209.2 15.5 %collective-permute-start.33 = (bf16[128,1152]{1,0:T(8,128)(2,1)}, bf16[128,1152]{1,0:T(8,128)(2,1)S(1)}, u32[]{:S(2)}, u32[]{:S(2)}) collective-permute-start(bf16[128,1152]{1,0:T(8,128)(2,1)} %get-tuple-element.156), channel_id=1, source_target_pairs={{0,8},{8,16},{16,24},{24,0},{1,9},{9,17},{17,25},{25,1},{2,10},{10... | collective-permute-start | bytes 884744 | tf_op jit(solution)/shard_map/ppermute | solution.py:742
  230.2 17.5 %all-to-all-start.2 = ((bf16[8,128,128]{2,1,0:T(8,128)(2,1)}), bf16[8,128,128]{2,1,0:T(8,128)(2,1)S(1)}, u32[]{:S(2)}, u32[]{:S(2)}) async-start(bf16[8,128,128]{2,1,0:T(8,128)(2,1)} %bitcast.29), calls=%async_computation.2 | async-start | bytes 524288 | tf_op jit(solution)/shard_map/all_to_all | solution.py:765
  248.5 15.1 %collective-permute-start.34 = (bf16[256,1024]{1,0:T(8,128)(2,1)}, bf16[256,1024]{1,0:T(8,128)(2,1)S(1)}, u32[]{:S(2)}, u32[]{:S(2)}) collective-permute-start(bf16[256,1024]{1,0:T(8,128)(2,1)} %convolution_convert_fusion.2), channel_id=1, source_target_pairs={{0,24},{8,0},{16,8},{24,16},{1,25},{9,1},{17,9},{25,17},{2,26},{10... | collective-permute-start | bytes 1572872 | tf_op jit(solution)/shard_map/ppermute | solution.py:742
  248.5 15.1 %collective-permute-start.35 = (bf16[256,1024]{1,0:T(8,128)(2,1)}, bf16[256,1024]{1,0:T(8,128)(2,1)S(1)}, u32[]{:S(2)}, u32[]{:S(2)}) collective-permute-start(bf16[256,1024]{1,0:T(8,128)(2,1)} %convolution_convert_fusion.1), channel_id=1, source_target_pairs={{0,16},{8,24},{16,0},{24,8},{1,17},{9,25},{17,1},{25,9},{2,18},{10... | collective-permute-start | bytes 1572872 | tf_op jit(solution)/shard_map/ppermute | solution.py:742
  250.2 23.3 %collective-permute-start.36 = (bf16[256,1024]{1,0:T(8,128)(2,1)S(1)}, bf16[256,1024]{1,0:T(8,128)(2,1)S(1)}, u32[]{:S(2)}, u32[]{:S(2)}) collective-permute-start(bf16[256,1024]{1,0:T(8,128)(2,1)S(1)} %convolution_convert_fusion), channel_id=1, source_target_pairs={{0,8},{8,16},{16,24},{24,0},{1,9},{9,17},{17,25},{25,1},{2,10},{10... | collective-permute-start | bytes 1572872 | tf_op jit(solution)/shard_map/ppermute | solution.py:742
  263.5 25.7 %copy-start.21 = (bf16[256,1024]{1,0:T(8,128)(2,1)}, bf16[256,1024]{1,0:T(8,128)(2,1)S(1)}, u32[]{:S(2)}) copy-start(bf16[256,1024]{1,0:T(8,128)(2,1)S(1)} %collective-permute-done.34.refs_5_) | copy-start | bytes 1572868
  263.5 25.7 %copy-start.22 = (bf16[256,1024]{1,0:T(8,128)(2,1)}, bf16[256,1024]{1,0:T(8,128)(2,1)S(1)}, u32[]{:S(2)}) copy-start(bf16[256,1024]{1,0:T(8,128)(2,1)S(1)} %collective-permute-done.35.refs_6_) | copy-start | bytes 1572868
  273.5 10.3 %collective-permute-start.37 = (bf16[1024,128]{1,0:T(8,128)(2,1)}, bf16[1024,128]{1,0:T(8,128)(2,1)S(1)}, u32[]{:S(2)}, u32[]{:S(2)}) collective-permute-start(bf16[1024,128]{1,0:T(8,128)(2,1)} %get-tuple-element.172), channel_id=1, source_target_pairs={{0,24},{8,0},{16,8},{24,16},{1,25},{9,1},{17,9},{25,17},{2,26},{10... | collective-permute-start | bytes 786440 | tf_op jit(solution)/shard_map/ppermute | solution.py:742
  276.7 12.6 %collective-permute-start.38 = (bf16[1024,128]{1,0:T(8,128)(2,1)}, bf16[1024,128]{1,0:T(8,128)(2,1)S(1)}, u32[]{:S(2)}, u32[]{:S(2)}) collective-permute-start(bf16[1024,128]{1,0:T(8,128)(2,1)} %get-tuple-element.173), channel_id=1, source_target_pairs={{0,16},{8,24},{16,0},{24,8},{1,17},{9,25},{17,1},{25,9},{2,18},{10... | collective-permute-start | bytes 786440 | tf_op jit(solution)/shard_map/ppermute | solution.py:742
  276.7 12.6 %collective-permute-start.39 = (bf16[1024,128]{1,0:T(8,128)(2,1)}, bf16[1024,128]{1,0:T(8,128)(2,1)}, u32[]{:S(2)}, u32[]{:S(2)}) collective-permute-start(bf16[1024,128]{1,0:T(8,128)(2,1)} %get-tuple-element.174), channel_id=1, source_target_pairs={{0,8},{8,16},{16,24},{24,0},{1,9},{9,17},{17,25},{25,1},{2,10},{10... | collective-permute-start | bytes 786440 | tf_op jit(solution)/shard_map/ppermute | solution.py:742
  297.4 3.3 collective-permute-start.40
  302.7 31.6 %collective-permute-start.44 = (bf16[2,160,1024]{2,1,0:T(8,128)(2,1)S(1)}, bf16[2,160,1024]{2,1,0:T(8,128)(2,1)S(1)}, u32[]{:S(2)}, u32[]{:S(2)}) collective-permute-start(bf16[2,160,1024]{2,1,0:T(8,128)(2,1)S(1)} %dynamic-slice_bitcast_fusion), channel_id=1, source_target_pairs={{0,2},{1,3},{2,0},{3,1},{4,6},{5,7},{6,4},{7,5},{8,10},{9,11},{10,... | collective-permute-start | bytes 1966088 | tf_op jit(solution)/shard_map/ppermute | solution.py:881
  303.0 8.0 %collective-permute-start.41 = (bf16[256,384]{1,0:T(8,128)(2,1)}, bf16[256,384]{1,0:T(8,128)(2,1)S(1)}, u32[]{:S(2)}, u32[]{:S(2)}) collective-permute-start(bf16[256,384]{1,0:T(8,128)(2,1)} %get-tuple-element.186), channel_id=1, source_target_pairs={{0,24},{8,0},{16,8},{24,16},{1,25},{9,1},{17,9},{25,17},{2,26},{10... | collective-permute-start | bytes 589832 | tf_op jit(solution)/shard_map/ppermute | solution.py:742
  303.3 8.3 %collective-permute-start.42 = (bf16[256,384]{1,0:T(8,128)(2,1)}, bf16[256,384]{1,0:T(8,128)(2,1)}, u32[]{:S(2)}, u32[]{:S(2)}) collective-permute-start(bf16[256,384]{1,0:T(8,128)(2,1)} %get-tuple-element.187), channel_id=1, source_target_pairs={{0,16},{8,24},{16,0},{24,8},{1,17},{9,25},{17,1},{25,9},{2,18},{10... | collective-permute-start | bytes 589832 | tf_op jit(solution)/shard_map/ppermute | solution.py:742
  304.5 11.9 %collective-permute-start.43 = (bf16[256,384]{1,0:T(8,128)(2,1)}, bf16[256,384]{1,0:T(8,128)(2,1)}, u32[]{:S(2)}, u32[]{:S(2)}) collective-permute-start(bf16[256,384]{1,0:T(8,128)(2,1)} %get-tuple-element.188), channel_id=1, source_target_pairs={{0,8},{8,16},{16,24},{24,0},{1,9},{9,17},{17,25},{25,1},{2,10},{10... | collective-permute-start | bytes 589832 | tf_op jit(solution)/shard_map/ppermute | solution.py:742
  306.5 33.8 %collective-permute-start.46 = (bf16[128,1024]{1,0:T(8,128)(2,1)}, bf16[128,1024]{1,0:T(8,128)(2,1)}, u32[]{:S(2)}, u32[]{:S(2)}) collective-permute-start(bf16[128,1024]{1,0:T(8,128)(2,1)} %get-tuple-element.195), channel_id=1, source_target_pairs={{0,24},{8,0},{16,8},{24,16},{1,25},{9,1},{17,9},{25,17},{2,26},{10... | collective-permute-start | bytes 786440 | tf_op jit(solution)/shard_map/ppermute | solution.py:742
  311.0 29.3 %collective-permute-start.47 = (bf16[128,1024]{1,0:T(8,128)(2,1)}, bf16[128,1024]{1,0:T(8,128)(2,1)}, u32[]{:S(2)}, u32[]{:S(2)}) collective-permute-start(bf16[128,1024]{1,0:T(8,128)(2,1)} %get-tuple-element.196), channel_id=1, source_target_pairs={{0,16},{8,24},{16,0},{24,8},{1,17},{9,25},{17,1},{25,9},{2,18},{10... | collective-permute-start | bytes 786440 | tf_op jit(solution)/shard_map/ppermute | solution.py:742
  311.7 28.6 %collective-permute-start.48 = (bf16[128,1024]{1,0:T(8,128)(2,1)}, bf16[128,1024]{1,0:T(8,128)(2,1)}, u32[]{:S(2)}, u32[]{:S(2)}) collective-permute-start(bf16[128,1024]{1,0:T(8,128)(2,1)} %get-tuple-element.197), channel_id=1, source_target_pairs={{0,8},{8,16},{16,24},{24,0},{1,9},{9,17},{17,25},{25,1},{2,10},{10... | collective-permute-start | bytes 786440 | tf_op jit(solution)/shard_map/ppermute | solution.py:742
  335.3 19.9 %collective-permute-start.45 = (bf16[1,160,1024]{2,1,0:T(8,128)(2,1)S(1)}, bf16[1,160,1024]{2,1,0:T(8,128)(2,1)S(1)}, u32[]{:S(2)}, u32[]{:S(2)}) collective-permute-start(bf16[1,160,1024]{2,1,0:T(8,128)(2,1)S(1)} %get-tuple-element.228), channel_id=1, source_target_pairs={{0,4},{1,5},{2,6},{3,7},{4,0},{5,1},{6,2},{7,3},{8,12},{9,13},{10,... | collective-permute-start | bytes 983048 | tf_op jit(solution)/shard_map/ppermute | solution.py:881
  335.3 21.4 %all-to-all-start.3 = ((bf16[8,32,384]{2,1,0:T(8,128)(2,1)}), bf16[8,32,384]{2,1,0:T(8,128)(2,1)S(1)}, u32[]{:S(2)}, u32[]{:S(2)}) async-start(bf16[8,32,384]{2,1,0:T(8,128)(2,1)} %bitcast.34), calls=%async_computation.3 | async-start | bytes 393216 | tf_op jit(solution)/shard_map/all_to_all | solution.py:765
  (46 other events, 278.3 us)
Sparse Core Ops, SparseCore 0:
  10.7 57.2 all-gather.4
  73.6 104.1 all-gather.6
  180.1 40.8 reduce-scatter.2
  226.0 114.4 reduce-scatter.4
where the time goes:
time: 373 us; the launch traced here: 367 us
  waiting for transfers between devices  147 us (39%)
  starting transfers between devices  87.6 us (23%)
  Pallas kernels  67.4 us (18%)
  other arithmetic  21.2 us (6%)
  local copies, waits for them, and re-layouts  19.6 us (5%)
  between operations  15.2 us (4%)
  matrix products  8.79 us (2%)
    ppermute x27, waiting for transfers between devices, send_ctx(): lax.ppermute(value, 'ctx', [(i, (i + by) % count) for i in range(count)])  66.3 us
    ppermute x27, starting transfers between devices, send_ctx(): lax.ppermute(value, 'ctx', [(i, (i + by) % count) for i in range(count)])  51.8 us
    pallas_call x2, Pallas kernels, run_experts(): pl.pallas_call(functools.partial(expert_kernel, ctx_count=ctx_count, expe...  34.9 us
    ppermute x6, waiting for transfers between devices, step(): return lax.ppermute(block, 'shard', pairs)  34.5 us
    ppermute x2, waiting for transfers between devices, halve_chips(): lax.ppermute(sent, 'shard', [(i, i ^ 2 * distance) for i in range(shards)])  25.4 us
    all_to_all x4, waiting for transfers between devices, all_to_all(): lax.all_to_all(value, 'shard', split_axis=0, concat_axis=0, tiled=True)  17.4 us
    all_to_all x4, starting transfers between devices, all_to_all(): lax.all_to_all(value, 'shard', split_axis=0, concat_axis=0, tiled=True)  15.8 us
    ppermute x6, starting transfers between devices, step(): return lax.ppermute(block, 'shard', pairs)  11.5 us
  transfers between devices with their start and end apart: 57, of which 26 were waited for; matrix products, arithmetic and copies ran while one was open for 10% of the time, Pallas kernels for 18%

commit v1 on v0

--- a/solution.py
+++ b/solution.py
@@ -241,7 +241,7 @@
             jax.ShapeDtypeStruct((heads, rows), F32),
         ],
         compiler_params=pltpu.CompilerParams(
-            dimension_semantics=("arbitrary",), vmem_limit_bytes=48 << 20
+            dimension_semantics=("arbitrary",), vmem_limit_bytes=60 << 20
         ),
         cost_estimate=pl.CostEstimate(
             flops=64 * width * rows * rows * ctx_count // 2,
@@ -373,7 +373,7 @@
             for k in range(ctx_count)
         ],
         compiler_params=pltpu.CompilerParams(
-            dimension_semantics=("arbitrary",), vmem_limit_bytes=56 << 20
+            dimension_semantics=("arbitrary",), vmem_limit_bytes=60 << 20
         ),
         cost_estimate=pl.CostEstimate(
             flops=96 * width * rows * rows * ctx_count // 2,
@@ -387,10 +387,10 @@
 def tail_kernel(
     at_ref, gq_ref, cos_ref, sin_ref, normed_ref, columns_ref, fine_ref, *refs, ctx_count, tile
 ):
-    kv_refs, early_refs = refs[:ctx_count], refs[ctx_count : 2 * ctx_count]
-    own_ref, other_ref = refs[2 * ctx_count : 2 * ctx_count + 2]
-    late_refs = refs[2 * ctx_count + 2 : 3 * ctx_count + 2]
-    tall, late = refs[3 * ctx_count + 2 :]
+    kv_refs = refs[:ctx_count]
+    own_ref, other_ref = refs[ctx_count : ctx_count + 2]
+    late_refs = refs[ctx_count + 2 : 2 * ctx_count + 2]
+    tall, late = refs[2 * ctx_count + 2 :]
     ctx, core = at_ref[0], at_ref[1]
     q_width = gq_ref.shape[0]
     lin_width = tall.shape[1]
@@ -414,30 +414,23 @@
         first = pl.multiple_of(lax.rem(ctx - k + ctx_count, ctx_count) * block, block)
         late_refs[k][:, :lin_width] = late[pl.ds(first, block), :]
         late_refs[k][:, lin_width:] = fine_ref[pl.ds(first, block), :]
-    early = add_up([ref[...] for ref in early_refs]).astype(BF16)
     chips = own_ref.shape[0]
-    small = own_ref.shape[1] - tile
-    swap = core == 1
     for chip in range(chips):
-        at = [slice((2 * chip + j) * small, (2 * chip + j + 1) * small) for j in range(2)]
-        own_ref[chip, tile:, :] = jnp.where(swap, early[at[1]], early[at[0]])
-        other_ref[chip, tile:, :] = jnp.where(swap, early[at[0]], early[at[1]])
         for side, ref in ((core, own_ref), (1 - core, other_ref)):
             first = pl.multiple_of((2 * chip + side) * tile, tile)
-            ref[chip, :tile, :] = dot(
+            ref[chip] = dot(
                 tall[pl.ds(first, tile), :], columns_ref[...], ((1,), (1,))
             ).astype(BF16)
 
 
-def tail(gq, cosine, sine, normed, columns, fine, kv_back, early_back, at, tile):
+def tail(gq, cosine, sine, normed, columns, fine, kv_back, at, tile):
     ctx_count = len(kv_back)
     rows, width = normed.shape
     lin_width = columns.shape[1]
     chips = rows // (2 * tile)
-    small = early_back[0].shape[0] // (2 * chips)
     block = width // ctx_count
-    args = [at, gq, cosine, sine, normed, columns, fine, *kv_back, *early_back]
-    shapes = [((chips, tile + small, width), BF16)] * 2 + [
+    args = [at, gq, cosine, sine, normed, columns, fine, *kv_back]
+    shapes = [((chips, tile, width), BF16)] * 2 + [
         ((block, lin_width + LANES), BF16)
     ] * ctx_count
     out = pl.pallas_call(
@@ -462,12 +455,13 @@
 ):
     parts = refs[:-8]
     tokens_ref, q_ref, k_ref, v_ref, out_ref, attn_ref, ffn_ref, router_ref = refs[-8:]
-    grad_normed = add_up([ref[:tile, :] for ref in parts])
+    parts, out_parts = parts[: len(parts) // 2], parts[len(parts) // 2 :]
+    grad_normed = add_up([ref[...] for ref in parts])
     inputs = token_ref[...].astype(F32)
     tokens_ref[...] = middle_ref[...] + norm_back(
         grad_normed, inputs, inverse_ref[...], norm_ref[...]
     )
-    out_ref[...] = add_up([ref[tile:, :] for ref in parts])
+    out_ref[...] = add_up([ref[...] for ref in out_parts])
     shards, rows, _ = late_ref.shape
     width = q_width + 2 * HEAD_SIZE
     gain_grad = jnp.zeros((rows, 1), F32)
@@ -1067,23 +1061,30 @@
     out = attend_back(queries, grad_heads, outcome_wide, level, kv_parts, ctx_index)
     early_parts, gq, kv_out = meet(early_parts, out[0], out[1:])
     kv_back = from_later(kv_out)
+    early = add_up(early_parts).astype(BF16).reshape(chips, 2, -1, MODEL_WIDTH)
+    mine = lax.dynamic_index_in_dim(early, shard % 2, 1, keepdims=False)
+    theirs = send_core(lax.dynamic_index_in_dim(early, 1 - shard % 2, 1, keepdims=False))
+    out_back, _ = halve_chips((mine.astype(F32) + theirs.astype(F32)).astype(BF16))
     mix_back = from_later(tie(mix_parts, kv_back))
     at = jnp.stack([ctx, shard % 2]).astype(jnp.int32)
     own, other, late_parts = tail(
-        gq, cosine, sine, normed, columns, fine, kv_back, early_parts, at, tile
+        gq, cosine, sine, normed, columns, fine, kv_back, at, tile
     )
     chip_sum = (own.astype(F32) + send_core(other).astype(F32)).astype(BF16)
-    token_back, halfway = halve_chips(chip_sum)
+    token_back, _ = halve_chips(chip_sum)
     late = to_ctx(tie(late_parts, chip_sum)).astype(BF16)
-    late = all_to_all(tie(late, halfway).reshape(shards, share_rows, -1))
+    late = all_to_all(late.reshape(shards, share_rows, -1))
     expert_grads = unpack(share_first, share_last, depth, down_depth, MODEL_WIDTH)
     block_out = (middle + RESIDUAL_SCALE * add_up(mix_back)).astype(BF16)
-    late, token_back, block_out, expert_grads = meet(late, token_back, block_out, expert_grads)
+    late, token_back, out_back, block_out, expert_grads = meet(
+        late, token_back, out_back, block_out, expert_grads
+    )
     first_row = (ctx * shards + shard) * share_rows
     own_gain = lax.dynamic_slice_in_dim(gain_attn, first_row, share_rows, 0)[:, None]
     grad_tokens, grad_query, grad_key, grad_value, grad_out, grad_gain, grad_gain_ffn, grad_router = (
         finish(
-            late, own_weights, own_gain, grad_middle, tokens, inverse_attn, gain_attn, token_back,
+            late, own_weights, own_gain, grad_middle, tokens, inverse_attn, gain_attn,
+            token_back + out_back,
             q_width, copies, expert_count
         )
     )

time: 373 us -> 369 us (0.989)
  waiting for transfers between devices: 147 us -> 142 us
    reduce_scatter x1, waiting for transfers between devices: 0.01 us -> 11 us  [local(): lax.psum_scatter(tie(grads_last, share_first, back), 'shard', scatter_dim...]
    ppermute x2 -> x4, waiting for transfers between devices: 25.4 us -> 14.7 us  [halve_chips(): lax.ppermute(sent, 'shard', [(i, i ^ 2 * distance) for i in range(shards)])]
    unnamed x112, local copies, waits for them, and re-layouts: 9.74 us -> 5.89 us
  transfers between devices with their start and end apart: 57 -> 60, of which waited for: 26 -> 26; matrix products, arithmetic and copies ran while one was open for 10% -> 11% of each run, Pallas kernels for 18% -> 18%
where the time goes in v1:
time: 369 us; the launch traced here: 362 us
  waiting for transfers between devices  142 us (38%)
  starting transfers between devices  90.7 us (25%)
  Pallas kernels  67.3 us (18%)
  other arithmetic  21.4 us (6%)
  local copies, waits for them, and re-layouts  16.5 us (4%)
  between operations  15.3 us (4%)
  matrix products  8.82 us (2%)
    ppermute x27, waiting for transfers between devices, send_ctx(): lax.ppermute(value, 'ctx', [(i, (i + by) % count) for i in range(count)])  65.1 us
    ppermute x27, starting transfers between devices, send_ctx(): lax.ppermute(value, 'ctx', [(i, (i + by) % count) for i in range(count)])  52.7 us
    pallas_call x2, Pallas kernels, run_experts(): pl.pallas_call(functools.partial(expert_kernel, ctx_count=ctx_count, expe...  34.9 us
    ppermute x6, waiting for transfers between devices, step(): return lax.ppermute(block, 'shard', pairs)  34.5 us
    all_to_all x4, waiting for transfers between devices, all_to_all(): lax.all_to_all(value, 'shard', split_axis=0, concat_axis=0, tiled=True)  17 us
    all_to_all x4, starting transfers between devices, all_to_all(): lax.all_to_all(value, 'shard', split_axis=0, concat_axis=0, tiled=True)  15.8 us
    ppermute x4, waiting for transfers between devices, halve_chips(): lax.ppermute(sent, 'shard', [(i, i ^ 2 * distance) for i in range(shards)])  14.7 us
    ppermute x6, starting transfers between devices, step(): return lax.ppermute(block, 'shard', pairs)  11.5 us
  transfers between devices with their start and end apart: 60, of which 26 were waited for; matrix products, arithmetic and copies ran while one was open for 11% of the time, Pallas kernels for 18%

profile of v1, /device:TPU:0, one launch (start us, length us, event | category | flops | bytes accessed | tf_op | source)
XLA Modules:
  0.0 362.4 jit_solution(15739496618893392894)
XLA Ops:
  11.0 4.9 %collective-permute-start = (bf16[144,1024]{1,0:T(8,128)(2,1)S(1)}, bf16[144,1024]{1,0:T(8,128)(2,1)S(1)}, u32[]{:S(2)}, u32[]{:S(2)}) collective-permute-start(bf16[144,1024]{1,0:T(8,128)(2,1)S(1)} %pad_maximum_fusion.3.refs_0_), channel_id=1, source_target_pairs={{0,2},{1,3},{2,4},{3,5},{4,6},{5,7},{8,10},{9,11},{10,12},{11,13},... | collective-permute-start | bytes 884744 | tf_op jit(solution)/shard_map/ppermute | solution.py:790
  17.3 6.0 %collective-permute-done = bf16[144,1024]{1,0:T(8,128)(2,1)S(1)} collective-permute-done((bf16[144,1024]{1,0:T(8,128)(2,1)S(1)}, bf16[144,1024]{1,0:T(8,128)(2,1)S(1)}, u32[]{:S(2)}, u32[]{:S(2)}) %collective-permute-start) | collective-permute-done | bytes 294944 | tf_op jit(solution)/shard_map/ppermute | solution.py:790
  25.0 9.4 %collective-permute-done.1 = bf16[144,1024]{1,0:T(8,128)(2,1)} collective-permute-done((bf16[144,1024]{1,0:T(8,128)(2,1)S(1)}, bf16[144,1024]{1,0:T(8,128)(2,1)}, u32[]{:S(2)}, u32[]{:S(2)}) %collective-permute-start.1) | collective-permute-done | bytes 294944 | tf_op jit(solution)/shard_map/ppermute | solution.py:790
  37.7 4.8 %all-to-all-start = ((bf16[8,128,256]{2,1,0:T(8,128)(2,1)}), bf16[8,128,256]{2,1,0:T(8,128)(2,1)S(1)}, u32[]{:S(2)}, u32[]{:S(2)}) async-start(bf16[8,128,256]{2,1,0:T(8,128)(2,1)} %copy.126), calls=%async_computation | async-start | bytes 1048576 | tf_op jit(solution)/shard_map/all_to_all | solution.py:759
  42.6 1.5 collective-permute-start.6
  44.1 1.5 collective-permute-start.7
  45.7 1.4 collective-permute-start.8
  50.7 10.0 %collective-permute-done.2 = bf16[144,1024]{1,0:T(8,128)(2,1)} collective-permute-done((bf16[144,1024]{1,0:T(8,128)(2,1)}, bf16[144,1024]{1,0:T(8,128)(2,1)}, u32[]{:S(2)}, u32[]{:S(2)}) %collective-permute-start.2) | collective-permute-done | bytes 294944 | tf_op jit(solution)/shard_map/ppermute | solution.py:790
  64.2 9.1 %collective-permute-done.3 = bf16[144,1024]{1,0:T(8,128)(2,1)S(1)} collective-permute-done((bf16[144,1024]{1,0:T(8,128)(2,1)}, bf16[144,1024]{1,0:T(8,128)(2,1)S(1)}, u32[]{:S(2)}, u32[]{:S(2)}) %collective-permute-start.3) | collective-permute-done | bytes 294944 | tf_op jit(solution)/shard_map/ppermute | solution.py:790
  77.5 4.7 %project.1 = (bf16[1024,1024]{1,0:T(8,128)(2,1)}, bf16[128,1024]{1,0:T(8,128)(2,1)}, bf16[128,1024]{1,0:T(8,128)(2,1)}, bf16[8,16,1024]{2,1,0:T(8,128)(2,1)}) custom-call(s32[2]{0:T(128)} %pad_add_fusion.1.at_ref, bf16[1024,256]{1,0:T(8,128)(2,1)} %bitcast.123, f32[32,1024]{1,0:T(8,128)} %get-tuple-element.242.cos_ref, ...), custom_call_target="tpu_custom_call" | custom-call | flops 536870912 | bytes 4194304 | tf_op jit(solution)/shard_map/project/pallas_call | solution.py:124
  83.1 1.5 collective-permute-start.13
  84.7 1.5 collective-permute-start.14
  86.2 1.4 collective-permute-start.15
  89.1 1.9 collective-permute-start.18
  90.9 2.5 collective-permute-done.13.refs_1_
  93.4 2.1 collective-permute-start.19
  95.5 3.0 collective-permute-done.14.refs_2_
  99.4 5.5 %attend.1 = (bf16[8,128,128]{2,1,0:T(8,128)(2,1)}, f32[128,1024]{1,0:T(8,128)}, f32[2,1024]{1,0:T(2,128)}) custom-call(s32[1]{0:T(128)} %bitcast.c_ref, bf16[128,1024]{1,0:T(8,128)(2,1)} %get-tuple-element.122.q_ref, bf16[128,1024]{1,0:T(8,128)(2,1)} %get-tuple-element.123.refs_0_, bf16[128,1024]{1,0:T(8,128)(2,1)} %copy-done.47, ...), custom_call_target="tpu_custom_call" | custom-call | flops 17179869184 | bytes 1048576 | tf_op jit(solution)/shard_map/attend/pallas_call | solution.py:218
  105.0 6.2 %collective-permute-start.20 = (bf16[4,2,16,1024]{3,2,1,0:T(8,128)(2,1)S(1)}, bf16[4,2,16,1024]{3,2,1,0:T(8,128)(2,1)S(1)}, u32[]{:S(2)}, u32[]{:S(2)}) collective-permute-start(bf16[4,2,16,1024]{3,2,1,0:T(8,128)(2,1)S(1)} %bitcast_dynamic-update-slice_fusion.refs_0_), channel_id=1, source_target_pairs={{0,8},{8,16},{16,24},{24,0},{1,9},{9,17},{17,25},{25,1},{2,10},{10... | collective-permute-start | bytes 786440 | tf_op jit(solution)/shard_map/ppermute | solution.py:736
  111.2 9.0 %collective-permute-start.21 = (bf16[4,2,16,1024]{3,2,1,0:T(8,128)(2,1)S(1)}, bf16[4,2,16,1024]{3,2,1,0:T(8,128)(2,1)S(1)}, u32[]{:S(2)}, u32[]{:S(2)}) collective-permute-start(bf16[4,2,16,1024]{3,2,1,0:T(8,128)(2,1)S(1)} %bitcast_dynamic-update-slice_fusion.refs_0_), channel_id=1, source_target_pairs={{0,16},{8,24},{16,0},{24,8},{1,17},{9,25},{17,1},{25,9},{2,18},{10... | collective-permute-start | bytes 786440 | tf_op jit(solution)/shard_map/ppermute | solution.py:736
  120.7 3.4 all-to-all-start.1
  124.6 2.2 collective-permute-done.20.refs_1_
  126.8 4.3 %collective-permute-done.21.refs_2_ = bf16[4,2,16,1024]{3,2,1,0:T(8,128)(2,1)S(1)} collective-permute-done((bf16[4,2,16,1024]{3,2,1,0:T(8,128)(2,1)S(1)}, bf16[4,2,16,1024]{3,2,1,0:T(8,128)(2,1)S(1)}, u32[]{:S(2)}, u32[]{:S(2)}) %collective-permute-start.21) | collective-permute-done | bytes 262176 | tf_op jit(solution)/shard_map/ppermute | solution.py:736
  135.8 7.4 %all-to-all-done.1 = bf16[8,128,128]{2,1,0:T(8,128)(2,1)S(1)} async-done(((bf16[8,128,128]{2,1,0:T(8,128)(2,1)}), bf16[8,128,128]{2,1,0:T(8,128)(2,1)S(1)}, u32[]{:S(2)}, u32[]{:S(2)}) %all-to-all-start.1) | async-done | bytes 262176 | tf_op jit(solution)/shard_map/all_to_all | solution.py:759
  143.9 3.0 assemble.1
  146.9 2.2 multiply_reduce_fusion.2
  150.2 1.7 collective-permute-start.27
  152.0 2.7 collective-permute-start.29
  155.9 5.3 %collective-permute-done.27.refs_1_ = bf16[128,1152]{1,0:T(8,128)(2,1)S(1)} collective-permute-done((bf16[128,1152]{1,0:T(8,128)(2,1)S(1)}, bf16[128,1152]{1,0:T(8,128)(2,1)S(1)}, u32[]{:S(2)}, u32[]{:S(2)}) %collective-permute-start.27) | collective-permute-done | bytes 294944 | tf_op jit(solution)/shard_map/ppermute | solution.py:736
  161.2 5.9 %collective-permute-done.28.refs_2_ = bf16[128,1152]{1,0:T(8,128)(2,1)S(1)} collective-permute-done((bf16[128,1152]{1,0:T(8,128)(2,1)S(1)}, bf16[128,1152]{1,0:T(8,128)(2,1)S(1)}, u32[]{:S(2)}, u32[]{:S(2)}) %collective-permute-start.28) | collective-permute-done | bytes 294944 | tf_op jit(solution)/shard_map/ppermute | solution.py:736
  168.8 10.0 %experts.2 = (f32[512,1024]{1,0:T(8,128)}, f32[512,1024]{1,0:T(8,128)}, f32[512,128]{1,0:T(8,128)}, bf16[8,1,384,512]{3,2,1,0:T(8,128)(2,1)}) custom-call(s32[1]{0:T(128)} %bitcast.c_ref, bf16[128,1152]{1,0:T(8,128)(2,1)} %copy-done.19, bf16[128,1152]{1,0:T(8,128)(2,1)} %copy-done.44, bf16[128,1152]{1,0:T(8,128)(2,1)} %copy-done.45, ...), custom_call_target="tpu_custom_call" | custom-call | flops 6442450944 | bytes 6291456 | tf_op jit(solution)/shard_map/experts/pallas_call | solution.py:686
  178.9 25.0 %experts.3 = (bf16[128,1152]{1,0:T(8,128)(2,1)}, bf16[128,1152]{1,0:T(8,128)(2,1)}, bf16[128,1152]{1,0:T(8,128)(2,1)}, bf16[128,1152]{1,0:T(8,128)(2,1)}, bf16[1...) custom-call(s32[1]{0:T(128)} %bitcast.c_ref, ...), custom_call_target="tpu_custom_call" | custom-call | flops 19327352832 | bytes 18874368 | tf_op jit(solution)/shard_map/experts/pallas_call | solution.py:686
  203.8 3.5 collective-permute-start.31
  207.4 1.8 collective-permute-start.32
  209.2 2.1 collective-permute-start.33
  211.3 2.9 collective-permute-done.31
  214.2 8.8 %collective-permute-done.32 = bf16[128,1152]{1,0:T(8,128)(2,1)S(1)} collective-permute-done((bf16[128,1152]{1,0:T(8,128)(2,1)}, bf16[128,1152]{1,0:T(8,128)(2,1)S(1)}, u32[]{:S(2)}, u32[]{:S(2)}) %collective-permute-start.32) | collective-permute-done | bytes 294944 | tf_op jit(solution)/shard_map/ppermute | solution.py:736
  223.0 1.7 collective-permute-done.33
  227.1 2.0 multiply_convert_fusion
  229.1 1.4 convolution_convert_fusion.4
  230.5 3.4 all-to-all-start.2
  238.4 9.6 %all-to-all-done.2.grad_ref = bf16[8,128,128]{2,1,0:T(8,128)(2,1)S(1)} async-done(((bf16[8,128,128]{2,1,0:T(8,128)(2,1)}), bf16[8,128,128]{2,1,0:T(8,128)(2,1)S(1)}, u32[]{:S(2)}, u32[]{:S(2)}) %all-to-all-start.2) | async-done | bytes 262176 | tf_op jit(solution)/shard_map/all_to_all | solution.py:759
  248.7 1.7 collective-permute-start.35
  251.4 7.3 %attend_back.1 = (f32[128,1024]{1,0:T(8,128)}, f32[1024,128]{1,0:T(8,128)}, bf16[1024,128]{1,0:T(8,128)(2,1)}, bf16[1024,128]{1,0:T(8,128)(2,1)}, bf16[1024,128]{1,0:T(8,128)(2,1)}) custom-call(s32[1]{0:T(128)} %bitcast.c_ref, bf16[128,1024]{1,0:T(8,128)(2,1)} %get-tuple-element.122.q_ref, bf16[8,128,128]{2,1,0:T(8,128)(2,1)} %copy-done.33, ...), custom_call_target="tpu_custom_call" | custom-call | flops 25769803776 | bytes 2097152 | tf_op jit(solution)/shard_map/attend_back/pallas_call | solution.py:349
  258.7 5.1 %collective-permute-done.34 = bf16[256,1024]{1,0:T(8,128)(2,1)S(1)} collective-permute-done((bf16[256,1024]{1,0:T(8,128)(2,1)}, bf16[256,1024]{1,0:T(8,128)(2,1)S(1)}, u32[]{:S(2)}, u32[]{:S(2)}) %collective-permute-start.34) | collective-permute-done | bytes 524320 | tf_op jit(solution)/shard_map/ppermute | solution.py:736
  263.8 9.9 %collective-permute-done.36 = bf16[256,1024]{1,0:T(8,128)(2,1)S(1)} collective-permute-done((bf16[256,1024]{1,0:T(8,128)(2,1)}, bf16[256,1024]{1,0:T(8,128)(2,1)S(1)}, u32[]{:S(2)}, u32[]{:S(2)}) %collective-permute-start.36) | collective-permute-done | bytes 524320 | tf_op jit(solution)/shard_map/ppermute | solution.py:736
  273.7 3.3 collective-permute-start.37
  278.7 5.3 %collective-permute-done.37.refs_1_ = bf16[1024,128]{1,0:T(8,128)(2,1)S(1)} collective-permute-done((bf16[1024,128]{1,0:T(8,128)(2,1)}, bf16[1024,128]{1,0:T(8,128)(2,1)S(1)}, u32[]{:S(2)}, u32[]{:S(2)}) %collective-permute-start.37) | collective-permute-done | bytes 262176 | tf_op jit(solution)/shard_map/ppermute | solution.py:736
  284.0 5.6 %collective-permute-done.38.refs_2_ = bf16[1024,128]{1,0:T(8,128)(2,1)} collective-permute-done((bf16[1024,128]{1,0:T(8,128)(2,1)}, bf16[1024,128]{1,0:T(8,128)(2,1)}, u32[]{:S(2)}, u32[]{:S(2)}) %collective-permute-start.38) | collective-permute-done | bytes 262176 | tf_op jit(solution)/shard_map/ppermute | solution.py:736
  289.6 6.0 %tail.1 = (bf16[4,128,1024]{2,1,0:T(8,128)(2,1)}, bf16[4,128,1024]{2,1,0:T(8,128)(2,1)}, bf16[256,384]{1,0:T(8,128)(2,1)}, bf16[256,384]{1,0:T(8,128)(2,1)}, bf1...) custom-call(s32[2]{0:T(128)} %pad_add_fusion.at_ref, f32[128,1024]{1,0:T(8,128)} %get-tuple-element.170.gq_ref, ...), custom_call_target="tpu_custom_call" | custom-call | flops 1073741824 | bytes 12582912 | tf_op jit(solution)/shard_map/tail/pallas_call | solution.py:436
  295.7 1.5 add_convert_fusion.1
  299.9 1.7 add_convert_fusion
  301.7 1.9 collective-permute-start.44
  303.6 1.6 collective-permute-start.41
  305.3 1.5 collective-permute-start.42
  306.8 2.2 collective-permute-done.47
  309.0 1.7 collective-permute-start.43
  313.1 4.3 %collective-permute-start.51 = (bf16[128,1024]{1,0:T(8,128)(2,1)}, bf16[128,1024]{1,0:T(8,128)(2,1)}, u32[]{:S(2)}, u32[]{:S(2)}) collective-permute-start(bf16[128,1024]{1,0:T(8,128)(2,1)} %get-tuple-element.197), channel_id=1, source_target_pairs={{0,8},{8,16},{16,24},{24,0},{1,9},{9,17},{17,25},{25,1},{2,10},{10... | collective-permute-start | bytes 786440 | tf_op jit(solution)/shard_map/ppermute | solution.py:736
  318.2 4.2 %all-to-all-start.3 = ((bf16[8,32,384]{2,1,0:T(8,128)(2,1)}), bf16[8,32,384]{2,1,0:T(8,128)(2,1)S(1)}, u32[]{:S(2)}, u32[]{:S(2)}) async-start(bf16[8,32,384]{2,1,0:T(8,128)(2,1)} %bitcast.32), calls=%async_computation.3 | async-start | bytes 393216 | tf_op jit(solution)/shard_map/all_to_all | solution.py:759
  322.4 12.3 %collective-permute-done.44 = bf16[2,128,1024]{2,1,0:T(8,128)(2,1)S(1)} collective-permute-done((bf16[2,128,1024]{2,1,0:T(8,128)(2,1)S(1)}, bf16[2,128,1024]{2,1,0:T(8,128)(2,1)S(1)}, u32[]{:S(2)}, u32[]{:S(2)}) %collective-permute-start.44) | collective-permute-done | bytes 524320 | tf_op jit(solution)/shard_map/ppermute | solution.py:875
  335.7 2.0 add_convert_fusion.2
  337.7 11.0 %reduce-scatter.5.cloned.1.call-done = bf16[1,3,384,512]{3,2,1,0:T(8,128)(2,1)} async-done(((bf16[8,3,384,512]{3,2,1,0:T(8,128)(2,1)}), bf16[1,3,384,512]{3,2,1,0:T(8,128)(2,1)}) %reduce-scatter.5.cloned.1.call-update) | async-done | bytes 1179664 | tf_op jit(solution)/shard_map/reduce_scatter | solution.py:1022
  348.6 3.4 unpack.1
  353.0 2.6 finish.1
  (265 shorter events, 52.6 us)
Async XLA Ops:
  7.2 66.2 %all-gather.5.cloned.1.call-start = ((), (), s32[]{:S(2)}) async-start(), calls=%async_computation.8 | async-start | bytes 3538944 | tf_op jit(solution)/shard_map/all_gather | solution.py:951
  11.0 24.7 %copy-start.10 = (bf16[144,1024]{1,0:T(8,128)(2,1)}, bf16[144,1024]{1,0:T(8,128)(2,1)S(1)}, u32[]{:S(2)}) copy-start(bf16[144,1024]{1,0:T(8,128)(2,1)S(1)} %pad_maximum_fusion.3.refs_0_) | copy-start | bytes 884740
  11.0 12.2 %collective-permute-start = (bf16[144,1024]{1,0:T(8,128)(2,1)S(1)}, bf16[144,1024]{1,0:T(8,128)(2,1)S(1)}, u32[]{:S(2)}, u32[]{:S(2)}) collective-permute-start(bf16[144,1024]{1,0:T(8,128)(2,1)S(1)} %pad_maximum_fusion.3.refs_0_), channel_id=1, source_target_pairs={{0,2},{1,3},{2,4},{3,5},{4,6},{5,7},{8,10},{9,11},{10,12},{11,13},... | collective-permute-start | bytes 884744 | tf_op jit(solution)/shard_map/ppermute | solution.py:790
  16.0 18.5 %collective-permute-start.1 = (bf16[144,1024]{1,0:T(8,128)(2,1)S(1)}, bf16[144,1024]{1,0:T(8,128)(2,1)}, u32[]{:S(2)}, u32[]{:S(2)}) collective-permute-start(bf16[144,1024]{1,0:T(8,128)(2,1)S(1)} %pad_maximum_fusion.3.refs_0_), channel_id=1, source_target_pairs={{2,0},{3,1},{4,2},{5,3},{6,4},{7,5},{10,8},{11,9},{12,10},{13,11},... | collective-permute-start | bytes 884744 | tf_op jit(solution)/shard_map/ppermute | solution.py:790
  23.2 23.9 %collective-permute-start.4 = (bf16[144,1024]{1,0:T(8,128)(2,1)S(1)}, bf16[144,1024]{1,0:T(8,128)(2,1)}, u32[]{:S(2)}, u32[]{:S(2)}) collective-permute-start(bf16[144,1024]{1,0:T(8,128)(2,1)S(1)} %collective-permute-done), channel_id=1, source_target_pairs={{2,4},{3,5},{4,6},{5,7},{10,12},{11,13},{12,14},{13,15},{18,20},{1... | collective-permute-start | bytes 884744 | tf_op jit(solution)/shard_map/ppermute | solution.py:790
  34.4 26.4 %collective-permute-start.2 = (bf16[144,1024]{1,0:T(8,128)(2,1)}, bf16[144,1024]{1,0:T(8,128)(2,1)}, u32[]{:S(2)}, u32[]{:S(2)}) collective-permute-start(bf16[144,1024]{1,0:T(8,128)(2,1)} %collective-permute-done.1), channel_id=1, source_target_pairs={{2,0},{3,1},{4,2},{5,3},{10,8},{11,9},{12,10},{13,11},{18,16},{19,... | collective-permute-start | bytes 884744 | tf_op jit(solution)/shard_map/ppermute | solution.py:790
  37.7 35.7 %all-to-all-start = ((bf16[8,128,256]{2,1,0:T(8,128)(2,1)}), bf16[8,128,256]{2,1,0:T(8,128)(2,1)S(1)}, u32[]{:S(2)}, u32[]{:S(2)}) async-start(bf16[8,128,256]{2,1,0:T(8,128)(2,1)} %copy.126), calls=%async_computation | async-start | bytes 1048576 | tf_op jit(solution)/shard_map/all_to_all | solution.py:759
  42.5 136.3 %all-gather.7.cloned.1.call-start = ((), (), s32[]{:S(2)}) async-start(), calls=%async_computation.9 | async-start | bytes 10616832 | tf_op jit(solution)/shard_map/all_gather | solution.py:952
  42.6 30.8 %collective-permute-start.6 = (bf16[128,1024]{1,0:T(8,128)(2,1)}, bf16[128,1024]{1,0:T(8,128)(2,1)}, u32[]{:S(2)}, u32[]{:S(2)}) collective-permute-start(bf16[128,1024]{1,0:T(8,128)(2,1)} %refs_4_.1), channel_id=1, source_target_pairs={{0,8},{8,16},{16,24},{24,0},{1,9},{9,17},{17,25},{25,1},{2,10},{10... | collective-permute-start | bytes 786440 | tf_op jit(solution)/shard_map/ppermute | solution.py:736
  44.1 29.3 %collective-permute-start.7 = (bf16[128,1024]{1,0:T(8,128)(2,1)}, bf16[128,1024]{1,0:T(8,128)(2,1)}, u32[]{:S(2)}, u32[]{:S(2)}) collective-permute-start(bf16[128,1024]{1,0:T(8,128)(2,1)} %refs_4_.1), channel_id=1, source_target_pairs={{0,16},{8,24},{16,0},{24,8},{1,17},{9,25},{17,1},{25,9},{2,18},{10... | collective-permute-start | bytes 786440 | tf_op jit(solution)/shard_map/ppermute | solution.py:736
  45.7 27.7 %collective-permute-start.8 = (bf16[128,1024]{1,0:T(8,128)(2,1)}, bf16[128,1024]{1,0:T(8,128)(2,1)}, u32[]{:S(2)}, u32[]{:S(2)}) collective-permute-start(bf16[128,1024]{1,0:T(8,128)(2,1)} %refs_4_.1), channel_id=1, source_target_pairs={{0,24},{8,0},{16,8},{24,16},{1,25},{9,1},{17,9},{25,17},{2,26},{10... | collective-permute-start | bytes 786440 | tf_op jit(solution)/shard_map/ppermute | solution.py:736
  47.1 16.0 %collective-permute-start.5 = (bf16[144,1024]{1,0:T(8,128)(2,1)}, bf16[144,1024]{1,0:T(8,128)(2,1)}, u32[]{:S(2)}, u32[]{:S(2)}) collective-permute-start(bf16[144,1024]{1,0:T(8,128)(2,1)} %collective-permute-done.4), channel_id=1, source_target_pairs={{4,6},{5,7},{12,14},{13,15},{20,22},{21,23},{28,30},{29,31}} | collective-permute-start | bytes 884744 | tf_op jit(solution)/shard_map/ppermute | solution.py:790
  60.8 12.5 %collective-permute-start.3 = (bf16[144,1024]{1,0:T(8,128)(2,1)}, bf16[144,1024]{1,0:T(8,128)(2,1)S(1)}, u32[]{:S(2)}, u32[]{:S(2)}) collective-permute-start(bf16[144,1024]{1,0:T(8,128)(2,1)} %collective-permute-done.2), channel_id=1, source_target_pairs={{2,0},{3,1},{10,8},{11,9},{18,16},{19,17},{26,24},{27,25}} | collective-permute-start | bytes 884744 | tf_op jit(solution)/shard_map/ppermute | solution.py:790
  73.6 2.9 collective-permute-start.10
  73.7 2.8 collective-permute-start.11
  74.2 2.4 collective-permute-start.12
  74.2 2.3 collective-permute-start.9
  82.9 4.7 %collective-permute-start.16 = (bf16[16,1024]{1,0:T(8,128)(2,1)S(1)}, bf16[16,1024]{1,0:T(8,128)(2,1)S(1)}, u32[]{:S(2)}, u32[]{:S(2)}) collective-permute-start(bf16[16,1024]{1,0:T(8,128)(2,1)S(1)} %dynamic-slice_bitcast_fusion.5), channel_id=1, source_target_pairs={{0,1},{1,0},{2,3},{3,2},{4,5},{5,4},{6,7},{7,6},{8,9},{9,8},{10,11... | collective-permute-start | bytes 98312 | tf_op jit(solution)/shard_map/ppermute | solution.py:772
  83.1 10.3 %collective-permute-start.13 = (bf16[128,1024]{1,0:T(8,128)(2,1)}, bf16[128,1024]{1,0:T(8,128)(2,1)S(1)}, u32[]{:S(2)}, u32[]{:S(2)}) collective-permute-start(bf16[128,1024]{1,0:T(8,128)(2,1)} %get-tuple-element.123.refs_0_), channel_id=1, source_target_pairs={{0,8},{8,16},{16,24},{24,0},{1,9},{9,17},{17,25},{25,1},{2,10},{10... | collective-permute-start | bytes 786440 | tf_op jit(solution)/shard_map/ppermute | solution.py:736
  84.7 13.9 %collective-permute-start.14 = (bf16[128,1024]{1,0:T(8,128)(2,1)}, bf16[128,1024]{1,0:T(8,128)(2,1)S(1)}, u32[]{:S(2)}, u32[]{:S(2)}) collective-permute-start(bf16[128,1024]{1,0:T(8,128)(2,1)} %get-tuple-element.123.refs_0_), channel_id=1, source_target_pairs={{0,16},{8,24},{16,0},{24,8},{1,17},{9,25},{17,1},{25,9},{2,18},{10... | collective-permute-start | bytes 786440 | tf_op jit(solution)/shard_map/ppermute | solution.py:736
  86.2 12.5 %collective-permute-start.15 = (bf16[128,1024]{1,0:T(8,128)(2,1)}, bf16[128,1024]{1,0:T(8,128)(2,1)S(1)}, u32[]{:S(2)}, u32[]{:S(2)}) collective-permute-start(bf16[128,1024]{1,0:T(8,128)(2,1)} %get-tuple-element.123.refs_0_), channel_id=1, source_target_pairs={{0,24},{8,0},{16,8},{24,16},{1,25},{9,1},{17,9},{25,17},{2,26},{10... | collective-permute-start | bytes 786440 | tf_op jit(solution)/shard_map/ppermute | solution.py:736
  88.4 16.4 %collective-permute-start.17 = (bf16[2,16,1024]{2,1,0:T(8,128)(2,1)S(1)}, bf16[2,16,1024]{2,1,0:T(8,128)(2,1)S(1)}, u32[]{:S(2)}, u32[]{:S(2)}) collective-permute-start(bf16[2,16,1024]{2,1,0:T(8,128)(2,1)S(1)} %pad_maximum_fusion.5), channel_id=1, source_target_pairs={{0,2},{1,3},{2,4},{3,5},{4,6},{5,7},{6,0},{7,1},{8,10},{9,11},{10,... | collective-permute-start | bytes 196616 | tf_op jit(solution)/shard_map/ppermute | solution.py:764
  89.1 15.8 %collective-permute-start.18 = (bf16[2,16,1024]{2,1,0:T(8,128)(2,1)S(1)}, bf16[2,16,1024]{2,1,0:T(8,128)(2,1)S(1)}, u32[]{:S(2)}, u32[]{:S(2)}) collective-permute-start(bf16[2,16,1024]{2,1,0:T(8,128)(2,1)S(1)} %pad_maximum_fusion.5), channel_id=1, source_target_pairs={{0,4},{1,5},{2,6},{3,7},{4,0},{5,1},{6,2},{7,3},{8,12},{9,13},{10,... | collective-permute-start | bytes 196616 | tf_op jit(solution)/shard_map/ppermute | solution.py:764
  93.4 11.4 %collective-permute-start.19 = (bf16[2,16,1024]{2,1,0:T(8,128)(2,1)S(1)}, bf16[2,16,1024]{2,1,0:T(8,128)(2,1)S(1)}, u32[]{:S(2)}, u32[]{:S(2)}) collective-permute-start(bf16[2,16,1024]{2,1,0:T(8,128)(2,1)S(1)} %pad_maximum_fusion.5), channel_id=1, source_target_pairs={{0,6},{1,7},{2,0},{3,1},{4,2},{5,3},{6,4},{7,5},{8,14},{9,15},{10,... | collective-permute-start | bytes 196616 | tf_op jit(solution)/shard_map/ppermute | solution.py:764
  99.4 33.7 %copy-start.6 = (bf16[128,8,256]{0,2,1:T(8,128)(2,1)S(1)}, bf16[128,8,256]{0,2,1:T(8,128)(2,1)}, u32[]{:S(2)}) copy-start(bf16[128,8,256]{0,2,1:T(8,128)(2,1)} %get-tuple-element.232) | copy-start | bytes 1572868
  105.0 38.2 %copy-start.13 = (bf16[4,2,16,1024]{3,2,1,0:T(8,128)(2,1)}, bf16[4,2,16,1024]{3,2,1,0:T(8,128)(2,1)S(1)}, u32[]{:S(2)}) copy-start(bf16[4,2,16,1024]{3,2,1,0:T(8,128)(2,1)S(1)} %bitcast_dynamic-update-slice_fusion.refs_0_) | copy-start | bytes 786436
  105.0 21.8 %collective-permute-start.20 = (bf16[4,2,16,1024]{3,2,1,0:T(8,128)(2,1)S(1)}, bf16[4,2,16,1024]{3,2,1,0:T(8,128)(2,1)S(1)}, u32[]{:S(2)}, u32[]{:S(2)}) collective-permute-start(bf16[4,2,16,1024]{3,2,1,0:T(8,128)(2,1)S(1)} %bitcast_dynamic-update-slice_fusion.refs_0_), channel_id=1, source_target_pairs={{0,8},{8,16},{16,24},{24,0},{1,9},{9,17},{17,25},{25,1},{2,10},{10... | collective-permute-start | bytes 786440 | tf_op jit(solution)/shard_map/ppermute | solution.py:736
  111.2 19.9 %collective-permute-start.21 = (bf16[4,2,16,1024]{3,2,1,0:T(8,128)(2,1)S(1)}, bf16[4,2,16,1024]{3,2,1,0:T(8,128)(2,1)S(1)}, u32[]{:S(2)}, u32[]{:S(2)}) collective-permute-start(bf16[4,2,16,1024]{3,2,1,0:T(8,128)(2,1)S(1)} %bitcast_dynamic-update-slice_fusion.refs_0_), channel_id=1, source_target_pairs={{0,16},{8,24},{16,0},{24,8},{1,17},{9,25},{17,1},{25,9},{2,18},{10... | collective-permute-start | bytes 786440 | tf_op jit(solution)/shard_map/ppermute | solution.py:736
  120.1 11.1 %collective-permute-start.22 = (bf16[4,2,16,1024]{3,2,1,0:T(8,128)(2,1)S(1)}, bf16[4,2,16,1024]{3,2,1,0:T(8,128)(2,1)S(1)}, u32[]{:S(2)}, u32[]{:S(2)}) collective-permute-start(bf16[4,2,16,1024]{3,2,1,0:T(8,128)(2,1)S(1)} %bitcast_dynamic-update-slice_fusion.refs_0_), channel_id=1, source_target_pairs={{0,24},{8,0},{16,8},{24,16},{1,25},{9,1},{17,9},{25,17},{2,26},{10... | collective-permute-start | bytes 786440 | tf_op jit(solution)/shard_map/ppermute | solution.py:736
  120.7 22.5 %all-to-all-start.1 = ((bf16[8,128,128]{2,1,0:T(8,128)(2,1)}), bf16[8,128,128]{2,1,0:T(8,128)(2,1)S(1)}, u32[]{:S(2)}, u32[]{:S(2)}) async-start(bf16[8,128,128]{2,1,0:T(8,128)(2,1)} %get-tuple-element.126), calls=%async_computation.1 | async-start | bytes 524288 | tf_op jit(solution)/shard_map/all_to_all | solution.py:759
  124.1 101.8 %reduce-scatter.3.cloned.1.call-start = ((), (), s32[]{:S(2)}) async-start(), calls=%async_computation.6 | async-start | bytes 3538944 | tf_op jit(solution)/shard_map/reduce_scatter | solution.py:1021
  124.2 11.7 %collective-permute-start.23 = (bf16[4,2,16,1024]{3,2,1,0:T(8,128)(2,1)S(1)}, bf16[4,2,16,1024]{3,2,1,0:T(8,128)(2,1)S(1)}, u32[]{:S(2)}, u32[]{:S(2)}) collective-permute-start(bf16[4,2,16,1024]{3,2,1,0:T(8,128)(2,1)S(1)} %bitcast_dynamic-update-slice_fusion.refs_0_), channel_id=1, source_target_pairs={{0,1},{1,0},{2,3},{3,2},{4,5},{5,4},{6,7},{7,6},{8,9},{9,8},{10,11... | collective-permute-start | bytes 786440 | tf_op jit(solution)/shard_map/ppermute | solution.py:772
  126.8 16.4 %collective-permute-start.24 = (bf16[4,2,16,1024]{3,2,1,0:T(8,128)(2,1)S(1)}, bf16[4,2,16,1024]{3,2,1,0:T(8,128)(2,1)S(1)}, u32[]{:S(2)}, u32[]{:S(2)}) collective-permute-start(bf16[4,2,16,1024]{3,2,1,0:T(8,128)(2,1)S(1)} %collective-permute-done.20.refs_1_), channel_id=1, source_target_pairs={{0,1},{1,0},{2,3},{3,2},{4,5},{5,4},{6,7},{7,6},{8,9},{9,8},{10,11... | collective-permute-start | bytes 786440 | tf_op jit(solution)/shard_map/ppermute | solution.py:772
  131.1 12.1 %collective-permute-start.25 = (bf16[4,2,16,1024]{3,2,1,0:T(8,128)(2,1)S(1)}, bf16[4,2,16,1024]{3,2,1,0:T(8,128)(2,1)}, u32[]{:S(2)}, u32[]{:S(2)}) collective-permute-start(bf16[4,2,16,1024]{3,2,1,0:T(8,128)(2,1)S(1)} %collective-permute-done.21.refs_2_), channel_id=1, source_target_pairs={{0,1},{1,0},{2,3},{3,2},{4,5},{5,4},{6,7},{7,6},{8,9},{9,8},{10,11... | collective-permute-start | bytes 786440 | tf_op jit(solution)/shard_map/ppermute | solution.py:772
  131.2 12.0 %collective-permute-start.26 = (bf16[4,2,16,1024]{3,2,1,0:T(8,128)(2,1)S(1)}, bf16[4,2,16,1024]{3,2,1,0:T(8,128)(2,1)}, u32[]{:S(2)}, u32[]{:S(2)}) collective-permute-start(bf16[4,2,16,1024]{3,2,1,0:T(8,128)(2,1)S(1)} %collective-permute-done.22.refs_3_), channel_id=1, source_target_pairs={{0,1},{1,0},{2,3},{3,2},{4,5},{5,4},{6,7},{7,6},{8,9},{9,8},{10,11... | collective-permute-start | bytes 786440 | tf_op jit(solution)/shard_map/ppermute | solution.py:772
  150.2 10.9 %collective-permute-start.27 = (bf16[128,1152]{1,0:T(8,128)(2,1)S(1)}, bf16[128,1152]{1,0:T(8,128)(2,1)S(1)}, u32[]{:S(2)}, u32[]{:S(2)}) collective-permute-start(bf16[128,1152]{1,0:T(8,128)(2,1)S(1)} %concatenate.24.refs_0_), channel_id=1, source_target_pairs={{0,8},{8,16},{16,24},{24,0},{1,9},{9,17},{17,25},{25,1},{2,10},{10... | collective-permute-start | bytes 884744 | tf_op jit(solution)/shard_map/ppermute | solution.py:736
  152.0 15.1 %collective-permute-start.28 = (bf16[128,1152]{1,0:T(8,128)(2,1)S(1)}, bf16[128,1152]{1,0:T(8,128)(2,1)S(1)}, u32[]{:S(2)}, u32[]{:S(2)}) collective-permute-start(bf16[128,1152]{1,0:T(8,128)(2,1)S(1)} %concatenate.24.refs_0_), channel_id=1, source_target_pairs={{0,16},{8,24},{16,0},{24,8},{1,17},{9,25},{17,1},{25,9},{2,18},{10... | collective-permute-start | bytes 884744 | tf_op jit(solution)/shard_map/ppermute | solution.py:736
  152.0 16.1 %collective-permute-start.29 = (bf16[128,1152]{1,0:T(8,128)(2,1)S(1)}, bf16[128,1152]{1,0:T(8,128)(2,1)S(1)}, u32[]{:S(2)}, u32[]{:S(2)}) collective-permute-start(bf16[128,1152]{1,0:T(8,128)(2,1)S(1)} %concatenate.24.refs_0_), channel_id=1, source_target_pairs={{0,24},{8,0},{16,8},{24,16},{1,25},{9,1},{17,9},{25,17},{2,26},{10... | collective-permute-start | bytes 884744 | tf_op jit(solution)/shard_map/ppermute | solution.py:736
  154.8 1.1 collective-permute-start.30
  178.8 169.9 %reduce-scatter.5.cloned.1.call-start = ((), (), s32[]{:S(2)}) async-start(), calls=%async_computation.7 | async-start | bytes 10616832 | tf_op jit(solution)/shard_map/reduce_scatter | solution.py:1022
  203.8 10.3 %collective-permute-start.31 = (bf16[128,1152]{1,0:T(8,128)(2,1)}, bf16[128,1152]{1,0:T(8,128)(2,1)S(1)}, u32[]{:S(2)}, u32[]{:S(2)}) collective-permute-start(bf16[128,1152]{1,0:T(8,128)(2,1)} %get-tuple-element.155), channel_id=1, source_target_pairs={{0,24},{8,0},{16,8},{24,16},{1,25},{9,1},{17,9},{25,17},{2,26},{10... | collective-permute-start | bytes 884744 | tf_op jit(solution)/shard_map/ppermute | solution.py:736
  207.4 15.6 %collective-permute-start.32 = (bf16[128,1152]{1,0:T(8,128)(2,1)}, bf16[128,1152]{1,0:T(8,128)(2,1)S(1)}, u32[]{:S(2)}, u32[]{:S(2)}) collective-permute-start(bf16[128,1152]{1,0:T(8,128)(2,1)} %get-tuple-element.156), channel_id=1, source_target_pairs={{0,16},{8,24},{16,0},{24,8},{1,17},{9,25},{17,1},{25,9},{2,18},{10... | collective-permute-start | bytes 884744 | tf_op jit(solution)/shard_map/ppermute | solution.py:736
  209.2 15.5 %collective-permute-start.33 = (bf16[128,1152]{1,0:T(8,128)(2,1)}, bf16[128,1152]{1,0:T(8,128)(2,1)S(1)}, u32[]{:S(2)}, u32[]{:S(2)}) collective-permute-start(bf16[128,1152]{1,0:T(8,128)(2,1)} %get-tuple-element.157), channel_id=1, source_target_pairs={{0,8},{8,16},{16,24},{24,0},{1,9},{9,17},{17,25},{25,1},{2,10},{10... | collective-permute-start | bytes 884744 | tf_op jit(solution)/shard_map/ppermute | solution.py:736
  230.5 17.5 %all-to-all-start.2 = ((bf16[8,128,128]{2,1,0:T(8,128)(2,1)}), bf16[8,128,128]{2,1,0:T(8,128)(2,1)S(1)}, u32[]{:S(2)}, u32[]{:S(2)}) async-start(bf16[8,128,128]{2,1,0:T(8,128)(2,1)} %bitcast.29), calls=%async_computation.2 | async-start | bytes 524288 | tf_op jit(solution)/shard_map/all_to_all | solution.py:759
  248.7 15.1 %collective-permute-start.34 = (bf16[256,1024]{1,0:T(8,128)(2,1)}, bf16[256,1024]{1,0:T(8,128)(2,1)S(1)}, u32[]{:S(2)}, u32[]{:S(2)}) collective-permute-start(bf16[256,1024]{1,0:T(8,128)(2,1)} %convolution_convert_fusion.2), channel_id=1, source_target_pairs={{0,24},{8,0},{16,8},{24,16},{1,25},{9,1},{17,9},{25,17},{2,26},{10... | collective-permute-start | bytes 1572872 | tf_op jit(solution)/shard_map/ppermute | solution.py:736
  248.7 15.1 %collective-permute-start.35 = (bf16[256,1024]{1,0:T(8,128)(2,1)}, bf16[256,1024]{1,0:T(8,128)(2,1)S(1)}, u32[]{:S(2)}, u32[]{:S(2)}) collective-permute-start(bf16[256,1024]{1,0:T(8,128)(2,1)} %convolution_convert_fusion.1), channel_id=1, source_target_pairs={{0,16},{8,24},{16,0},{24,8},{1,17},{9,25},{17,1},{25,9},{2,18},{10... | collective-permute-start | bytes 1572872 | tf_op jit(solution)/shard_map/ppermute | solution.py:736
  250.4 23.3 %collective-permute-start.36 = (bf16[256,1024]{1,0:T(8,128)(2,1)}, bf16[256,1024]{1,0:T(8,128)(2,1)S(1)}, u32[]{:S(2)}, u32[]{:S(2)}) collective-permute-start(bf16[256,1024]{1,0:T(8,128)(2,1)} %convolution_convert_fusion), channel_id=1, source_target_pairs={{0,8},{8,16},{16,24},{24,0},{1,9},{9,17},{17,25},{25,1},{2,10},{10... | collective-permute-start | bytes 1572872 | tf_op jit(solution)/shard_map/ppermute | solution.py:736
  273.7 10.3 %collective-permute-start.37 = (bf16[1024,128]{1,0:T(8,128)(2,1)}, bf16[1024,128]{1,0:T(8,128)(2,1)S(1)}, u32[]{:S(2)}, u32[]{:S(2)}) collective-permute-start(bf16[1024,128]{1,0:T(8,128)(2,1)} %get-tuple-element.173), channel_id=1, source_target_pairs={{0,24},{8,0},{16,8},{24,16},{1,25},{9,1},{17,9},{25,17},{2,26},{10... | collective-permute-start | bytes 786440 | tf_op jit(solution)/shard_map/ppermute | solution.py:736
  276.9 12.6 %collective-permute-start.38 = (bf16[1024,128]{1,0:T(8,128)(2,1)}, bf16[1024,128]{1,0:T(8,128)(2,1)}, u32[]{:S(2)}, u32[]{:S(2)}) collective-permute-start(bf16[1024,128]{1,0:T(8,128)(2,1)} %get-tuple-element.174), channel_id=1, source_target_pairs={{0,16},{8,24},{16,0},{24,8},{1,17},{9,25},{17,1},{25,9},{2,18},{10... | collective-permute-start | bytes 786440 | tf_op jit(solution)/shard_map/ppermute | solution.py:736
  276.9 12.6 %collective-permute-start.39 = (bf16[1024,128]{1,0:T(8,128)(2,1)}, bf16[1024,128]{1,0:T(8,128)(2,1)}, u32[]{:S(2)}, u32[]{:S(2)}) collective-permute-start(bf16[1024,128]{1,0:T(8,128)(2,1)} %get-tuple-element.175), channel_id=1, source_target_pairs={{0,8},{8,16},{16,24},{24,0},{1,9},{9,17},{17,25},{25,1},{2,10},{10... | collective-permute-start | bytes 786440 | tf_op jit(solution)/shard_map/ppermute | solution.py:736
  295.6 4.3 %collective-permute-start.40 = (bf16[4,128,1024]{2,1,0:T(8,128)(2,1)}, bf16[4,128,1024]{2,1,0:T(8,128)(2,1)}, u32[]{:S(2)}, u32[]{:S(2)}) collective-permute-start(bf16[4,128,1024]{2,1,0:T(8,128)(2,1)} %get-tuple-element.181), channel_id=1, source_target_pairs={{0,1},{1,0},{2,3},{3,2},{4,5},{5,4},{6,7},{7,6},{8,9},{9,8},{10,11... | collective-permute-start | bytes 3145736 | tf_op jit(solution)/shard_map/ppermute | solution.py:772
  297.2 2.4 collective-permute-start.46
  299.2 36.4 %collective-permute-start.49 = (bf16[128,1024]{1,0:T(8,128)(2,1)}, bf16[128,1024]{1,0:T(8,128)(2,1)}, u32[]{:S(2)}, u32[]{:S(2)}) collective-permute-start(bf16[128,1024]{1,0:T(8,128)(2,1)} %get-tuple-element.195), channel_id=1, source_target_pairs={{0,24},{8,0},{16,8},{24,16},{1,25},{9,1},{17,9},{25,17},{2,26},{10... | collective-permute-start | bytes 786440 | tf_op jit(solution)/shard_map/ppermute | solution.py:736
  299.7 9.3 %collective-permute-start.47 = (bf16[2,32,1024]{2,1,0:T(8,128)(2,1)S(1)}, bf16[2,32,1024]{2,1,0:T(8,128)(2,1)S(1)}, u32[]{:S(2)}, u32[]{:S(2)}) collective-permute-start(bf16[2,32,1024]{2,1,0:T(8,128)(2,1)S(1)} %dynamic-slice_bitcast_fusion.3), channel_id=1, source_target_pairs={{0,2},{1,3},{2,0},{3,1},{4,6},{5,7},{6,4},{7,5},{8,10},{9,11},{10,... | collective-permute-start | bytes 393224 | tf_op jit(solution)/shard_map/ppermute | solution.py:875
  301.7 33.0 %collective-permute-start.44 = (bf16[2,128,1024]{2,1,0:T(8,128)(2,1)S(1)}, bf16[2,128,1024]{2,1,0:T(8,128)(2,1)S(1)}, u32[]{:S(2)}, u32[]{:S(2)}) collective-permute-start(bf16[2,128,1024]{2,1,0:T(8,128)(2,1)S(1)} %dynamic-slice_bitcast_fusion), channel_id=1, source_target_pairs={{0,2},{1,3},{2,0},{3,1},{4,6},{5,7},{6,4},{7,5},{8,10},{9,11},{10,... | collective-permute-start | bytes 1572872 | tf_op jit(solution)/shard_map/ppermute | solution.py:875
  303.6 9.1 %collective-permute-start.41 = (bf16[256,384]{1,0:T(8,128)(2,1)S(1)}, bf16[256,384]{1,0:T(8,128)(2,1)S(1)}, u32[]{:S(2)}, u32[]{:S(2)}) collective-permute-start(bf16[256,384]{1,0:T(8,128)(2,1)S(1)} %copy-done.52), channel_id=1, source_target_pairs={{0,24},{8,0},{16,8},{24,16},{1,25},{9,1},{17,9},{25,17},{2,26},{10... | collective-permute-start | bytes 589832 | tf_op jit(solution)/shard_map/ppermute | solution.py:736
  305.3 7.9 %collective-permute-start.42 = (bf16[256,384]{1,0:T(8,128)(2,1)S(1)}, bf16[256,384]{1,0:T(8,128)(2,1)S(1)}, u32[]{:S(2)}, u32[]{:S(2)}) collective-permute-start(bf16[256,384]{1,0:T(8,128)(2,1)S(1)} %copy-done.51), channel_id=1, source_target_pairs={{0,16},{8,24},{16,0},{24,8},{1,17},{9,25},{17,1},{25,9},{2,18},{10... | collective-permute-start | bytes 589832 | tf_op jit(solution)/shard_map/ppermute | solution.py:736
  309.0 8.4 %collective-permute-start.43 = (bf16[256,384]{1,0:T(8,128)(2,1)S(1)}, bf16[256,384]{1,0:T(8,128)(2,1)S(1)}, u32[]{:S(2)}, u32[]{:S(2)}) collective-permute-start(bf16[256,384]{1,0:T(8,128)(2,1)S(1)} %copy-done.50), channel_id=1, source_target_pairs={{0,8},{8,16},{16,24},{24,0},{1,9},{9,17},{17,25},{25,1},{2,10},{10... | collective-permute-start | bytes 589832 | tf_op jit(solution)/shard_map/ppermute | solution.py:736
  310.7 25.0 %copy-start.24 = (bf16[128,1024]{1,0:T(8,128)(2,1)S(1)}, bf16[128,1024]{1,0:T(8,128)(2,1)}, u32[]{:S(2)}) copy-start(bf16[128,1024]{1,0:T(8,128)(2,1)} %get-tuple-element.194) | copy-start | bytes 786436
  312.7 22.9 %collective-permute-start.50 = (bf16[128,1024]{1,0:T(8,128)(2,1)}, bf16[128,1024]{1,0:T(8,128)(2,1)S(1)}, u32[]{:S(2)}, u32[]{:S(2)}) collective-permute-start(bf16[128,1024]{1,0:T(8,128)(2,1)} %get-tuple-element.196), channel_id=1, source_target_pairs={{0,16},{8,24},{16,0},{24,8},{1,17},{9,25},{17,1},{25,9},{2,18},{10... | collective-permute-start | bytes 786440 | tf_op jit(solution)/shard_map/ppermute | solution.py:736
  313.1 22.6 %collective-permute-start.51 = (bf16[128,1024]{1,0:T(8,128)(2,1)}, bf16[128,1024]{1,0:T(8,128)(2,1)}, u32[]{:S(2)}, u32[]{:S(2)}) collective-permute-start(bf16[128,1024]{1,0:T(8,128)(2,1)} %get-tuple-element.197), channel_id=1, source_target_pairs={{0,8},{8,16},{16,24},{24,0},{1,9},{9,17},{17,25},{25,1},{2,10},{10... | collective-permute-start | bytes 786440 | tf_op jit(solution)/shard_map/ppermute | solution.py:736
  317.4 34.6 %collective-permute-start.48 = (bf16[1,32,1024]{2,1,0:T(8,128)(2,1)S(1)}, bf16[1,32,1024]{2,1,0:T(8,128)(2,1)S(1)}, u32[]{:S(2)}, u32[]{:S(2)}) collective-permute-start(bf16[1,32,1024]{2,1,0:T(8,128)(2,1)S(1)} %get-tuple-element.239), channel_id=1, source_target_pairs={{0,4},{1,5},{2,6},{3,7},{4,0},{5,1},{6,2},{7,3},{8,12},{9,13},{10,... | collective-permute-start | bytes 196616 | tf_op jit(solution)/shard_map/ppermute | solution.py:875
  318.2 33.8 %all-to-all-start.3 = ((bf16[8,32,384]{2,1,0:T(8,128)(2,1)}), bf16[8,32,384]{2,1,0:T(8,128)(2,1)S(1)}, u32[]{:S(2)}, u32[]{:S(2)}) async-start(bf16[8,32,384]{2,1,0:T(8,128)(2,1)} %bitcast.32), calls=%async_computation.3 | async-start | bytes 393216 | tf_op jit(solution)/shard_map/all_to_all | solution.py:759
  335.7 16.6 %collective-permute-start.45 = (bf16[1,128,1024]{2,1,0:T(8,128)(2,1)S(1)}, bf16[1,128,1024]{2,1,0:T(8,128)(2,1)S(1)}, u32[]{:S(2)}, u32[]{:S(2)}) collective-permute-start(bf16[1,128,1024]{2,1,0:T(8,128)(2,1)S(1)} %get-tuple-element.230), channel_id=1, source_target_pairs={{0,4},{1,5},{2,6},{3,7},{4,0},{5,1},{6,2},{7,3},{8,12},{9,13},{10,... | collective-permute-start | bytes 786440 | tf_op jit(solution)/shard_map/ppermute | solution.py:875
  (49 other events, 354.3 us)
Sparse Core Ops, SparseCore 0:
  10.8 57.2 all-gather.4
  73.6 104.1 all-gather.6
  180.2 40.7 reduce-scatter.2
  226.0 122.5 reduce-scatter.4

commit v2 on v1

--- a/solution.py
+++ b/solution.py
@@ -565,7 +565,7 @@
     last = pl.num_programs(0) - 1
     width = u_all.shape[1]
     count = ctx_count * tile
-    chunk = min(2 * tile, count)
+    chunk = min(4 * tile, count)
     column = c_ref[0] * experts + first + e
 
     @pl.when(e == 0)

time: 369 us -> 369 us (level)
  transfers between devices with their start and end apart: 60 -> 60, of which waited for: 26 -> 25; matrix products, arithmetic and copies ran while one was open for 11% -> 11% of each run, Pallas kernels for 18% -> 18%
where the time goes in v2:
time: 369 us; the launch traced here: 362 us
  waiting for transfers between devices  143 us (39%)
  starting transfers between devices  90.9 us (25%)
  Pallas kernels  66.1 us (18%)
  other arithmetic  21.3 us (6%)
  local copies, waits for them, and re-layouts  16.5 us (4%)
  between operations  15.4 us (4%)
  matrix products  8.82 us (2%)
    ppermute x27, waiting for transfers between devices, send_ctx(): lax.ppermute(value, 'ctx', [(i, (i + by) % count) for i in range(count)])  65.1 us
    ppermute x27, starting transfers between devices, send_ctx(): lax.ppermute(value, 'ctx', [(i, (i + by) % count) for i in range(count)])  52.6 us
    ppermute x6, waiting for transfers between devices, step(): return lax.ppermute(block, 'shard', pairs)  34.5 us
    pallas_call x2, Pallas kernels, run_experts(): pl.pallas_call(functools.partial(expert_kernel, ctx_count=ctx_count, expe...  33.8 us
    all_to_all x4, waiting for transfers between devices, all_to_all(): lax.all_to_all(value, 'shard', split_axis=0, concat_axis=0, tiled=True)  17 us
    all_to_all x4, starting transfers between devices, all_to_all(): lax.all_to_all(value, 'shard', split_axis=0, concat_axis=0, tiled=True)  16 us
    ppermute x4, waiting for transfers between devices, halve_chips(): lax.ppermute(sent, 'shard', [(i, i ^ 2 * distance) for i in range(shards)])  14.7 us
    reduce_scatter x1, waiting for transfers between devices, local(): lax.psum_scatter(tie(grads_last, share_first, back), 'shard', scatter_dim...  11.9 us
  transfers between devices with their start and end apart: 60, of which 25 were waited for; matrix products, arithmetic and copies ran while one was open for 11% of the time, Pallas kernels for 18%

profile of v2, /device:TPU:0, one launch (start us, length us, event | category | flops | bytes accessed | tf_op | source)
XLA Modules:
  0.0 362.3 jit_solution(18337308270979863410)
XLA Ops:
  11.0 4.9 %collective-permute-start = (bf16[144,1024]{1,0:T(8,128)(2,1)S(1)}, bf16[144,1024]{1,0:T(8,128)(2,1)S(1)}, u32[]{:S(2)}, u32[]{:S(2)}) collective-permute-start(bf16[144,1024]{1,0:T(8,128)(2,1)S(1)} %pad_maximum_fusion.3.refs_0_), channel_id=1, source_target_pairs={{0,2},{1,3},{2,4},{3,5},{4,6},{5,7},{8,10},{9,11},{10,12},{11,13},... | collective-permute-start | bytes 884744 | tf_op jit(solution)/shard_map/ppermute | solution.py:790
  17.3 6.0 %collective-permute-done = bf16[144,1024]{1,0:T(8,128)(2,1)S(1)} collective-permute-done((bf16[144,1024]{1,0:T(8,128)(2,1)S(1)}, bf16[144,1024]{1,0:T(8,128)(2,1)S(1)}, u32[]{:S(2)}, u32[]{:S(2)}) %collective-permute-start) | collective-permute-done | bytes 294944 | tf_op jit(solution)/shard_map/ppermute | solution.py:790
  25.0 9.4 %collective-permute-done.1 = bf16[144,1024]{1,0:T(8,128)(2,1)} collective-permute-done((bf16[144,1024]{1,0:T(8,128)(2,1)S(1)}, bf16[144,1024]{1,0:T(8,128)(2,1)}, u32[]{:S(2)}, u32[]{:S(2)}) %collective-permute-start.1) | collective-permute-done | bytes 294944 | tf_op jit(solution)/shard_map/ppermute | solution.py:790
  37.7 4.8 %all-to-all-start = ((bf16[8,128,256]{2,1,0:T(8,128)(2,1)}), bf16[8,128,256]{2,1,0:T(8,128)(2,1)S(1)}, u32[]{:S(2)}, u32[]{:S(2)}) async-start(bf16[8,128,256]{2,1,0:T(8,128)(2,1)} %copy.126), calls=%async_computation | async-start | bytes 1048576 | tf_op jit(solution)/shard_map/all_to_all | solution.py:759
  42.6 1.5 collective-permute-start.6
  44.1 1.5 collective-permute-start.7
  45.7 1.4 collective-permute-start.8
  50.7 10.0 %collective-permute-done.2 = bf16[144,1024]{1,0:T(8,128)(2,1)} collective-permute-done((bf16[144,1024]{1,0:T(8,128)(2,1)}, bf16[144,1024]{1,0:T(8,128)(2,1)}, u32[]{:S(2)}, u32[]{:S(2)}) %collective-permute-start.2) | collective-permute-done | bytes 294944 | tf_op jit(solution)/shard_map/ppermute | solution.py:790
  64.2 9.1 %collective-permute-done.3 = bf16[144,1024]{1,0:T(8,128)(2,1)S(1)} collective-permute-done((bf16[144,1024]{1,0:T(8,128)(2,1)}, bf16[144,1024]{1,0:T(8,128)(2,1)S(1)}, u32[]{:S(2)}, u32[]{:S(2)}) %collective-permute-start.3) | collective-permute-done | bytes 294944 | tf_op jit(solution)/shard_map/ppermute | solution.py:790
  77.5 4.7 %project.1 = (bf16[1024,1024]{1,0:T(8,128)(2,1)}, bf16[128,1024]{1,0:T(8,128)(2,1)}, bf16[128,1024]{1,0:T(8,128)(2,1)}, bf16[8,16,1024]{2,1,0:T(8,128)(2,1)}) custom-call(s32[2]{0:T(128)} %pad_add_fusion.1.at_ref, bf16[1024,256]{1,0:T(8,128)(2,1)} %bitcast.123, f32[32,1024]{1,0:T(8,128)} %get-tuple-element.242.cos_ref, ...), custom_call_target="tpu_custom_call" | custom-call | flops 536870912 | bytes 4194304 | tf_op jit(solution)/shard_map/project/pallas_call | solution.py:124
  83.1 1.6 collective-permute-start.13
  84.7 1.5 collective-permute-start.14
  86.2 1.4 collective-permute-start.15
  89.1 1.9 collective-permute-start.18
  90.9 2.5 collective-permute-done.13.refs_1_
  93.4 2.1 collective-permute-start.19
  95.6 3.0 collective-permute-done.14.refs_2_
  99.4 5.5 %attend.1 = (bf16[8,128,128]{2,1,0:T(8,128)(2,1)}, f32[128,1024]{1,0:T(8,128)}, f32[2,1024]{1,0:T(2,128)}) custom-call(s32[1]{0:T(128)} %bitcast.c_ref, bf16[128,1024]{1,0:T(8,128)(2,1)} %get-tuple-element.122.q_ref, bf16[128,1024]{1,0:T(8,128)(2,1)} %get-tuple-element.123.refs_0_, bf16[128,1024]{1,0:T(8,128)(2,1)} %copy-done.47, ...), custom_call_target="tpu_custom_call" | custom-call | flops 17179869184 | bytes 1048576 | tf_op jit(solution)/shard_map/attend/pallas_call | solution.py:218
  105.0 6.2 %collective-permute-start.20 = (bf16[4,2,16,1024]{3,2,1,0:T(8,128)(2,1)S(1)}, bf16[4,2,16,1024]{3,2,1,0:T(8,128)(2,1)S(1)}, u32[]{:S(2)}, u32[]{:S(2)}) collective-permute-start(bf16[4,2,16,1024]{3,2,1,0:T(8,128)(2,1)S(1)} %bitcast_dynamic-update-slice_fusion.refs_0_), channel_id=1, source_target_pairs={{0,8},{8,16},{16,24},{24,0},{1,9},{9,17},{17,25},{25,1},{2,10},{10... | collective-permute-start | bytes 786440 | tf_op jit(solution)/shard_map/ppermute | solution.py:736
  111.2 8.9 %collective-permute-start.21 = (bf16[4,2,16,1024]{3,2,1,0:T(8,128)(2,1)S(1)}, bf16[4,2,16,1024]{3,2,1,0:T(8,128)(2,1)S(1)}, u32[]{:S(2)}, u32[]{:S(2)}) collective-permute-start(bf16[4,2,16,1024]{3,2,1,0:T(8,128)(2,1)S(1)} %bitcast_dynamic-update-slice_fusion.refs_0_), channel_id=1, source_target_pairs={{0,16},{8,24},{16,0},{24,8},{1,17},{9,25},{17,1},{25,9},{2,18},{10... | collective-permute-start | bytes 786440 | tf_op jit(solution)/shard_map/ppermute | solution.py:736
  120.7 3.4 all-to-all-start.1
  124.6 2.3 collective-permute-done.20.refs_1_
  126.8 4.3 %collective-permute-done.21.refs_2_ = bf16[4,2,16,1024]{3,2,1,0:T(8,128)(2,1)S(1)} collective-permute-done((bf16[4,2,16,1024]{3,2,1,0:T(8,128)(2,1)S(1)}, bf16[4,2,16,1024]{3,2,1,0:T(8,128)(2,1)S(1)}, u32[]{:S(2)}, u32[]{:S(2)}) %collective-permute-start.21) | collective-permute-done | bytes 262176 | tf_op jit(solution)/shard_map/ppermute | solution.py:736
  135.8 7.4 %all-to-all-done.1 = bf16[8,128,128]{2,1,0:T(8,128)(2,1)S(1)} async-done(((bf16[8,128,128]{2,1,0:T(8,128)(2,1)}), bf16[8,128,128]{2,1,0:T(8,128)(2,1)S(1)}, u32[]{:S(2)}, u32[]{:S(2)}) %all-to-all-start.1) | async-done | bytes 262176 | tf_op jit(solution)/shard_map/all_to_all | solution.py:759
  143.9 3.0 assemble.1
  146.9 2.2 multiply_reduce_fusion.2
  150.3 1.7 collective-permute-start.27
  152.0 2.7 collective-permute-start.29
  155.9 5.3 %collective-permute-done.27.refs_1_ = bf16[128,1152]{1,0:T(8,128)(2,1)S(1)} collective-permute-done((bf16[128,1152]{1,0:T(8,128)(2,1)S(1)}, bf16[128,1152]{1,0:T(8,128)(2,1)S(1)}, u32[]{:S(2)}, u32[]{:S(2)}) %collective-permute-start.27) | collective-permute-done | bytes 294944 | tf_op jit(solution)/shard_map/ppermute | solution.py:736
  161.2 5.9 %collective-permute-done.28.refs_2_ = bf16[128,1152]{1,0:T(8,128)(2,1)S(1)} collective-permute-done((bf16[128,1152]{1,0:T(8,128)(2,1)S(1)}, bf16[128,1152]{1,0:T(8,128)(2,1)S(1)}, u32[]{:S(2)}, u32[]{:S(2)}) %collective-permute-start.28) | collective-permute-done | bytes 294944 | tf_op jit(solution)/shard_map/ppermute | solution.py:736
  168.8 9.8 %experts.2 = (f32[512,1024]{1,0:T(8,128)}, f32[512,1024]{1,0:T(8,128)}, f32[512,128]{1,0:T(8,128)}, bf16[8,1,384,512]{3,2,1,0:T(8,128)(2,1)}) custom-call(s32[1]{0:T(128)} %bitcast.c_ref, bf16[128,1152]{1,0:T(8,128)(2,1)} %copy-done.19, bf16[128,1152]{1,0:T(8,128)(2,1)} %copy-done.44, bf16[128,1152]{1,0:T(8,128)(2,1)} %copy-done.45, ...), custom_call_target="tpu_custom_call" | custom-call | flops 6442450944 | bytes 6291456 | tf_op jit(solution)/shard_map/experts/pallas_call | solution.py:686
  178.7 24.0 %experts.3 = (bf16[128,1152]{1,0:T(8,128)(2,1)}, bf16[128,1152]{1,0:T(8,128)(2,1)}, bf16[128,1152]{1,0:T(8,128)(2,1)}, bf16[128,1152]{1,0:T(8,128)(2,1)}, bf16[1...) custom-call(s32[1]{0:T(128)} %bitcast.c_ref, ...), custom_call_target="tpu_custom_call" | custom-call | flops 19327352832 | bytes 18874368 | tf_op jit(solution)/shard_map/experts/pallas_call | solution.py:686
  202.7 3.5 collective-permute-start.31
  206.2 1.8 collective-permute-start.32
  208.0 2.0 collective-permute-start.33
  210.0 3.2 collective-permute-done.31
  213.2 8.6 %collective-permute-done.32 = bf16[128,1152]{1,0:T(8,128)(2,1)S(1)} collective-permute-done((bf16[128,1152]{1,0:T(8,128)(2,1)}, bf16[128,1152]{1,0:T(8,128)(2,1)S(1)}, u32[]{:S(2)}, u32[]{:S(2)}) %collective-permute-start.32) | collective-permute-done | bytes 294944 | tf_op jit(solution)/shard_map/ppermute | solution.py:736
  221.8 1.7 collective-permute-done.33
  225.9 2.0 multiply_convert_fusion
  227.9 1.4 convolution_convert_fusion.4
  229.3 3.6 all-to-all-start.2
  237.4 9.6 %all-to-all-done.2.grad_ref = bf16[8,128,128]{2,1,0:T(8,128)(2,1)S(1)} async-done(((bf16[8,128,128]{2,1,0:T(8,128)(2,1)}), bf16[8,128,128]{2,1,0:T(8,128)(2,1)S(1)}, u32[]{:S(2)}, u32[]{:S(2)}) %all-to-all-start.2) | async-done | bytes 262176 | tf_op jit(solution)/shard_map/all_to_all | solution.py:759
  247.7 1.7 collective-permute-start.35
  250.3 7.3 %attend_back.1 = (f32[128,1024]{1,0:T(8,128)}, f32[1024,128]{1,0:T(8,128)}, bf16[1024,128]{1,0:T(8,128)(2,1)}, bf16[1024,128]{1,0:T(8,128)(2,1)}, bf16[1024,128]{1,0:T(8,128)(2,1)}) custom-call(s32[1]{0:T(128)} %bitcast.c_ref, bf16[128,1024]{1,0:T(8,128)(2,1)} %get-tuple-element.122.q_ref, bf16[8,128,128]{2,1,0:T(8,128)(2,1)} %copy-done.33, ...), custom_call_target="tpu_custom_call" | custom-call | flops 25769803776 | bytes 2097152 | tf_op jit(solution)/shard_map/attend_back/pallas_call | solution.py:349
  257.6 5.1 %collective-permute-done.34 = bf16[256,1024]{1,0:T(8,128)(2,1)S(1)} collective-permute-done((bf16[256,1024]{1,0:T(8,128)(2,1)}, bf16[256,1024]{1,0:T(8,128)(2,1)S(1)}, u32[]{:S(2)}, u32[]{:S(2)}) %collective-permute-start.34) | collective-permute-done | bytes 524320 | tf_op jit(solution)/shard_map/ppermute | solution.py:736
  262.7 9.9 %collective-permute-done.36 = bf16[256,1024]{1,0:T(8,128)(2,1)S(1)} collective-permute-done((bf16[256,1024]{1,0:T(8,128)(2,1)}, bf16[256,1024]{1,0:T(8,128)(2,1)S(1)}, u32[]{:S(2)}, u32[]{:S(2)}) %collective-permute-start.36) | collective-permute-done | bytes 524320 | tf_op jit(solution)/shard_map/ppermute | solution.py:736
  272.7 3.3 collective-permute-start.37
  277.7 5.3 %collective-permute-done.37.refs_1_ = bf16[1024,128]{1,0:T(8,128)(2,1)S(1)} collective-permute-done((bf16[1024,128]{1,0:T(8,128)(2,1)}, bf16[1024,128]{1,0:T(8,128)(2,1)S(1)}, u32[]{:S(2)}, u32[]{:S(2)}) %collective-permute-start.37) | collective-permute-done | bytes 262176 | tf_op jit(solution)/shard_map/ppermute | solution.py:736
  283.0 5.6 %collective-permute-done.38.refs_2_ = bf16[1024,128]{1,0:T(8,128)(2,1)} collective-permute-done((bf16[1024,128]{1,0:T(8,128)(2,1)}, bf16[1024,128]{1,0:T(8,128)(2,1)}, u32[]{:S(2)}, u32[]{:S(2)}) %collective-permute-start.38) | collective-permute-done | bytes 262176 | tf_op jit(solution)/shard_map/ppermute | solution.py:736
  288.6 5.9 %tail.1 = (bf16[4,128,1024]{2,1,0:T(8,128)(2,1)}, bf16[4,128,1024]{2,1,0:T(8,128)(2,1)}, bf16[256,384]{1,0:T(8,128)(2,1)}, bf16[256,384]{1,0:T(8,128)(2,1)}, bf1...) custom-call(s32[2]{0:T(128)} %pad_add_fusion.at_ref, f32[128,1024]{1,0:T(8,128)} %get-tuple-element.170.gq_ref, ...), custom_call_target="tpu_custom_call" | custom-call | flops 1073741824 | bytes 12582912 | tf_op jit(solution)/shard_map/tail/pallas_call | solution.py:436
  294.6 1.5 add_convert_fusion.1
  299.0 1.7 add_convert_fusion
  300.7 1.9 collective-permute-start.44
  302.7 1.6 collective-permute-start.41
  304.3 1.4 collective-permute-start.42
  305.7 2.3 collective-permute-done.47
  308.0 1.6 collective-permute-start.43
  312.2 4.3 %collective-permute-start.51 = (bf16[128,1024]{1,0:T(8,128)(2,1)}, bf16[128,1024]{1,0:T(8,128)(2,1)}, u32[]{:S(2)}, u32[]{:S(2)}) collective-permute-start(bf16[128,1024]{1,0:T(8,128)(2,1)} %get-tuple-element.197), channel_id=1, source_target_pairs={{0,8},{8,16},{16,24},{24,0},{1,9},{9,17},{17,25},{25,1},{2,10},{10... | collective-permute-start | bytes 786440 | tf_op jit(solution)/shard_map/ppermute | solution.py:736
  317.3 4.2 %all-to-all-start.3 = ((bf16[8,32,384]{2,1,0:T(8,128)(2,1)}), bf16[8,32,384]{2,1,0:T(8,128)(2,1)S(1)}, u32[]{:S(2)}, u32[]{:S(2)}) async-start(bf16[8,32,384]{2,1,0:T(8,128)(2,1)} %bitcast.32), calls=%async_computation.3 | async-start | bytes 393216 | tf_op jit(solution)/shard_map/all_to_all | solution.py:759
  321.5 12.4 %collective-permute-done.44 = bf16[2,128,1024]{2,1,0:T(8,128)(2,1)S(1)} collective-permute-done((bf16[2,128,1024]{2,1,0:T(8,128)(2,1)S(1)}, bf16[2,128,1024]{2,1,0:T(8,128)(2,1)S(1)}, u32[]{:S(2)}, u32[]{:S(2)}) %collective-permute-start.44) | collective-permute-done | bytes 524320 | tf_op jit(solution)/shard_map/ppermute | solution.py:875
  334.9 2.0 add_convert_fusion.2
  336.9 11.9 %reduce-scatter.5.cloned.1.call-done = bf16[1,3,384,512]{3,2,1,0:T(8,128)(2,1)} async-done(((bf16[8,3,384,512]{3,2,1,0:T(8,128)(2,1)}), bf16[1,3,384,512]{3,2,1,0:T(8,128)(2,1)}) %reduce-scatter.5.cloned.1.call-update) | async-done | bytes 1179664 | tf_op jit(solution)/shard_map/reduce_scatter | solution.py:1022
  348.8 3.4 unpack.1
  352.9 2.6 finish.1
  (265 shorter events, 52.7 us)
Async XLA Ops:
  7.2 66.2 %all-gather.5.cloned.1.call-start = ((), (), s32[]{:S(2)}) async-start(), calls=%async_computation.8 | async-start | bytes 3538944 | tf_op jit(solution)/shard_map/all_gather | solution.py:951
  11.0 24.7 %copy-start.10 = (bf16[144,1024]{1,0:T(8,128)(2,1)}, bf16[144,1024]{1,0:T(8,128)(2,1)S(1)}, u32[]{:S(2)}) copy-start(bf16[144,1024]{1,0:T(8,128)(2,1)S(1)} %pad_maximum_fusion.3.refs_0_) | copy-start | bytes 884740
  11.0 12.2 %collective-permute-start = (bf16[144,1024]{1,0:T(8,128)(2,1)S(1)}, bf16[144,1024]{1,0:T(8,128)(2,1)S(1)}, u32[]{:S(2)}, u32[]{:S(2)}) collective-permute-start(bf16[144,1024]{1,0:T(8,128)(2,1)S(1)} %pad_maximum_fusion.3.refs_0_), channel_id=1, source_target_pairs={{0,2},{1,3},{2,4},{3,5},{4,6},{5,7},{8,10},{9,11},{10,12},{11,13},... | collective-permute-start | bytes 884744 | tf_op jit(solution)/shard_map/ppermute | solution.py:790
  16.0 18.5 %collective-permute-start.1 = (bf16[144,1024]{1,0:T(8,128)(2,1)S(1)}, bf16[144,1024]{1,0:T(8,128)(2,1)}, u32[]{:S(2)}, u32[]{:S(2)}) collective-permute-start(bf16[144,1024]{1,0:T(8,128)(2,1)S(1)} %pad_maximum_fusion.3.refs_0_), channel_id=1, source_target_pairs={{2,0},{3,1},{4,2},{5,3},{6,4},{7,5},{10,8},{11,9},{12,10},{13,11},... | collective-permute-start | bytes 884744 | tf_op jit(solution)/shard_map/ppermute | solution.py:790
  23.2 23.9 %collective-permute-start.4 = (bf16[144,1024]{1,0:T(8,128)(2,1)S(1)}, bf16[144,1024]{1,0:T(8,128)(2,1)}, u32[]{:S(2)}, u32[]{:S(2)}) collective-permute-start(bf16[144,1024]{1,0:T(8,128)(2,1)S(1)} %collective-permute-done), channel_id=1, source_target_pairs={{2,4},{3,5},{4,6},{5,7},{10,12},{11,13},{12,14},{13,15},{18,20},{1... | collective-permute-start | bytes 884744 | tf_op jit(solution)/shard_map/ppermute | solution.py:790
  34.4 26.4 %collective-permute-start.2 = (bf16[144,1024]{1,0:T(8,128)(2,1)}, bf16[144,1024]{1,0:T(8,128)(2,1)}, u32[]{:S(2)}, u32[]{:S(2)}) collective-permute-start(bf16[144,1024]{1,0:T(8,128)(2,1)} %collective-permute-done.1), channel_id=1, source_target_pairs={{2,0},{3,1},{4,2},{5,3},{10,8},{11,9},{12,10},{13,11},{18,16},{19,... | collective-permute-start | bytes 884744 | tf_op jit(solution)/shard_map/ppermute | solution.py:790
  37.7 35.7 %all-to-all-start = ((bf16[8,128,256]{2,1,0:T(8,128)(2,1)}), bf16[8,128,256]{2,1,0:T(8,128)(2,1)S(1)}, u32[]{:S(2)}, u32[]{:S(2)}) async-start(bf16[8,128,256]{2,1,0:T(8,128)(2,1)} %copy.126), calls=%async_computation | async-start | bytes 1048576 | tf_op jit(solution)/shard_map/all_to_all | solution.py:759
  42.5 136.1 %all-gather.7.cloned.1.call-start = ((), (), s32[]{:S(2)}) async-start(), calls=%async_computation.9 | async-start | bytes 10616832 | tf_op jit(solution)/shard_map/all_gather | solution.py:952
  42.6 30.8 %collective-permute-start.6 = (bf16[128,1024]{1,0:T(8,128)(2,1)}, bf16[128,1024]{1,0:T(8,128)(2,1)}, u32[]{:S(2)}, u32[]{:S(2)}) collective-permute-start(bf16[128,1024]{1,0:T(8,128)(2,1)} %refs_4_.1), channel_id=1, source_target_pairs={{0,8},{8,16},{16,24},{24,0},{1,9},{9,17},{17,25},{25,1},{2,10},{10... | collective-permute-start | bytes 786440 | tf_op jit(solution)/shard_map/ppermute | solution.py:736
  44.1 29.3 %collective-permute-start.7 = (bf16[128,1024]{1,0:T(8,128)(2,1)}, bf16[128,1024]{1,0:T(8,128)(2,1)}, u32[]{:S(2)}, u32[]{:S(2)}) collective-permute-start(bf16[128,1024]{1,0:T(8,128)(2,1)} %refs_4_.1), channel_id=1, source_target_pairs={{0,16},{8,24},{16,0},{24,8},{1,17},{9,25},{17,1},{25,9},{2,18},{10... | collective-permute-start | bytes 786440 | tf_op jit(solution)/shard_map/ppermute | solution.py:736
  45.7 27.7 %collective-permute-start.8 = (bf16[128,1024]{1,0:T(8,128)(2,1)}, bf16[128,1024]{1,0:T(8,128)(2,1)}, u32[]{:S(2)}, u32[]{:S(2)}) collective-permute-start(bf16[128,1024]{1,0:T(8,128)(2,1)} %refs_4_.1), channel_id=1, source_target_pairs={{0,24},{8,0},{16,8},{24,16},{1,25},{9,1},{17,9},{25,17},{2,26},{10... | collective-permute-start | bytes 786440 | tf_op jit(solution)/shard_map/ppermute | solution.py:736
  47.1 16.0 %collective-permute-start.5 = (bf16[144,1024]{1,0:T(8,128)(2,1)}, bf16[144,1024]{1,0:T(8,128)(2,1)}, u32[]{:S(2)}, u32[]{:S(2)}) collective-permute-start(bf16[144,1024]{1,0:T(8,128)(2,1)} %collective-permute-done.4), channel_id=1, source_target_pairs={{4,6},{5,7},{12,14},{13,15},{20,22},{21,23},{28,30},{29,31}} | collective-permute-start | bytes 884744 | tf_op jit(solution)/shard_map/ppermute | solution.py:790
  60.8 12.5 %collective-permute-start.3 = (bf16[144,1024]{1,0:T(8,128)(2,1)}, bf16[144,1024]{1,0:T(8,128)(2,1)S(1)}, u32[]{:S(2)}, u32[]{:S(2)}) collective-permute-start(bf16[144,1024]{1,0:T(8,128)(2,1)} %collective-permute-done.2), channel_id=1, source_target_pairs={{2,0},{3,1},{10,8},{11,9},{18,16},{19,17},{26,24},{27,25}} | collective-permute-start | bytes 884744 | tf_op jit(solution)/shard_map/ppermute | solution.py:790
  73.6 2.9 collective-permute-start.10
  73.7 2.8 collective-permute-start.11
  74.2 2.4 collective-permute-start.12
  74.2 2.3 collective-permute-start.9
  82.9 4.7 %collective-permute-start.16 = (bf16[16,1024]{1,0:T(8,128)(2,1)S(1)}, bf16[16,1024]{1,0:T(8,128)(2,1)S(1)}, u32[]{:S(2)}, u32[]{:S(2)}) collective-permute-start(bf16[16,1024]{1,0:T(8,128)(2,1)S(1)} %dynamic-slice_bitcast_fusion.5), channel_id=1, source_target_pairs={{0,1},{1,0},{2,3},{3,2},{4,5},{5,4},{6,7},{7,6},{8,9},{9,8},{10,11... | collective-permute-start | bytes 98312 | tf_op jit(solution)/shard_map/ppermute | solution.py:772
  83.1 10.3 %collective-permute-start.13 = (bf16[128,1024]{1,0:T(8,128)(2,1)}, bf16[128,1024]{1,0:T(8,128)(2,1)S(1)}, u32[]{:S(2)}, u32[]{:S(2)}) collective-permute-start(bf16[128,1024]{1,0:T(8,128)(2,1)} %get-tuple-element.123.refs_0_), channel_id=1, source_target_pairs={{0,8},{8,16},{16,24},{24,0},{1,9},{9,17},{17,25},{25,1},{2,10},{10... | collective-permute-start | bytes 786440 | tf_op jit(solution)/shard_map/ppermute | solution.py:736
  84.7 13.9 %collective-permute-start.14 = (bf16[128,1024]{1,0:T(8,128)(2,1)}, bf16[128,1024]{1,0:T(8,128)(2,1)S(1)}, u32[]{:S(2)}, u32[]{:S(2)}) collective-permute-start(bf16[128,1024]{1,0:T(8,128)(2,1)} %get-tuple-element.123.refs_0_), channel_id=1, source_target_pairs={{0,16},{8,24},{16,0},{24,8},{1,17},{9,25},{17,1},{25,9},{2,18},{10... | collective-permute-start | bytes 786440 | tf_op jit(solution)/shard_map/ppermute | solution.py:736
  86.2 12.5 %collective-permute-start.15 = (bf16[128,1024]{1,0:T(8,128)(2,1)}, bf16[128,1024]{1,0:T(8,128)(2,1)S(1)}, u32[]{:S(2)}, u32[]{:S(2)}) collective-permute-start(bf16[128,1024]{1,0:T(8,128)(2,1)} %get-tuple-element.123.refs_0_), channel_id=1, source_target_pairs={{0,24},{8,0},{16,8},{24,16},{1,25},{9,1},{17,9},{25,17},{2,26},{10... | collective-permute-start | bytes 786440 | tf_op jit(solution)/shard_map/ppermute | solution.py:736
  88.4 16.4 %collective-permute-start.17 = (bf16[2,16,1024]{2,1,0:T(8,128)(2,1)S(1)}, bf16[2,16,1024]{2,1,0:T(8,128)(2,1)S(1)}, u32[]{:S(2)}, u32[]{:S(2)}) collective-permute-start(bf16[2,16,1024]{2,1,0:T(8,128)(2,1)S(1)} %pad_maximum_fusion.5), channel_id=1, source_target_pairs={{0,2},{1,3},{2,4},{3,5},{4,6},{5,7},{6,0},{7,1},{8,10},{9,11},{10,... | collective-permute-start | bytes 196616 | tf_op jit(solution)/shard_map/ppermute | solution.py:764
  89.1 15.8 %collective-permute-start.18 = (bf16[2,16,1024]{2,1,0:T(8,128)(2,1)S(1)}, bf16[2,16,1024]{2,1,0:T(8,128)(2,1)S(1)}, u32[]{:S(2)}, u32[]{:S(2)}) collective-permute-start(bf16[2,16,1024]{2,1,0:T(8,128)(2,1)S(1)} %pad_maximum_fusion.5), channel_id=1, source_target_pairs={{0,4},{1,5},{2,6},{3,7},{4,0},{5,1},{6,2},{7,3},{8,12},{9,13},{10,... | collective-permute-start | bytes 196616 | tf_op jit(solution)/shard_map/ppermute | solution.py:764
  93.4 11.4 %collective-permute-start.19 = (bf16[2,16,1024]{2,1,0:T(8,128)(2,1)S(1)}, bf16[2,16,1024]{2,1,0:T(8,128)(2,1)S(1)}, u32[]{:S(2)}, u32[]{:S(2)}) collective-permute-start(bf16[2,16,1024]{2,1,0:T(8,128)(2,1)S(1)} %pad_maximum_fusion.5), channel_id=1, source_target_pairs={{0,6},{1,7},{2,0},{3,1},{4,2},{5,3},{6,4},{7,5},{8,14},{9,15},{10,... | collective-permute-start | bytes 196616 | tf_op jit(solution)/shard_map/ppermute | solution.py:764
  99.4 33.6 %copy-start.6 = (bf16[128,8,256]{0,2,1:T(8,128)(2,1)S(1)}, bf16[128,8,256]{0,2,1:T(8,128)(2,1)}, u32[]{:S(2)}) copy-start(bf16[128,8,256]{0,2,1:T(8,128)(2,1)} %get-tuple-element.232) | copy-start | bytes 1572868
  105.0 38.3 %copy-start.13 = (bf16[4,2,16,1024]{3,2,1,0:T(8,128)(2,1)}, bf16[4,2,16,1024]{3,2,1,0:T(8,128)(2,1)S(1)}, u32[]{:S(2)}) copy-start(bf16[4,2,16,1024]{3,2,1,0:T(8,128)(2,1)S(1)} %bitcast_dynamic-update-slice_fusion.refs_0_) | copy-start | bytes 786436
  105.0 21.8 %collective-permute-start.20 = (bf16[4,2,16,1024]{3,2,1,0:T(8,128)(2,1)S(1)}, bf16[4,2,16,1024]{3,2,1,0:T(8,128)(2,1)S(1)}, u32[]{:S(2)}, u32[]{:S(2)}) collective-permute-start(bf16[4,2,16,1024]{3,2,1,0:T(8,128)(2,1)S(1)} %bitcast_dynamic-update-slice_fusion.refs_0_), channel_id=1, source_target_pairs={{0,8},{8,16},{16,24},{24,0},{1,9},{9,17},{17,25},{25,1},{2,10},{10... | collective-permute-start | bytes 786440 | tf_op jit(solution)/shard_map/ppermute | solution.py:736
  111.2 19.9 %collective-permute-start.21 = (bf16[4,2,16,1024]{3,2,1,0:T(8,128)(2,1)S(1)}, bf16[4,2,16,1024]{3,2,1,0:T(8,128)(2,1)S(1)}, u32[]{:S(2)}, u32[]{:S(2)}) collective-permute-start(bf16[4,2,16,1024]{3,2,1,0:T(8,128)(2,1)S(1)} %bitcast_dynamic-update-slice_fusion.refs_0_), channel_id=1, source_target_pairs={{0,16},{8,24},{16,0},{24,8},{1,17},{9,25},{17,1},{25,9},{2,18},{10... | collective-permute-start | bytes 786440 | tf_op jit(solution)/shard_map/ppermute | solution.py:736
  120.1 11.1 %collective-permute-start.22 = (bf16[4,2,16,1024]{3,2,1,0:T(8,128)(2,1)S(1)}, bf16[4,2,16,1024]{3,2,1,0:T(8,128)(2,1)S(1)}, u32[]{:S(2)}, u32[]{:S(2)}) collective-permute-start(bf16[4,2,16,1024]{3,2,1,0:T(8,128)(2,1)S(1)} %bitcast_dynamic-update-slice_fusion.refs_0_), channel_id=1, source_target_pairs={{0,24},{8,0},{16,8},{24,16},{1,25},{9,1},{17,9},{25,17},{2,26},{10... | collective-permute-start | bytes 786440 | tf_op jit(solution)/shard_map/ppermute | solution.py:736
  120.7 22.5 %all-to-all-start.1 = ((bf16[8,128,128]{2,1,0:T(8,128)(2,1)}), bf16[8,128,128]{2,1,0:T(8,128)(2,1)S(1)}, u32[]{:S(2)}, u32[]{:S(2)}) async-start(bf16[8,128,128]{2,1,0:T(8,128)(2,1)} %get-tuple-element.126), calls=%async_computation.1 | async-start | bytes 524288 | tf_op jit(solution)/shard_map/all_to_all | solution.py:759
  124.1 100.6 %reduce-scatter.3.cloned.1.call-start = ((), (), s32[]{:S(2)}) async-start(), calls=%async_computation.6 | async-start | bytes 3538944 | tf_op jit(solution)/shard_map/reduce_scatter | solution.py:1021
  124.1 11.7 %collective-permute-start.23 = (bf16[4,2,16,1024]{3,2,1,0:T(8,128)(2,1)S(1)}, bf16[4,2,16,1024]{3,2,1,0:T(8,128)(2,1)S(1)}, u32[]{:S(2)}, u32[]{:S(2)}) collective-permute-start(bf16[4,2,16,1024]{3,2,1,0:T(8,128)(2,1)S(1)} %bitcast_dynamic-update-slice_fusion.refs_0_), channel_id=1, source_target_pairs={{0,1},{1,0},{2,3},{3,2},{4,5},{5,4},{6,7},{7,6},{8,9},{9,8},{10,11... | collective-permute-start | bytes 786440 | tf_op jit(solution)/shard_map/ppermute | solution.py:772
  126.8 16.4 %collective-permute-start.24 = (bf16[4,2,16,1024]{3,2,1,0:T(8,128)(2,1)S(1)}, bf16[4,2,16,1024]{3,2,1,0:T(8,128)(2,1)S(1)}, u32[]{:S(2)}, u32[]{:S(2)}) collective-permute-start(bf16[4,2,16,1024]{3,2,1,0:T(8,128)(2,1)S(1)} %collective-permute-done.20.refs_1_), channel_id=1, source_target_pairs={{0,1},{1,0},{2,3},{3,2},{4,5},{5,4},{6,7},{7,6},{8,9},{9,8},{10,11... | collective-permute-start | bytes 786440 | tf_op jit(solution)/shard_map/ppermute | solution.py:772
  131.1 12.1 %collective-permute-start.25 = (bf16[4,2,16,1024]{3,2,1,0:T(8,128)(2,1)S(1)}, bf16[4,2,16,1024]{3,2,1,0:T(8,128)(2,1)}, u32[]{:S(2)}, u32[]{:S(2)}) collective-permute-start(bf16[4,2,16,1024]{3,2,1,0:T(8,128)(2,1)S(1)} %collective-permute-done.21.refs_2_), channel_id=1, source_target_pairs={{0,1},{1,0},{2,3},{3,2},{4,5},{5,4},{6,7},{7,6},{8,9},{9,8},{10,11... | collective-permute-start | bytes 786440 | tf_op jit(solution)/shard_map/ppermute | solution.py:772
  131.2 12.0 %collective-permute-start.26 = (bf16[4,2,16,1024]{3,2,1,0:T(8,128)(2,1)S(1)}, bf16[4,2,16,1024]{3,2,1,0:T(8,128)(2,1)}, u32[]{:S(2)}, u32[]{:S(2)}) collective-permute-start(bf16[4,2,16,1024]{3,2,1,0:T(8,128)(2,1)S(1)} %collective-permute-done.22.refs_3_), channel_id=1, source_target_pairs={{0,1},{1,0},{2,3},{3,2},{4,5},{5,4},{6,7},{7,6},{8,9},{9,8},{10,11... | collective-permute-start | bytes 786440 | tf_op jit(solution)/shard_map/ppermute | solution.py:772
  150.3 10.9 %collective-permute-start.27 = (bf16[128,1152]{1,0:T(8,128)(2,1)S(1)}, bf16[128,1152]{1,0:T(8,128)(2,1)S(1)}, u32[]{:S(2)}, u32[]{:S(2)}) collective-permute-start(bf16[128,1152]{1,0:T(8,128)(2,1)S(1)} %concatenate.24.refs_0_), channel_id=1, source_target_pairs={{0,8},{8,16},{16,24},{24,0},{1,9},{9,17},{17,25},{25,1},{2,10},{10... | collective-permute-start | bytes 884744 | tf_op jit(solution)/shard_map/ppermute | solution.py:736
  152.0 15.1 %collective-permute-start.28 = (bf16[128,1152]{1,0:T(8,128)(2,1)S(1)}, bf16[128,1152]{1,0:T(8,128)(2,1)S(1)}, u32[]{:S(2)}, u32[]{:S(2)}) collective-permute-start(bf16[128,1152]{1,0:T(8,128)(2,1)S(1)} %concatenate.24.refs_0_), channel_id=1, source_target_pairs={{0,16},{8,24},{16,0},{24,8},{1,17},{9,25},{17,1},{25,9},{2,18},{10... | collective-permute-start | bytes 884744 | tf_op jit(solution)/shard_map/ppermute | solution.py:736
  152.0 16.1 %collective-permute-start.29 = (bf16[128,1152]{1,0:T(8,128)(2,1)S(1)}, bf16[128,1152]{1,0:T(8,128)(2,1)S(1)}, u32[]{:S(2)}, u32[]{:S(2)}) collective-permute-start(bf16[128,1152]{1,0:T(8,128)(2,1)S(1)} %concatenate.24.refs_0_), channel_id=1, source_target_pairs={{0,24},{8,0},{16,8},{24,16},{1,25},{9,1},{17,9},{25,17},{2,26},{10... | collective-permute-start | bytes 884744 | tf_op jit(solution)/shard_map/ppermute | solution.py:736
  154.8 1.1 collective-permute-start.30
  178.6 170.2 %reduce-scatter.5.cloned.1.call-start = ((), (), s32[]{:S(2)}) async-start(), calls=%async_computation.7 | async-start | bytes 10616832 | tf_op jit(solution)/shard_map/reduce_scatter | solution.py:1022
  202.7 10.5 %collective-permute-start.31 = (bf16[128,1152]{1,0:T(8,128)(2,1)}, bf16[128,1152]{1,0:T(8,128)(2,1)S(1)}, u32[]{:S(2)}, u32[]{:S(2)}) collective-permute-start(bf16[128,1152]{1,0:T(8,128)(2,1)} %get-tuple-element.155), channel_id=1, source_target_pairs={{0,24},{8,0},{16,8},{24,16},{1,25},{9,1},{17,9},{25,17},{2,26},{10... | collective-permute-start | bytes 884744 | tf_op jit(solution)/shard_map/ppermute | solution.py:736
  206.2 15.6 %collective-permute-start.32 = (bf16[128,1152]{1,0:T(8,128)(2,1)}, bf16[128,1152]{1,0:T(8,128)(2,1)S(1)}, u32[]{:S(2)}, u32[]{:S(2)}) collective-permute-start(bf16[128,1152]{1,0:T(8,128)(2,1)} %get-tuple-element.156), channel_id=1, source_target_pairs={{0,16},{8,24},{16,0},{24,8},{1,17},{9,25},{17,1},{25,9},{2,18},{10... | collective-permute-start | bytes 884744 | tf_op jit(solution)/shard_map/ppermute | solution.py:736
  208.0 15.5 %collective-permute-start.33 = (bf16[128,1152]{1,0:T(8,128)(2,1)}, bf16[128,1152]{1,0:T(8,128)(2,1)S(1)}, u32[]{:S(2)}, u32[]{:S(2)}) collective-permute-start(bf16[128,1152]{1,0:T(8,128)(2,1)} %get-tuple-element.157), channel_id=1, source_target_pairs={{0,8},{8,16},{16,24},{24,0},{1,9},{9,17},{17,25},{25,1},{2,10},{10... | collective-permute-start | bytes 884744 | tf_op jit(solution)/shard_map/ppermute | solution.py:736
  229.3 17.7 %all-to-all-start.2 = ((bf16[8,128,128]{2,1,0:T(8,128)(2,1)}), bf16[8,128,128]{2,1,0:T(8,128)(2,1)S(1)}, u32[]{:S(2)}, u32[]{:S(2)}) async-start(bf16[8,128,128]{2,1,0:T(8,128)(2,1)} %bitcast.29), calls=%async_computation.2 | async-start | bytes 524288 | tf_op jit(solution)/shard_map/all_to_all | solution.py:759
  247.7 15.1 %collective-permute-start.34 = (bf16[256,1024]{1,0:T(8,128)(2,1)}, bf16[256,1024]{1,0:T(8,128)(2,1)S(1)}, u32[]{:S(2)}, u32[]{:S(2)}) collective-permute-start(bf16[256,1024]{1,0:T(8,128)(2,1)} %convolution_convert_fusion.2), channel_id=1, source_target_pairs={{0,24},{8,0},{16,8},{24,16},{1,25},{9,1},{17,9},{25,17},{2,26},{10... | collective-permute-start | bytes 1572872 | tf_op jit(solution)/shard_map/ppermute | solution.py:736
  247.7 15.1 %collective-permute-start.35 = (bf16[256,1024]{1,0:T(8,128)(2,1)}, bf16[256,1024]{1,0:T(8,128)(2,1)S(1)}, u32[]{:S(2)}, u32[]{:S(2)}) collective-permute-start(bf16[256,1024]{1,0:T(8,128)(2,1)} %convolution_convert_fusion.1), channel_id=1, source_target_pairs={{0,16},{8,24},{16,0},{24,8},{1,17},{9,25},{17,1},{25,9},{2,18},{10... | collective-permute-start | bytes 1572872 | tf_op jit(solution)/shard_map/ppermute | solution.py:736
  249.4 23.3 %collective-permute-start.36 = (bf16[256,1024]{1,0:T(8,128)(2,1)}, bf16[256,1024]{1,0:T(8,128)(2,1)S(1)}, u32[]{:S(2)}, u32[]{:S(2)}) collective-permute-start(bf16[256,1024]{1,0:T(8,128)(2,1)} %convolution_convert_fusion), channel_id=1, source_target_pairs={{0,8},{8,16},{16,24},{24,0},{1,9},{9,17},{17,25},{25,1},{2,10},{10... | collective-permute-start | bytes 1572872 | tf_op jit(solution)/shard_map/ppermute | solution.py:736
  272.7 10.4 %collective-permute-start.37 = (bf16[1024,128]{1,0:T(8,128)(2,1)}, bf16[1024,128]{1,0:T(8,128)(2,1)S(1)}, u32[]{:S(2)}, u32[]{:S(2)}) collective-permute-start(bf16[1024,128]{1,0:T(8,128)(2,1)} %get-tuple-element.173), channel_id=1, source_target_pairs={{0,24},{8,0},{16,8},{24,16},{1,25},{9,1},{17,9},{25,17},{2,26},{10... | collective-permute-start | bytes 786440 | tf_op jit(solution)/shard_map/ppermute | solution.py:736
  275.9 12.7 %collective-permute-start.38 = (bf16[1024,128]{1,0:T(8,128)(2,1)}, bf16[1024,128]{1,0:T(8,128)(2,1)}, u32[]{:S(2)}, u32[]{:S(2)}) collective-permute-start(bf16[1024,128]{1,0:T(8,128)(2,1)} %get-tuple-element.174), channel_id=1, source_target_pairs={{0,16},{8,24},{16,0},{24,8},{1,17},{9,25},{17,1},{25,9},{2,18},{10... | collective-permute-start | bytes 786440 | tf_op jit(solution)/shard_map/ppermute | solution.py:736
  275.9 12.7 %collective-permute-start.39 = (bf16[1024,128]{1,0:T(8,128)(2,1)}, bf16[1024,128]{1,0:T(8,128)(2,1)}, u32[]{:S(2)}, u32[]{:S(2)}) collective-permute-start(bf16[1024,128]{1,0:T(8,128)(2,1)} %get-tuple-element.175), channel_id=1, source_target_pairs={{0,8},{8,16},{16,24},{24,0},{1,9},{9,17},{17,25},{25,1},{2,10},{10... | collective-permute-start | bytes 786440 | tf_op jit(solution)/shard_map/ppermute | solution.py:736
  294.6 4.4 %collective-permute-start.40 = (bf16[4,128,1024]{2,1,0:T(8,128)(2,1)}, bf16[4,128,1024]{2,1,0:T(8,128)(2,1)}, u32[]{:S(2)}, u32[]{:S(2)}) collective-permute-start(bf16[4,128,1024]{2,1,0:T(8,128)(2,1)} %get-tuple-element.181), channel_id=1, source_target_pairs={{0,1},{1,0},{2,3},{3,2},{4,5},{5,4},{6,7},{7,6},{8,9},{9,8},{10,11... | collective-permute-start | bytes 3145736 | tf_op jit(solution)/shard_map/ppermute | solution.py:772
  296.2 2.5 collective-permute-start.46
  298.2 36.7 %collective-permute-start.49 = (bf16[128,1024]{1,0:T(8,128)(2,1)}, bf16[128,1024]{1,0:T(8,128)(2,1)}, u32[]{:S(2)}, u32[]{:S(2)}) collective-permute-start(bf16[128,1024]{1,0:T(8,128)(2,1)} %get-tuple-element.195), channel_id=1, source_target_pairs={{0,24},{8,0},{16,8},{24,16},{1,25},{9,1},{17,9},{25,17},{2,26},{10... | collective-permute-start | bytes 786440 | tf_op jit(solution)/shard_map/ppermute | solution.py:736
  298.7 9.3 %collective-permute-start.47 = (bf16[2,32,1024]{2,1,0:T(8,128)(2,1)S(1)}, bf16[2,32,1024]{2,1,0:T(8,128)(2,1)S(1)}, u32[]{:S(2)}, u32[]{:S(2)}) collective-permute-start(bf16[2,32,1024]{2,1,0:T(8,128)(2,1)S(1)} %dynamic-slice_bitcast_fusion.3), channel_id=1, source_target_pairs={{0,2},{1,3},{2,0},{3,1},{4,6},{5,7},{6,4},{7,5},{8,10},{9,11},{10,... | collective-permute-start | bytes 393224 | tf_op jit(solution)/shard_map/ppermute | solution.py:875
  300.7 33.2 %collective-permute-start.44 = (bf16[2,128,1024]{2,1,0:T(8,128)(2,1)S(1)}, bf16[2,128,1024]{2,1,0:T(8,128)(2,1)S(1)}, u32[]{:S(2)}, u32[]{:S(2)}) collective-permute-start(bf16[2,128,1024]{2,1,0:T(8,128)(2,1)S(1)} %dynamic-slice_bitcast_fusion), channel_id=1, source_target_pairs={{0,2},{1,3},{2,0},{3,1},{4,6},{5,7},{6,4},{7,5},{8,10},{9,11},{10,... | collective-permute-start | bytes 1572872 | tf_op jit(solution)/shard_map/ppermute | solution.py:875
  302.7 8.9 %collective-permute-start.41 = (bf16[256,384]{1,0:T(8,128)(2,1)S(1)}, bf16[256,384]{1,0:T(8,128)(2,1)S(1)}, u32[]{:S(2)}, u32[]{:S(2)}) collective-permute-start(bf16[256,384]{1,0:T(8,128)(2,1)S(1)} %copy-done.52), channel_id=1, source_target_pairs={{0,24},{8,0},{16,8},{24,16},{1,25},{9,1},{17,9},{25,17},{2,26},{10... | collective-permute-start | bytes 589832 | tf_op jit(solution)/shard_map/ppermute | solution.py:736
  304.3 7.9 %collective-permute-start.42 = (bf16[256,384]{1,0:T(8,128)(2,1)S(1)}, bf16[256,384]{1,0:T(8,128)(2,1)S(1)}, u32[]{:S(2)}, u32[]{:S(2)}) collective-permute-start(bf16[256,384]{1,0:T(8,128)(2,1)S(1)} %copy-done.51), channel_id=1, source_target_pairs={{0,16},{8,24},{16,0},{24,8},{1,17},{9,25},{17,1},{25,9},{2,18},{10... | collective-permute-start | bytes 589832 | tf_op jit(solution)/shard_map/ppermute | solution.py:736
  308.0 8.5 %collective-permute-start.43 = (bf16[256,384]{1,0:T(8,128)(2,1)S(1)}, bf16[256,384]{1,0:T(8,128)(2,1)S(1)}, u32[]{:S(2)}, u32[]{:S(2)}) collective-permute-start(bf16[256,384]{1,0:T(8,128)(2,1)S(1)} %copy-done.50), channel_id=1, source_target_pairs={{0,8},{8,16},{16,24},{24,0},{1,9},{9,17},{17,25},{25,1},{2,10},{10... | collective-permute-start | bytes 589832 | tf_op jit(solution)/shard_map/ppermute | solution.py:736
  309.6 25.3 %copy-start.24 = (bf16[128,1024]{1,0:T(8,128)(2,1)S(1)}, bf16[128,1024]{1,0:T(8,128)(2,1)}, u32[]{:S(2)}) copy-start(bf16[128,1024]{1,0:T(8,128)(2,1)} %get-tuple-element.194) | copy-start | bytes 786436
  311.6 23.3 %collective-permute-start.50 = (bf16[128,1024]{1,0:T(8,128)(2,1)}, bf16[128,1024]{1,0:T(8,128)(2,1)S(1)}, u32[]{:S(2)}, u32[]{:S(2)}) collective-permute-start(bf16[128,1024]{1,0:T(8,128)(2,1)} %get-tuple-element.196), channel_id=1, source_target_pairs={{0,16},{8,24},{16,0},{24,8},{1,17},{9,25},{17,1},{25,9},{2,18},{10... | collective-permute-start | bytes 786440 | tf_op jit(solution)/shard_map/ppermute | solution.py:736
  312.2 22.7 %collective-permute-start.51 = (bf16[128,1024]{1,0:T(8,128)(2,1)}, bf16[128,1024]{1,0:T(8,128)(2,1)}, u32[]{:S(2)}, u32[]{:S(2)}) collective-permute-start(bf16[128,1024]{1,0:T(8,128)(2,1)} %get-tuple-element.197), channel_id=1, source_target_pairs={{0,8},{8,16},{16,24},{24,0},{1,9},{9,17},{17,25},{25,1},{2,10},{10... | collective-permute-start | bytes 786440 | tf_op jit(solution)/shard_map/ppermute | solution.py:736
  316.5 35.7 %collective-permute-start.48 = (bf16[1,32,1024]{2,1,0:T(8,128)(2,1)S(1)}, bf16[1,32,1024]{2,1,0:T(8,128)(2,1)S(1)}, u32[]{:S(2)}, u32[]{:S(2)}) collective-permute-start(bf16[1,32,1024]{2,1,0:T(8,128)(2,1)S(1)} %get-tuple-element.239), channel_id=1, source_target_pairs={{0,4},{1,5},{2,6},{3,7},{4,0},{5,1},{6,2},{7,3},{8,12},{9,13},{10,... | collective-permute-start | bytes 196616 | tf_op jit(solution)/shard_map/ppermute | solution.py:875
  317.3 34.9 %all-to-all-start.3 = ((bf16[8,32,384]{2,1,0:T(8,128)(2,1)}), bf16[8,32,384]{2,1,0:T(8,128)(2,1)S(1)}, u32[]{:S(2)}, u32[]{:S(2)}) async-start(bf16[8,32,384]{2,1,0:T(8,128)(2,1)} %bitcast.32), calls=%async_computation.3 | async-start | bytes 393216 | tf_op jit(solution)/shard_map/all_to_all | solution.py:759
  334.9 17.3 %collective-permute-start.45 = (bf16[1,128,1024]{2,1,0:T(8,128)(2,1)S(1)}, bf16[1,128,1024]{2,1,0:T(8,128)(2,1)S(1)}, u32[]{:S(2)}, u32[]{:S(2)}) collective-permute-start(bf16[1,128,1024]{2,1,0:T(8,128)(2,1)S(1)} %get-tuple-element.230), channel_id=1, source_target_pairs={{0,4},{1,5},{2,6},{3,7},{4,0},{5,1},{6,2},{7,3},{8,12},{9,13},{10,... | collective-permute-start | bytes 786440 | tf_op jit(solution)/shard_map/ppermute | solution.py:875
  (49 other events, 354.9 us)
Sparse Core Ops, SparseCore 0:
  10.8 57.2 all-gather.4
  73.6 104.1 all-gather.6
  180.2 40.5 reduce-scatter.2
  224.8 123.8 reduce-scatter.4
